TPU v7x, 128 devices: a whole 4x4x4 slice. The times are simulated.
128 devices in a mesh: row: 8 (over z_hi, y), col: 16 (over z_lo, x, core).
Axes of the slice: x: 4, y: 4, z: 4 (z_hi: 2, z_lo: 2; z = z_hi * 2 + z_lo), core: 2. Of those that a mesh axis runs over, the one named last changes fastest.
Arguments:
- features: bfloat16 [65536, 256], P(('col', 'row')), may hold values from -6 to 6
- weight: bfloat16 [256, 256], replicated, may hold values from -0.375 to 0.375
- bias: float32 [256], replicated, may hold values from -4 to 4
- cotangent: bfloat16 [65536, 256], P(('row', 'col')), may hold values from -6 to 6
- tiles: bfloat16 [8, 16, 384, 128, 128], P('row', 'col'), may hold values from -0.0546875 to 0.0546875
- tile_rows: int32 [8, 16, 384], P('row', 'col'), may hold values from 0 to 63, as said below
- tile_cols: int32 [8, 16, 384], P('row', 'col'), may hold values from 0 to 31
- tile_counts: int32 [8, 16], P('row', 'col'), may hold values from 24 to 384, as said below
Outputs:
- hidden: bfloat16 [65536, 256], P(('row', 'col'))
- grad_weight: float32 [256, 256], replicated
- grad_bias: float32 [256], replicated
- grad_features: bfloat16 [65536, 256], P(('col', 'row'))
Inputs may be any that keep to these rules, and one draw needn't show every extreme that they name: `tile_rows`: on each grid cell the slots name distinct blocks. `tile_counts`: slots at or after a cell's count are unused; some cell uses all 384 slots.
All inputs are finite; a program needn't handle non-finite values.
Results may differ from a plain program's by a relative error of at most 0.013.
Values may be sent and summed in bfloat16 or wider, within the bound.
A program may use at most 128 MiB of HBM per device.

v0:
```python
import math

import jax
import jax.numpy as jnp
from jax import lax
from jax.sharding import PartitionSpec as P


def accumulate(tiles, dest_ids, source_ids, live_count, source_blocks, out_blocks, backward):
    slots = tiles.shape[0]
    group = math.gcd(slots, 32)
    block = tiles.shape[-1]
    width = source_blocks.shape[-1]
    in_blocks = source_blocks.shape[0]
    flat_source = source_blocks.reshape(in_blocks, block * width)
    in_range = jnp.arange(in_blocks, dtype=jnp.int32)
    out_range = jnp.arange(out_blocks, dtype=jnp.int32)

    def one_group(step_index, total):
        start = step_index * group
        tile_group = lax.dynamic_slice_in_dim(tiles, start, group, 0)
        dest_group = lax.dynamic_slice_in_dim(dest_ids, start, group, 0)
        source_group = lax.dynamic_slice_in_dim(source_ids, start, group, 0)
        live = start + jnp.arange(group, dtype=jnp.int32) < live_count
        if backward:
            fetch_ids = dest_group
            target = source_group
        else:
            fetch_ids = source_group
            target = dest_group
        picker = (fetch_ids[:, None] == in_range[None, :]).astype(jnp.bfloat16)
        fetched = jnp.dot(picker, flat_source, preferred_element_type=jnp.float32)
        fetched = fetched.astype(jnp.bfloat16).reshape(group, block, width)
        if backward:
            contrib = jnp.einsum(
                "tji,tjf->tif", tile_group, fetched, preferred_element_type=jnp.float32
            )
        else:
            contrib = jnp.einsum(
                "tij,tjf->tif", tile_group, fetched, preferred_element_type=jnp.float32
            )
        placer = ((target[:, None] == out_range[None, :]) & live[:, None]).astype(jnp.float32)
        added = jnp.dot(
            placer.T,
            contrib.reshape(group, block * width),
            precision=lax.Precision.HIGHEST,
            preferred_element_type=jnp.float32,
        )
        return total + added

    start_total = jnp.zeros((out_blocks, block * width), jnp.float32)
    result = lax.fori_loop(0, slots // group, one_group, start_total)
    return result.reshape(out_blocks, block, width)


def per_device(features, weight, bias, cotangent, tiles, tile_rows, tile_cols, tile_counts):
    tile_set = tiles[0, 0]
    dest_ids = tile_rows[0, 0]
    source_ids = tile_cols[0, 0]
    live_count = tile_counts[0, 0]
    block = tile_set.shape[-1]
    own_nodes = features.shape[0]
    width = features.shape[1]
    row_count = lax.axis_size("row")
    col_count = lax.axis_size("col")
    blocks_down = own_nodes * col_count // block
    blocks_across = own_nodes * row_count // block
    factor = 1.0 / math.sqrt(own_nodes * row_count * col_count)
    panel = lax.all_gather(features, "row", axis=0, tiled=True)
    panel_blocks = panel.reshape(blocks_across, block, width)
    partial_value = accumulate(
        tile_set, dest_ids, source_ids, live_count, panel_blocks, blocks_down, False
    )
    term = partial_value.reshape(blocks_down * block, width)
    summed = lax.psum_scatter(term, "col", scatter_dimension=0, tiled=True)
    aggregated = summed.astype(jnp.bfloat16)
    preact = jnp.dot(aggregated, weight, preferred_element_type=jnp.float32) + bias
    hidden = jax.nn.silu(preact).astype(jnp.bfloat16)
    sigma = jax.nn.sigmoid(preact)
    slope = sigma * (1.0 + preact * (1.0 - sigma))
    grad_pre = (cotangent.astype(jnp.float32) * slope).astype(jnp.bfloat16)
    local_weight = jnp.einsum("nf,ng->fg", aggregated, grad_pre, preferred_element_type=jnp.float32)
    local_bias = jnp.sum(grad_pre.astype(jnp.float32), axis=0)
    grad_agg = jnp.dot(grad_pre, weight.T, preferred_element_type=jnp.float32).astype(jnp.bfloat16)
    grad_panel = lax.all_gather(grad_agg, "col", axis=0, tiled=True)
    grad_blocks = grad_panel.reshape(blocks_down, block, width)
    partial_back = accumulate(
        tile_set, dest_ids, source_ids, live_count, grad_blocks, blocks_across, True
    )
    term_back = partial_back.reshape(blocks_across * block, width)
    grad_features = lax.psum_scatter(
        term_back.astype(jnp.bfloat16), "row", scatter_dimension=0, tiled=True
    )
    grad_weight, grad_bias = lax.psum((local_weight, local_bias), ("row", "col"))
    grad_weight = grad_weight * factor
    grad_bias = grad_bias * factor
    return (hidden, grad_weight, grad_bias, grad_features)


def solution(mesh):
    in_specs = (
        P(("col", "row"), None),
        P(),
        P(),
        P(("row", "col"), None),
        P("row", "col", None, None, None),
        P("row", "col", None),
        P("row", "col", None),
        P("row", "col"),
    )
    out_specs = (P(("row", "col"), None), P(), P(), P(("col", "row"), None))
    return jax.shard_map(
        per_device, mesh=mesh, in_specs=in_specs, out_specs=out_specs, check_vma=False
    )
```

profile of v0, /device:TPU:0, one launch (start us, length us, event | category | flops | bytes accessed | tf_op | source)
XLA Modules:
  0.0 667.1 jit_solution(5247763881698745133)
XLA Ops:
  9.4 58.5 %all-gather.3.cloned.1.call-done = bf16[4096,256]{1,0:T(8,128)(2,1)} async-done(((bf16[512,256]{1,0:T(8,128)(2,1)}), bf16[4096,256]{1,0:T(8,128)(2,1)}) %all-gather.3.cloned.1.call-update) | async-done | bytes 2097168 | tf_op jit(solution)/shard_map/all_gather | solution.py:69
  70.7 196.6 %while.28 = (s32[]{:T(128)}, f32[64,32768]{1,0:T(8,128)}, s32[384]{0:T(512)S(1)}, s32[]{:T(128)}, bf16[384,128,128]{2,1,0:T(8,128)(2,1)}, /*index=5*/s32[384]{0:...) while((s32[]{:T(128)}, f32[64,32768]{1,0:T(8,128)}, ...), condition=%wide.region_1.0_spmd.clone, body=%wide.region_0.0_spmd.clone.sunk | while | flops 1146098688 | bytes 103810120 | solution.py:52
  77.4 6.5 convolution_add_fusion.5
  93.8 6.5 convolution_add_fusion.5
  110.1 6.5 convolution_add_fusion.5
  126.5 6.5 convolution_add_fusion.5
  142.9 6.5 convolution_add_fusion.5
  159.3 6.5 convolution_add_fusion.5
  175.7 6.5 convolution_add_fusion.5
  192.0 6.5 convolution_add_fusion.5
  208.4 6.5 convolution_add_fusion.5
  224.8 6.5 convolution_add_fusion.5
  241.2 6.5 convolution_add_fusion.5
  257.6 6.5 convolution_add_fusion.5
  267.3 9.2 %reshape_reshape.11 = f32[8192,256]{1,0:T(8,128)} reshape(f32[64,32768]{1,0:T(8,128)} %get-tuple-element.312) | data formatting | bytes 16777216 | tf_op jit(solution)/shard_map/reshape;reshape | solution.py:74
  276.6 73.4 %reduce-scatter.3.cloned.1.call-done = f32[512,256]{1,0:T(8,128)} async-done(((f32[8192,256]{1,0:T(8,128)}), f32[512,256]{1,0:T(8,128)}) %reduce-scatter.3.cloned.1.call-update) | async-done | bytes 524304 | tf_op jit(solution)/shard_map/reduce_scatter | solution.py:75
  353.4 16.7 %copy.12 = bf16[1,1,384,128,128]{3,4,2,1,0:T(8,128)(2,1)} copy(bf16[1,1,384,128,128]{4,3,2,1,0:T(8,128)(2,1)} %bitcast.60) | data formatting | bytes 25165824 | tf_op args[4]
  371.2 18.1 %all-gather.5.cloned.1.call-done = bf16[8192,256]{1,0:T(8,128)(2,1)} async-done(((bf16[512,256]{1,0:T(8,128)(2,1)}), bf16[8192,256]{1,0:T(8,128)(2,1)}) %all-gather.5.cloned.1.call-update) | async-done | bytes 4194320 | tf_op jit(solution)/shard_map/all_gather | solution.py:85
  389.2 7.4 %reshape_reshape.12 = bf16[64,32768]{1,0:T(8,128)(2,1)} reshape(bf16[8192,256]{1,0:T(8,128)(2,1)} %all-gather.5.cloned.1.call-done) | data formatting | bytes 8388608 | tf_op jit(solution)/shard_map/reshape;reshape | solution.py:15
  396.6 183.3 %while.29 = (s32[]{:T(128)}, f32[32,32768]{1,0:T(8,128)}, s32[384]{0:T(512)S(1)}, s32[]{:T(128)}, bf16[384,128,128]{1,2,0:T(8,128)(2,1)}, /*index=5*/s32[384]{0:...) while((s32[]{:T(128)}, f32[32,32768]{1,0:T(8,128)}, ...), condition=%wide.region_7.8_spmd.clone, body=%wide.region_6.7_spmd.clone.sunk | while | flops 808456256 | bytes 72352824 | solution.py:52
  405.3 4.7 convolution_add_fusion.6
  420.6 4.7 convolution_add_fusion.6
  435.8 4.7 convolution_add_fusion.6
  451.1 4.7 convolution_add_fusion.6
  466.4 4.7 convolution_add_fusion.6
  481.7 4.7 convolution_add_fusion.6
  496.9 4.7 convolution_add_fusion.6
  512.2 4.7 convolution_add_fusion.6
  542.7 4.7 convolution_add_fusion.6
  558.0 4.7 convolution_add_fusion.6
  573.3 4.7 convolution_add_fusion.6
  584.7 69.3 %psum.15 = f32[256]{0:T(256)S(1)} all-reduce(f32[256]{0:T(256)S(1)} %get-tuple-element.405), channel_id=1, replica_groups=mesh['row'=8,'col'=16] {'row','col'}, use_global_device_ids=true, to_apply=%region_5.6 | all-reduce | flops 256 | bytes 2048 | tf_op jit(solution)/shard_map/psum | solution.py:94
  (335 shorter events, 269.5 us)
Async XLA Ops:
  7.2 342.9 %copy-start = (bf16[256,256]{1,0:T(8,128)(2,1)S(1)}, bf16[256,256]{1,0:T(8,128)(2,1)}, u32[]{:S(2)}) copy-start(bf16[256,256]{1,0:T(8,128)(2,1)} %param.13) | copy-start | bytes 393220
  7.2 60.7 %all-gather.3.cloned.1.call-start = ((), (), s32[]{:S(2)}) async-start(), calls=%async_computation.2 | async-start | bytes 2359296 | tf_op jit(solution)/shard_map/all_gather | solution.py:69
  7.9 342.1 %reduce-scatter.3.cloned.1.call-start = ((), (), s32[]{:S(2)}) async-start(), calls=%async_computation.3 | async-start | bytes 8912896 | tf_op jit(solution)/shard_map/reduce_scatter | solution.py:75
  72.8 4.5 slice-start
  83.9 3.2 copy-start.2
  89.2 4.5 slice-start
  100.3 3.2 copy-start.2
  105.6 4.5 slice-start
  116.7 3.2 copy-start.2
  122.0 4.5 slice-start
  133.0 3.2 copy-start.2
  138.3 4.5 slice-start
  154.7 4.5 slice-start
  165.8 3.2 copy-start.2
  171.1 4.5 slice-start
  182.2 3.2 copy-start.2
  187.5 4.5 slice-start
  203.8 4.5 slice-start
  214.9 3.2 copy-start.2
  220.2 4.5 slice-start
  231.3 3.2 copy-start.2
  236.6 4.5 slice-start
  247.7 3.2 copy-start.2
  253.0 4.5 slice-start
  264.1 3.2 copy-start.2
  276.6 73.5 %copy-start.6 = (bf16[512,256]{1,0:T(8,128)(2,1)S(1)}, bf16[512,256]{1,0:T(8,128)(2,1)}, u32[]{:S(2)}) copy-start(bf16[512,256]{1,0:T(8,128)(2,1)} %param.15) | copy-start | bytes 786436
  276.6 73.5 %copy-start.7 = (f32[256]{0:T(256)S(1)}, f32[256]{0:T(256)}, u32[]{:S(2)}) copy-start(f32[256]{0:T(256)} %param.14) | copy-start | bytes 3076
  276.6 112.7 %all-gather.5.cloned.1.call-start = ((), (), s32[]{:S(2)}) async-start(), calls=%async_computation.5 | async-start | bytes 4456448 | tf_op jit(solution)/shard_map/all_gather | solution.py:85
  353.2 301.4 %all-reduce.2.cloned.1.call-start = ((), (), s32[]{:S(2)}) async-start(), calls=%async_computation.4 | async-start | bytes 524288 | tf_op jit(solution)/shard_map/psum | solution.py:94
  353.4 16.7 %copy-start.5 = (f32[512,256]{1,0:T(8,128)S(1)}, f32[512,256]{1,0:T(8,128)}, u32[]{:S(2)}) copy-start(f32[512,256]{1,0:T(8,128)} %reduce-scatter.3.cloned.1.call-done) | copy-start | bytes 1572868
  371.1 289.5 %reduce-scatter.5.cloned.1.call-start = ((), (), s32[]{:S(2)}) async-start(), calls=%async_computation.6 | async-start | bytes 2359296 | tf_op jit(solution)/shard_map/reduce_scatter | solution.py:91
  579.9 80.7 %copy-start.1 = (bf16[256,256]{1,0:T(8,128)(2,1)S(1)}, bf16[256,256]{1,0:T(8,128)(2,1)}, u32[]{:S(2)}) copy-start(bf16[256,256]{1,0:T(8,128)(2,1)} %param.13) | copy-start | bytes 393220
  (38 other events, 88.7 us)
Sparse Core Ops, SparseCore 0:
  10.4 57.4 all-gather.2
  276.7 73.2 reduce-scatter.2
  353.3 35.9 all-gather.4
  394.4 141.9 all-reduce.1
  584.8 75.7 reduce-scatter.4
where the time goes:
time: 669 us; the launch traced here: 667 us
  matrix products  231 us (35%)
  local copies, waits for them, and re-layouts  174 us (26%)
  waiting for transfers between devices  155 us (23%)
  blocking collectives  69.3 us (10%)
  other arithmetic  21.7 us (3%)
  between operations  13.8 us (2%)
    dot_general x24, matrix products, one_group(): jnp.dot(placer.T, contrib.reshape(group, block * width), precision=lax.Pr...  134 us
    while x168, local copies, waits for them, and re-layouts  132 us
    reduce_scatter x1, waiting for transfers between devices, per_device(): summed = lax.psum_scatter(term, 'col', scatter_dimension=0, tiled=True)  73.4 us
    psum x1, blocking collectives, per_device(): lax.psum((local_weight, local_bias), ('row', 'col'))  69.3 us
    all_gather x1, waiting for transfers between devices, per_device(): panel = lax.all_gather(features, 'row', axis=0, tiled=True)  58.5 us
    dot_general x24, matrix products, one_group(): fetched = jnp.dot(picker, flat_source, preferred_element_type=jnp.float32)  44.3 us
    dot_general x12, matrix products, one_group(): jnp.einsum('tij,tjf->tif', tile_group, fetched, preferred_element_type=jn...  25 us
    dot_general x12, matrix products, one_group(): jnp.einsum('tji,tjf->tif', tile_group, fetched, preferred_element_type=jn...  23.2 us
  transfers between devices with their start and end apart: 5, of which 4 were waited for; matrix products, arithmetic and copies ran while one was open for 29% of the time, Pallas kernels for 0%

commit v1 on v0

--- a/solution.py
+++ b/solution.py
@@ -1,56 +1,86 @@
+import functools
 import math
 
 import jax
 import jax.numpy as jnp
 from jax import lax
+from jax.experimental import pallas as pl
+from jax.experimental.pallas import tpu as pltpu
 from jax.sharding import PartitionSpec as P
+
+GROUP = 32
+
+
+def accumulate_kernel(backward, dest_ref, source_ref, count_ref, tiles_ref, panel_ref, out_ref):
+    step = pl.program_id(0)
+    group = tiles_ref.shape[0]
+    out_blocks = out_ref.shape[0]
+    in_blocks = panel_ref.shape[0]
+
+    @pl.when(step == 0)
+    def _():
+        out_ref[...] = jnp.zeros_like(out_ref)
+
+    base = step * group
+    live_count = count_ref[0]
+
+    def one_tile(i, carry):
+        slot = base + i
+
+        @pl.when(slot < live_count)
+        def _():
+            if backward:
+                fetch = jnp.clip(dest_ref[slot], 0, in_blocks - 1)
+                target = jnp.clip(source_ref[slot], 0, out_blocks - 1)
+                contrib = lax.dot_general(
+                    tiles_ref[i], panel_ref[fetch], (((0,), (0,)), ((), ())),
+                    preferred_element_type=jnp.float32,
+                )
+            else:
+                fetch = jnp.clip(source_ref[slot], 0, in_blocks - 1)
+                target = jnp.clip(dest_ref[slot], 0, out_blocks - 1)
+                contrib = jnp.dot(
+                    tiles_ref[i], panel_ref[fetch], preferred_element_type=jnp.float32
+                )
+            out_ref[target] += contrib
+
+        return carry
+
+    lax.fori_loop(0, group, one_tile, 0)
 
 
 def accumulate(tiles, dest_ids, source_ids, live_count, source_blocks, out_blocks, backward):
-    slots = tiles.shape[0]
-    group = math.gcd(slots, 32)
-    block = tiles.shape[-1]
+    slots, block, _ = tiles.shape
     width = source_blocks.shape[-1]
     in_blocks = source_blocks.shape[0]
-    flat_source = source_blocks.reshape(in_blocks, block * width)
-    in_range = jnp.arange(in_blocks, dtype=jnp.int32)
-    out_range = jnp.arange(out_blocks, dtype=jnp.int32)
+    group = math.gcd(slots, GROUP)
+    steps = slots // group
 
-    def one_group(step_index, total):
-        start = step_index * group
-        tile_group = lax.dynamic_slice_in_dim(tiles, start, group, 0)
-        dest_group = lax.dynamic_slice_in_dim(dest_ids, start, group, 0)
-        source_group = lax.dynamic_slice_in_dim(source_ids, start, group, 0)
-        live = start + jnp.arange(group, dtype=jnp.int32) < live_count
-        if backward:
-            fetch_ids = dest_group
-            target = source_group
-        else:
-            fetch_ids = source_group
-            target = dest_group
-        picker = (fetch_ids[:, None] == in_range[None, :]).astype(jnp.bfloat16)
-        fetched = jnp.dot(picker, flat_source, preferred_element_type=jnp.float32)
-        fetched = fetched.astype(jnp.bfloat16).reshape(group, block, width)
-        if backward:
-            contrib = jnp.einsum(
-                "tji,tjf->tif", tile_group, fetched, preferred_element_type=jnp.float32
-            )
-        else:
-            contrib = jnp.einsum(
-                "tij,tjf->tif", tile_group, fetched, preferred_element_type=jnp.float32
-            )
-        placer = ((target[:, None] == out_range[None, :]) & live[:, None]).astype(jnp.float32)
-        added = jnp.dot(
-            placer.T,
-            contrib.reshape(group, block * width),
-            precision=lax.Precision.HIGHEST,
-            preferred_element_type=jnp.float32,
-        )
-        return total + added
+    def tile_map(g, dest, source, count):
+        last = jnp.maximum(count[0] - 1, 0) // group
+        return (jnp.minimum(g, last), 0, 0)
 
-    start_total = jnp.zeros((out_blocks, block * width), jnp.float32)
-    result = lax.fori_loop(0, slots // group, one_group, start_total)
-    return result.reshape(out_blocks, block, width)
+    flops = 2 * slots * block * block * width
+    bytes_accessed = tiles.size * 2 + source_blocks.size * 2 + out_blocks * block * width * 4
+    return pl.pallas_call(
+        functools.partial(accumulate_kernel, backward),
+        out_shape=jax.ShapeDtypeStruct((out_blocks, block, width), jnp.float32),
+        grid_spec=pltpu.PrefetchScalarGridSpec(
+            num_scalar_prefetch=3,
+            grid=(steps,),
+            in_specs=[
+                pl.BlockSpec((group, block, block), tile_map),
+                pl.BlockSpec((in_blocks, block, width), lambda g, d, s, c: (0, 0, 0)),
+            ],
+            out_specs=pl.BlockSpec((out_blocks, block, width), lambda g, d, s, c: (0, 0, 0)),
+        ),
+        compiler_params=pltpu.CompilerParams(
+            dimension_semantics=("arbitrary",), vmem_limit_bytes=60 * 1024 * 1024
+        ),
+        cost_estimate=pl.CostEstimate(
+            flops=flops, transcendentals=0, bytes_accessed=bytes_accessed
+        ),
+    )(dest_ids, source_ids, live_count.reshape(1), tiles, source_blocks)
 
 
 def per_device(features, weight, bias, cotangent, tiles, tile_rows, tile_cols, tile_counts):

time: 669 us -> 478 us (0.71)
  matrix products: 231 us -> 4.17 us
  local copies, waits for them, and re-layouts: 174 us -> 0.02 us
  waiting for transfers between devices: 155 us -> 289 us
  blocking collectives: 69.3 us -> 132 us
  Pallas kernels: 0 us -> 29.4 us
  other arithmetic: 21.7 us -> 8.57 us
    dot_general x72 -> x0, matrix products: 227 us -> none  [the longest x24 134 us: one_group(): jnp.dot(placer.T, contrib.reshape(group, block * width), precision=lax.Pr...]
    while x168 -> x0, local copies, waits for them, and re-layouts: 132 us -> none
    reduce_scatter x1, waiting for transfers between devices: 4.32 us -> 71.8 us  [per_device(): lax.psum_scatter(term_back.astype(jnp.bfloat16), 'row', scatter_dimension...]
    psum x1, blocking collectives: 69.3 us -> 132 us  [per_device(): lax.psum((local_weight, local_bias), ('row', 'col'))]
    reduce_scatter x1, waiting for transfers between devices: 73.4 us -> 125 us  [per_device(): summed = lax.psum_scatter(term, 'col', scatter_dimension=0, tiled=True)]
    pallas_call x0 -> x2, Pallas kernels: none -> 29.4 us  [accumulate(): pl.pallas_call(functools.partial(accumulate_kernel, backward), out_shape=...]
    another operation x3 -> x0, local copies, waits for them, and re-layouts: 19.5 us -> none  [the longest x2 10.2 us: accumulate(): flat_source = source_blocks.reshape(in_blocks, block * width)]
    all_gather x1, waiting for transfers between devices: 18.1 us -> 35.1 us  [per_device(): grad_panel = lax.all_gather(grad_agg, 'col', axis=0, tiled=True)]
  transfers between devices with their start and end apart: 5 -> 5, of which waited for: 4 -> 4; matrix products, arithmetic and copies ran while one was open for 29% -> 2% of each run, Pallas kernels for 0% -> 3%
where the time goes in v1:
time: 478 us; the launch traced here: 477 us
  waiting for transfers between devices  289 us (60%)
  blocking collectives  132 us (28%)
  Pallas kernels  29.4 us (6%)
  between operations  14.5 us (3%)
  other arithmetic  8.57 us (2%)
    psum x1, blocking collectives, per_device(): lax.psum((local_weight, local_bias), ('row', 'col'))  132 us
    reduce_scatter x1, waiting for transfers between devices, per_device(): summed = lax.psum_scatter(term, 'col', scatter_dimension=0, tiled=True)  125 us
    reduce_scatter x1, waiting for transfers between devices, per_device(): lax.psum_scatter(term_back.astype(jnp.bfloat16), 'row', scatter_dimension...  71.8 us
    all_gather x1, waiting for transfers between devices, per_device(): panel = lax.all_gather(features, 'row', axis=0, tiled=True)  56.8 us
    all_gather x1, waiting for transfers between devices, per_device(): grad_panel = lax.all_gather(grad_agg, 'col', axis=0, tiled=True)  35.1 us
    pallas_call x2, Pallas kernels, accumulate(): pl.pallas_call(functools.partial(accumulate_kernel, backward), out_shape=...  29.4 us
  transfers between devices with their start and end apart: 5, of which 4 were waited for; matrix products, arithmetic and copies ran while one was open for 2% of the time, Pallas kernels for 3%

profile of v1, /device:TPU:0, one launch (start us, length us, event | category | flops | bytes accessed | tf_op | source)
XLA Modules:
  0.0 477.4 jit_solution(15845919674759865017)
XLA Ops:
  7.2 0.0 copy-start
  7.2 0.0 all-gather.3.cloned.1.call-start
  7.2 0.7 all-gather.3.cloned.1.call-update
  7.9 0.0 reduce-scatter.3.cloned.1.call-start
  8.6 1.3 reduce.dest_ref
  9.9 1.2 reduce.1.source_ref
  11.1 56.8 %all-gather.3.cloned.1.call-done = bf16[4096,256]{1,0:T(8,128)(2,1)} async-done(((bf16[512,256]{1,0:T(8,128)(2,1)}), bf16[4096,256]{1,0:T(8,128)(2,1)}) %all-gather.3.cloned.1.call-update) | async-done | bytes 2097168 | tf_op jit(solution)/shard_map/all_gather | solution.py:99
  67.9 14.6 %shard_map.111 = f32[64,128,256]{2,1,0:T(8,128)} custom-call(s32[384]{0:T(512)} %reduce.dest_ref, s32[384]{0:T(512)} %reduce.1.source_ref, s32[1]{0:T(128)} %bitcast.10.count_ref, bf16[384,128,128]{2,1,0:T(8,128)(2,1)} %bitcast.12, bf16[32,128,256]{2,1,0:T(8,128)(2,1)} %bitcast.17), custom_call_target="tpu_custom_call" | custom-call | flops 3221225472 | bytes 23068672 | tf_op jit(solution)/shard_map/pallas_call | solution.py:65
  82.5 0.0 copy-start.2
  82.5 0.0 copy-start.3
  82.5 0.0 reduce-scatter.3.cloned.1.call-update
  82.5 0.0 all-gather.5.cloned.1.call-start
  82.6 124.6 %reduce-scatter.3.cloned.1.call-done = f32[512,256]{1,0:T(8,128)} async-done(((f32[8192,256]{1,0:T(8,128)}), f32[512,256]{1,0:T(8,128)}) %reduce-scatter.3.cloned.1.call-update) | async-done | bytes 524304 | tf_op jit(solution)/shard_map/reduce_scatter | solution.py:105
  207.2 0.0 copy-done
  207.2 0.0 copy-done.2
  207.2 0.0 copy-done.3
  207.2 2.2 convert_reduce_fusion
  209.4 1.0 convolution_convert_fusion
  210.4 0.0 all-gather.5.cloned.1.call-update
  210.4 0.0 all-reduce.2.cloned.1.call-start
  210.4 0.0 copy-done.1
  210.5 1.0 fusion
  211.4 0.0 all-reduce.2.cloned.1.call-update
  211.5 0.0 reduce-scatter.5.cloned.1.call-start
  211.5 35.1 %all-gather.5.cloned.1.call-done = bf16[8192,256]{1,0:T(8,128)(2,1)} async-done(((bf16[512,256]{1,0:T(8,128)(2,1)}), bf16[8192,256]{1,0:T(8,128)(2,1)}) %all-gather.5.cloned.1.call-update) | async-done | bytes 4194320 | tf_op jit(solution)/shard_map/all_gather | solution.py:115
  246.6 14.8 %shard_map.112 = f32[32,128,256]{2,1,0:T(8,128)} custom-call(s32[384]{0:T(512)} %reduce.dest_ref, s32[384]{0:T(512)} %reduce.1.source_ref, s32[1]{0:T(128)} %bitcast.11.count_ref, bf16[384,128,128]{2,1,0:T(8,128)(2,1)} %bitcast.13, bf16[64,128,256]{2,1,0:T(8,128)(2,1)} %bitcast.16), custom_call_target="tpu_custom_call" | custom-call | flops 3221225472 | bytes 20971520 | tf_op jit(solution)/shard_map/pallas_call | solution.py:65
  261.4 3.8 convert_element_type.30
  265.2 0.0 reduce-scatter.5.cloned.1.call-update
  265.2 131.5 %psum.15 = f32[256]{0:T(256)S(1)} all-reduce(f32[256]{0:T(256)S(1)} %get-tuple-element.4), channel_id=1, replica_groups=mesh['row'=8,'col'=16] {'row','col'}, use_global_device_ids=true, to_apply=%region_3.4 | all-reduce | flops 256 | bytes 2048 | tf_op jit(solution)/shard_map/psum | solution.py:124
  396.8 0.6 broadcast_multiply_fusion.1
  397.3 1.7 broadcast_multiply_fusion
  399.0 71.8 %reduce-scatter.5.cloned.1.call-done = bf16[512,256]{1,0:T(8,128)(2,1)} async-done(((bf16[4096,256]{1,0:T(8,128)(2,1)}), bf16[512,256]{1,0:T(8,128)(2,1)}) %reduce-scatter.5.cloned.1.call-update) | async-done | bytes 262160 | tf_op jit(solution)/shard_map/reduce_scatter | solution.py:121
  (2 shorter events, 0.0 us)
Async XLA Ops:
  7.2 200.0 %copy-start = (bf16[256,256]{1,0:T(8,128)(2,1)S(1)}, bf16[256,256]{1,0:T(8,128)(2,1)}, u32[]{:S(2)}) copy-start(bf16[256,256]{1,0:T(8,128)(2,1)} %param.9) | copy-start | bytes 393220
  7.2 60.7 %all-gather.3.cloned.1.call-start = ((), (), s32[]{:S(2)}) async-start(), calls=%async_computation.2 | async-start | bytes 2359296 | tf_op jit(solution)/shard_map/all_gather | solution.py:99
  7.9 199.2 %reduce-scatter.3.cloned.1.call-start = ((), (), s32[]{:S(2)}) async-start(), calls=%async_computation.3 | async-start | bytes 8912896 | tf_op jit(solution)/shard_map/reduce_scatter | solution.py:105
  82.5 124.7 %copy-start.2 = (bf16[512,256]{1,0:T(8,128)(2,1)S(1)}, bf16[512,256]{1,0:T(8,128)(2,1)}, u32[]{:S(2)}) copy-start(bf16[512,256]{1,0:T(8,128)(2,1)} %param.11) | copy-start | bytes 786436
  82.5 124.7 %copy-start.3 = (f32[256]{0:T(256)S(1)}, f32[256]{0:T(256)}, u32[]{:S(2)}) copy-start(f32[256]{0:T(256)} %param.10) | copy-start | bytes 3076
  82.5 164.1 %all-gather.5.cloned.1.call-start = ((), (), s32[]{:S(2)}) async-start(), calls=%async_computation.5 | async-start | bytes 4456448 | tf_op jit(solution)/shard_map/all_gather | solution.py:115
  207.2 3.3 copy-start.1
  210.4 186.9 %all-reduce.2.cloned.1.call-start = ((), (), s32[]{:S(2)}) async-start(), calls=%async_computation.4 | async-start | bytes 524288 | tf_op jit(solution)/shard_map/psum | solution.py:124
  211.5 259.4 %reduce-scatter.5.cloned.1.call-start = ((), (), s32[]{:S(2)}) async-start(), calls=%async_computation.6 | async-start | bytes 2359296 | tf_op jit(solution)/shard_map/reduce_scatter | solution.py:121
Sparse Core Ops, SparseCore 0:
  10.3 57.4 all-gather.2
  82.6 124.4 reduce-scatter.2
  210.5 36.0 all-gather.4
  251.8 142.2 all-reduce.1
  398.2 72.5 reduce-scatter.4

commit v2 on v1

--- a/solution.py
+++ b/solution.py
@@ -83,6 +83,16 @@
     )(dest_ids, source_ids, live_count.reshape(1), tiles, source_blocks)
 
 
+def butterfly_sum(value, axis):
+    size = lax.axis_size(axis)
+    distance = 1
+    while distance < size:
+        pairs = [(i, i ^ distance) for i in range(size)]
+        value = value + lax.ppermute(value, axis, pairs)
+        distance *= 2
+    return value
+
+
 def per_device(features, weight, bias, cotangent, tiles, tile_rows, tile_cols, tile_counts):
     tile_set = tiles[0, 0]
     dest_ids = tile_rows[0, 0]
@@ -102,7 +112,7 @@
         tile_set, dest_ids, source_ids, live_count, panel_blocks, blocks_down, False
     )
     term = partial_value.reshape(blocks_down * block, width)
-    summed = lax.psum_scatter(term, "col", scatter_dimension=0, tiled=True)
+    summed = lax.psum_scatter(term.astype(jnp.bfloat16), "col", scatter_dimension=0, tiled=True)
     aggregated = summed.astype(jnp.bfloat16)
     preact = jnp.dot(aggregated, weight, preferred_element_type=jnp.float32) + bias
     hidden = jax.nn.silu(preact).astype(jnp.bfloat16)
@@ -121,9 +131,10 @@
     grad_features = lax.psum_scatter(
         term_back.astype(jnp.bfloat16), "row", scatter_dimension=0, tiled=True
     )
-    grad_weight, grad_bias = lax.psum((local_weight, local_bias), ("row", "col"))
-    grad_weight = grad_weight * factor
-    grad_bias = grad_bias * factor
+    packed = jnp.concatenate([local_weight, local_bias[None, :]], axis=0)
+    packed = butterfly_sum(butterfly_sum(packed, "col"), "row")
+    grad_weight = packed[:width] * factor
+    grad_bias = packed[width] * factor
     return (hidden, grad_weight, grad_bias, grad_features)
 
 

time: 478 us -> 414 us (0.87)
  blocking collectives: 132 us -> 0 us
  starting transfers between devices: 0.2 us -> 68.4 us
  waiting for transfers between devices: 289 us -> 260 us
  Pallas kernels: 29.4 us -> 53.3 us
  other arithmetic: 8.57 us -> 13.9 us
    psum x1 -> x0, blocking collectives: 132 us -> none  [per_device(): lax.psum((local_weight, local_bias), ('row', 'col'))]
    ppermute x0 -> x7, starting transfers between devices: none -> 68.3 us  [butterfly_sum(): value = value + lax.ppermute(value, axis, pairs)]
    reduce_scatter x1, waiting for transfers between devices: 71.8 us -> 20.3 us  [per_device(): lax.psum_scatter(term_back.astype(jnp.bfloat16), 'row', scatter_dimension...]
    ppermute x0 -> x7, waiting for transfers between devices: none -> 40.4 us  [butterfly_sum(): value = value + lax.ppermute(value, axis, pairs)]
    pallas_call x2, Pallas kernels: 29.4 us -> 53.3 us  [accumulate(): pl.pallas_call(functools.partial(accumulate_kernel, backward), out_shape=...]
    reduce_scatter x1, waiting for transfers between devices: 125 us -> 106 us  [per_device(): lax.psum_scatter(term.astype(jnp.bfloat16), 'col', scatter_dimension=0, t...]
    convert_element_type x0 -> x1, other arithmetic: none -> 5.97 us  [per_device(): term.astype(jnp.bfloat16)]
  transfers between devices with their start and end apart: 5 -> 11, of which waited for: 4 -> 11; matrix products, arithmetic and copies ran while one was open for 2% -> 1% of each run, Pallas kernels for 3% -> 0%
where the time goes in v2:
time: 414 us; the launch traced here: 413 us
  waiting for transfers between devices  260 us (63%)
  starting transfers between devices  68.4 us (17%)
  Pallas kernels  53.3 us (13%)
  between operations  14.5 us (4%)
  other arithmetic  13.9 us (3%)
    reduce_scatter x1, waiting for transfers between devices, per_device(): lax.psum_scatter(term.astype(jnp.bfloat16), 'col', scatter_dimension=0, t...  106 us
    ppermute x7, starting transfers between devices, butterfly_sum(): value = value + lax.ppermute(value, axis, pairs)  68.3 us
    all_gather x1, waiting for transfers between devices, per_device(): panel = lax.all_gather(features, 'row', axis=0, tiled=True)  56.7 us
    pallas_call x2, Pallas kernels, accumulate(): pl.pallas_call(functools.partial(accumulate_kernel, backward), out_shape=...  53.3 us
    ppermute x7, waiting for transfers between devices, butterfly_sum(): value = value + lax.ppermute(value, axis, pairs)  40.4 us
    all_gather x1, waiting for transfers between devices, per_device(): grad_panel = lax.all_gather(grad_agg, 'col', axis=0, tiled=True)  35.9 us
    reduce_scatter x1, waiting for transfers between devices, per_device(): lax.psum_scatter(term_back.astype(jnp.bfloat16), 'row', scatter_dimension...  20.3 us
  transfers between devices with their start and end apart: 11, of which 11 were waited for; matrix products, arithmetic and copies ran while one was open for 1% of the time, Pallas kernels for 0%

profile of v2, /device:TPU:0, one launch (start us, length us, event | category | flops | bytes accessed | tf_op | source)
XLA Modules:
  0.0 413.4 jit_solution(15244938631344479589)
XLA Ops:
  7.2 0.7 all-gather.3.cloned.1.call-update
  8.6 1.3 reduce.dest_ref
  9.9 1.3 reduce.1.source_ref
  11.1 56.7 %all-gather.3.cloned.1.call-done = bf16[4096,256]{1,0:T(8,128)(2,1)} async-done(((bf16[512,256]{1,0:T(8,128)(2,1)}), bf16[4096,256]{1,0:T(8,128)(2,1)}) %all-gather.3.cloned.1.call-update) | async-done | bytes 2097168 | tf_op jit(solution)/shard_map/all_gather | solution.py:109
  67.9 25.0 %shard_map.111 = f32[64,128,256]{2,1,0:T(8,128)} custom-call(s32[384]{0:T(512)} %reduce.dest_ref, s32[384]{0:T(512)} %reduce.1.source_ref, s32[1]{0:T(128)} %bitcast.14.count_ref, bf16[384,128,128]{2,1,0:T(8,128)(2,1)} %bitcast.16, bf16[32,128,256]{2,1,0:T(8,128)(2,1)} %bitcast.21), custom_call_target="tpu_custom_call" | custom-call | flops 3221225472 | bytes 23068672 | tf_op jit(solution)/shard_map/pallas_call | solution.py:65
  92.9 6.0 %convert_element_type.27 = bf16[64,128,256]{2,1,0:T(8,128)(2,1)} convert(f32[64,128,256]{2,1,0:T(8,128)} %shard_map.111) | non-fusion elementwise | flops 2097152 | bytes 12582912 | tf_op jit(solution)/shard_map/convert_element_type | solution.py:115
  98.9 0.0 all-gather.5.cloned.1.call-start
  98.9 105.9 %reduce-scatter.3.cloned.1.call-done = bf16[512,256]{1,0:T(8,128)(2,1)} async-done(((bf16[8192,256]{1,0:T(8,128)(2,1)}), bf16[512,256]{1,0:T(8,128)(2,1)}) %reduce-scatter.3.cloned.1.call-update) | async-done | bytes 262160 | tf_op jit(solution)/shard_map/reduce_scatter | solution.py:115
  204.8 2.1 convert_reduce_fusion
  206.9 1.0 convolution_convert_fusion
  207.9 35.9 %all-gather.5.cloned.1.call-done = bf16[8192,256]{1,0:T(8,128)(2,1)} async-done(((bf16[512,256]{1,0:T(8,128)(2,1)}), bf16[8192,256]{1,0:T(8,128)(2,1)}) %all-gather.5.cloned.1.call-update) | async-done | bytes 4194320 | tf_op jit(solution)/shard_map/all_gather | solution.py:125
  243.8 28.3 %shard_map.112 = f32[32,128,256]{2,1,0:T(8,128)} custom-call(s32[384]{0:T(512)} %reduce.dest_ref, s32[384]{0:T(512)} %reduce.1.source_ref, s32[1]{0:T(128)} %bitcast.15.count_ref, bf16[384,128,128]{2,1,0:T(8,128)(2,1)} %bitcast.17, bf16[64,128,256]{2,1,0:T(8,128)(2,1)} %bitcast.20), custom_call_target="tpu_custom_call" | custom-call | flops 3221225472 | bytes 20971520 | tf_op jit(solution)/shard_map/pallas_call | solution.py:65
  272.1 3.9 convert_element_type.34
  276.0 0.3 fusion.1
  276.3 0.1 collective-permute-start
  276.4 1.5 collective-permute-done
  277.9 0.1 fusion
  278.0 19.5 %collective-permute-start.1 = (f32[257,256]{1,0:T(8,128)S(1)}, f32[257,256]{1,0:T(8,128)S(1)}, u32[]{:S(2)}, u32[]{:S(2)}) collective-permute-start(f32[257,256]{1,0:T(8,128)S(1)} %fusion), channel_id=1, source_target_pairs={{0,2},{1,3},{2,0},{3,1},{4,6},{5,7},{6,4},{7,5},{8,10},{9,11},{10,... | collective-permute-start | bytes 789512 | tf_op jit(solution)/shard_map/ppermute | solution.py:91
  297.5 6.8 %collective-permute-done.1 = f32[257,256]{1,0:T(8,128)S(1)} collective-permute-done((f32[257,256]{1,0:T(8,128)S(1)}, f32[257,256]{1,0:T(8,128)S(1)}, u32[]{:S(2)}, u32[]{:S(2)}) %collective-permute-start.1) | collective-permute-done | bytes 263200 | tf_op jit(solution)/shard_map/ppermute | solution.py:91
  304.3 20.6 %collective-permute-start.2 = (f32[257,256]{1,0:T(8,128)S(1)}, f32[257,256]{1,0:T(8,128)S(1)}, u32[]{:S(2)}, u32[]{:S(2)}) collective-permute-start(f32[257,256]{1,0:T(8,128)S(1)} %add.46), channel_id=1, source_target_pairs={{0,4},{1,5},{2,6},{3,7},{4,0},{5,1},{6,2},{7,3},{8,12},{9,13},{10,... | collective-permute-start | bytes 789512 | tf_op jit(solution)/shard_map/ppermute | solution.py:91
  324.9 6.0 %collective-permute-done.2 = f32[257,256]{1,0:T(8,128)S(1)} collective-permute-done((f32[257,256]{1,0:T(8,128)S(1)}, f32[257,256]{1,0:T(8,128)S(1)}, u32[]{:S(2)}, u32[]{:S(2)}) %collective-permute-start.2) | collective-permute-done | bytes 263200 | tf_op jit(solution)/shard_map/ppermute | solution.py:91
  330.9 19.0 %collective-permute-start.3 = (f32[257,256]{1,0:T(8,128)S(1)}, f32[257,256]{1,0:T(8,128)S(1)}, u32[]{:S(2)}, u32[]{:S(2)}) collective-permute-start(f32[257,256]{1,0:T(8,128)S(1)} %add.47), channel_id=1, source_target_pairs={{0,8},{1,9},{2,10},{3,11},{4,12},{5,13},{6,14},{7,15},{8,0},{9,1},... | collective-permute-start | bytes 789512 | tf_op jit(solution)/shard_map/ppermute | solution.py:91
  349.9 8.7 %collective-permute-done.3 = f32[257,256]{1,0:T(8,128)S(1)} collective-permute-done((f32[257,256]{1,0:T(8,128)S(1)}, f32[257,256]{1,0:T(8,128)S(1)}, u32[]{:S(2)}, u32[]{:S(2)}) %collective-permute-start.3) | collective-permute-done | bytes 263200 | tf_op jit(solution)/shard_map/ppermute | solution.py:91
  358.7 1.9 collective-permute-start.4
  360.6 6.6 %collective-permute-done.4 = f32[257,256]{1,0:T(8,128)S(1)} collective-permute-done((f32[257,256]{1,0:T(8,128)S(1)}, f32[257,256]{1,0:T(8,128)S(1)}, u32[]{:S(2)}, u32[]{:S(2)}) %collective-permute-start.4) | collective-permute-done | bytes 263200 | tf_op jit(solution)/shard_map/ppermute | solution.py:91
  367.3 4.0 collective-permute-start.5
  371.3 5.4 %collective-permute-done.5 = f32[257,256]{1,0:T(8,128)S(1)} collective-permute-done((f32[257,256]{1,0:T(8,128)S(1)}, f32[257,256]{1,0:T(8,128)S(1)}, u32[]{:S(2)}, u32[]{:S(2)}) %collective-permute-start.5) | collective-permute-done | bytes 263200 | tf_op jit(solution)/shard_map/ppermute | solution.py:91
  376.8 3.1 collective-permute-start.6
  379.9 5.4 %collective-permute-done.6 = f32[257,256]{1,0:T(8,128)S(1)} collective-permute-done((f32[257,256]{1,0:T(8,128)S(1)}, f32[257,256]{1,0:T(8,128)S(1)}, u32[]{:S(2)}, u32[]{:S(2)}) %collective-permute-start.6) | collective-permute-done | bytes 263200 | tf_op jit(solution)/shard_map/ppermute | solution.py:91
  385.3 0.6 slice_multiply_fusion.1
  385.9 0.7 slice_multiply_fusion
  386.6 20.3 %reduce-scatter.5.cloned.1.call-done = bf16[512,256]{1,0:T(8,128)(2,1)} async-done(((bf16[4096,256]{1,0:T(8,128)(2,1)}), bf16[512,256]{1,0:T(8,128)(2,1)}) %reduce-scatter.5.cloned.1.call-update) | async-done | bytes 262160 | tf_op jit(solution)/shard_map/reduce_scatter | solution.py:131
  (21 shorter events, 0.4 us)
Async XLA Ops:
  7.2 197.7 %copy-start = (bf16[256,256]{1,0:T(8,128)(2,1)S(1)}, bf16[256,256]{1,0:T(8,128)(2,1)}, u32[]{:S(2)}) copy-start(bf16[256,256]{1,0:T(8,128)(2,1)} %param.9) | copy-start | bytes 393220
  7.2 60.7 %all-gather.3.cloned.1.call-start = ((), (), s32[]{:S(2)}) async-start(), calls=%async_computation.2 | async-start | bytes 2359296 | tf_op jit(solution)/shard_map/all_gather | solution.py:109
  7.9 196.9 %reduce-scatter.3.cloned.1.call-start = ((), (), s32[]{:S(2)}) async-start(), calls=%async_computation.3 | async-start | bytes 4456448 | tf_op jit(solution)/shard_map/reduce_scatter | solution.py:115
  98.8 106.0 %copy-start.2 = (bf16[512,256]{1,0:T(8,128)(2,1)S(1)}, bf16[512,256]{1,0:T(8,128)(2,1)}, u32[]{:S(2)}) copy-start(bf16[512,256]{1,0:T(8,128)(2,1)} %param.11) | copy-start | bytes 786436
  98.8 106.0 %copy-start.3 = (f32[256]{0:T(256)S(1)}, f32[256]{0:T(256)}, u32[]{:S(2)}) copy-start(f32[256]{0:T(256)} %param.10) | copy-start | bytes 3076
  98.9 145.0 %all-gather.5.cloned.1.call-start = ((), (), s32[]{:S(2)}) async-start(), calls=%async_computation.4 | async-start | bytes 4456448 | tf_op jit(solution)/shard_map/all_gather | solution.py:125
  207.9 199.0 %reduce-scatter.5.cloned.1.call-start = ((), (), s32[]{:S(2)}) async-start(), calls=%async_computation.5 | async-start | bytes 2359296 | tf_op jit(solution)/shard_map/reduce_scatter | solution.py:131
  272.1 3.9 copy-start.1
  276.3 1.6 collective-permute-start
  278.0 26.3 %collective-permute-start.1 = (f32[257,256]{1,0:T(8,128)S(1)}, f32[257,256]{1,0:T(8,128)S(1)}, u32[]{:S(2)}, u32[]{:S(2)}) collective-permute-start(f32[257,256]{1,0:T(8,128)S(1)} %fusion), channel_id=1, source_target_pairs={{0,2},{1,3},{2,0},{3,1},{4,6},{5,7},{6,4},{7,5},{8,10},{9,11},{10,... | collective-permute-start | bytes 789512 | tf_op jit(solution)/shard_map/ppermute | solution.py:91
  304.3 26.5 %collective-permute-start.2 = (f32[257,256]{1,0:T(8,128)S(1)}, f32[257,256]{1,0:T(8,128)S(1)}, u32[]{:S(2)}, u32[]{:S(2)}) collective-permute-start(f32[257,256]{1,0:T(8,128)S(1)} %add.46), channel_id=1, source_target_pairs={{0,4},{1,5},{2,6},{3,7},{4,0},{5,1},{6,2},{7,3},{8,12},{9,13},{10,... | collective-permute-start | bytes 789512 | tf_op jit(solution)/shard_map/ppermute | solution.py:91
  330.9 27.7 %collective-permute-start.3 = (f32[257,256]{1,0:T(8,128)S(1)}, f32[257,256]{1,0:T(8,128)S(1)}, u32[]{:S(2)}, u32[]{:S(2)}) collective-permute-start(f32[257,256]{1,0:T(8,128)S(1)} %add.47), channel_id=1, source_target_pairs={{0,8},{1,9},{2,10},{3,11},{4,12},{5,13},{6,14},{7,15},{8,0},{9,1},... | collective-permute-start | bytes 789512 | tf_op jit(solution)/shard_map/ppermute | solution.py:91
  358.7 8.6 %collective-permute-start.4 = (f32[257,256]{1,0:T(8,128)S(1)}, f32[257,256]{1,0:T(8,128)S(1)}, u32[]{:S(2)}, u32[]{:S(2)}) collective-permute-start(f32[257,256]{1,0:T(8,128)S(1)} %add.48), channel_id=1, source_target_pairs={{0,16},{16,0},{32,48},{48,32},{64,80},{80,64},{96,112},{112,96},{1... | collective-permute-start | bytes 789512 | tf_op jit(solution)/shard_map/ppermute | solution.py:91
  367.3 9.5 %collective-permute-start.5 = (f32[257,256]{1,0:T(8,128)S(1)}, f32[257,256]{1,0:T(8,128)S(1)}, u32[]{:S(2)}, u32[]{:S(2)}) collective-permute-start(f32[257,256]{1,0:T(8,128)S(1)} %add.49), channel_id=1, source_target_pairs={{0,32},{16,48},{32,0},{48,16},{64,96},{80,112},{96,64},{112,80},{1... | collective-permute-start | bytes 789512 | tf_op jit(solution)/shard_map/ppermute | solution.py:91
  376.8 8.5 %collective-permute-start.6 = (f32[257,256]{1,0:T(8,128)S(1)}, f32[257,256]{1,0:T(8,128)S(1)}, u32[]{:S(2)}, u32[]{:S(2)}) collective-permute-start(f32[257,256]{1,0:T(8,128)S(1)} %add.50), channel_id=1, source_target_pairs={{0,64},{16,80},{32,96},{48,112},{64,0},{80,16},{96,32},{112,48},{1... | collective-permute-start | bytes 789512 | tf_op jit(solution)/shard_map/ppermute | solution.py:91
Sparse Core Ops, SparseCore 0:
  10.3 57.4 all-gather.2
  99.0 105.7 reduce-scatter.2
  208.0 35.7 all-gather.4
  276.1 130.7 reduce-scatter.4

commit v3 on v2

--- a/solution.py
+++ b/solution.py
@@ -93,6 +93,18 @@
     return value
 
 
+def gather_all(value, axis, size):
+    spread = jnp.broadcast_to(value[None], (size,) + value.shape)
+    got = lax.all_to_all(spread, axis, 0, 0, tiled=False)
+    return got.reshape((size * value.shape[0],) + value.shape[1:])
+
+
+def scatter_sum(value, axis, size):
+    parts = value.reshape((size, value.shape[0] // size) + value.shape[1:])
+    got = lax.all_to_all(parts, axis, 0, 0, tiled=False)
+    return jnp.sum(got.astype(jnp.float32), axis=0)
+
+
 def per_device(features, weight, bias, cotangent, tiles, tile_rows, tile_cols, tile_counts):
     tile_set = tiles[0, 0]
     dest_ids = tile_rows[0, 0]
@@ -106,13 +118,13 @@
     blocks_down = own_nodes * col_count // block
     blocks_across = own_nodes * row_count // block
     factor = 1.0 / math.sqrt(own_nodes * row_count * col_count)
-    panel = lax.all_gather(features, "row", axis=0, tiled=True)
+    panel = gather_all(features, "row", row_count)
     panel_blocks = panel.reshape(blocks_across, block, width)
     partial_value = accumulate(
         tile_set, dest_ids, source_ids, live_count, panel_blocks, blocks_down, False
     )
     term = partial_value.reshape(blocks_down * block, width)
-    summed = lax.psum_scatter(term.astype(jnp.bfloat16), "col", scatter_dimension=0, tiled=True)
+    summed = scatter_sum(term, "col", col_count)
     aggregated = summed.astype(jnp.bfloat16)
     preact = jnp.dot(aggregated, weight, preferred_element_type=jnp.float32) + bias
     hidden = jax.nn.silu(preact).astype(jnp.bfloat16)
@@ -122,14 +134,14 @@
     local_weight = jnp.einsum("nf,ng->fg", aggregated, grad_pre, preferred_element_type=jnp.float32)
     local_bias = jnp.sum(grad_pre.astype(jnp.float32), axis=0)
     grad_agg = jnp.dot(grad_pre, weight.T, preferred_element_type=jnp.float32).astype(jnp.bfloat16)
-    grad_panel = lax.all_gather(grad_agg, "col", axis=0, tiled=True)
+    grad_panel = gather_all(grad_agg, "col", col_count)
     grad_blocks = grad_panel.reshape(blocks_down, block, width)
     partial_back = accumulate(
         tile_set, dest_ids, source_ids, live_count, grad_blocks, blocks_across, True
     )
     term_back = partial_back.reshape(blocks_across * block, width)
-    grad_features = lax.psum_scatter(
-        term_back.astype(jnp.bfloat16), "row", scatter_dimension=0, tiled=True
+    grad_features = scatter_sum(term_back.astype(jnp.bfloat16), "row", row_count).astype(
+        jnp.bfloat16
     )
     packed = jnp.concatenate([local_weight, local_bias[None, :]], axis=0)
     packed = butterfly_sum(butterfly_sum(packed, "col"), "row")

time: 414 us -> 422 us (1.019)
  the two profiles are of different devices: /device:TPU:0 before, /device:TPU:2 now
where the time goes in v3:
time: 422 us; the launch traced here: 421 us
  Pallas kernels  149 us (35%)
  waiting for transfers between devices  126 us (30%)
  blocking collectives  95.4 us (23%)
  starting transfers between devices  29.8 us (7%)
  other arithmetic  11.6 us (3%)
  local copies, waits for them, and re-layouts  6.23 us (1%)
    pallas_call x2, Pallas kernels, accumulate(): pl.pallas_call(functools.partial(accumulate_kernel, backward), out_shape=...  149 us
    all_to_all x1, blocking collectives, scatter_sum(): got = lax.all_to_all(parts, axis, 0, 0, tiled=False)  95.4 us
    all_to_all x2, waiting for transfers between devices, gather_all(): got = lax.all_to_all(spread, axis, 0, 0, tiled=False)  81.5 us
    ppermute x7, waiting for transfers between devices, butterfly_sum(): value = value + lax.ppermute(value, axis, pairs)  44.7 us
    all_to_all x2, starting transfers between devices, gather_all(): got = lax.all_to_all(spread, axis, 0, 0, tiled=False)  15.3 us
    ppermute x7, starting transfers between devices, butterfly_sum(): value = value + lax.ppermute(value, axis, pairs)  10.8 us
  transfers between devices with their start and end apart: 10, of which 8 were waited for; matrix products, arithmetic and copies ran while one was open for 2% of the time, Pallas kernels for 20%

profile of v3, /device:TPU:2, one launch (start us, length us, event | category | flops | bytes accessed | tf_op | source)
XLA Modules:
  0.0 421.2 jit_solution(7407208267029965861)
XLA Ops:
  0.7 2.5 broadcast_in_dim.6
  3.1 7.8 %all-to-all-start = ((bf16[8,512,256]{2,1,0:T(8,128)(2,1)}), bf16[8,512,256]{2,1,0:T(8,128)(2,1)S(1)}, u32[]{:S(2)}, u32[]{:S(2)}) async-start(bf16[8,512,256]{2,1,0:T(8,128)(2,1)} %broadcast_in_dim.6), calls=%async_computation | async-start | bytes 4194304 | tf_op jit(solution)/shard_map/all_to_all | solution.py:98
  11.6 0.6 reduce.1.dest_ref
  12.2 0.6 reduce.2.source_ref
  12.8 26.6 %all-to-all-done = bf16[8,512,256]{2,1,0:T(8,128)(2,1)S(1)} async-done(((bf16[8,512,256]{2,1,0:T(8,128)(2,1)}), bf16[8,512,256]{2,1,0:T(8,128)(2,1)S(1)}, u32[]{:S(2)}, u32[]{:S(2)}) %all-to-all-start) | async-done | bytes 2097184 | tf_op jit(solution)/shard_map/all_to_all | solution.py:98
  39.4 1.4 copy-done.1
  40.7 66.5 %shard_map.111 = f32[64,128,256]{2,1,0:T(8,128)} custom-call(s32[384]{0:T(512)} %reduce.1.dest_ref, s32[384]{0:T(512)} %reduce.2.source_ref, s32[1]{0:T(128)} %bitcast.14.count_ref, bf16[384,128,128]{2,1,0:T(8,128)(2,1)} %bitcast.16, bf16[32,128,256]{2,1,0:T(8,128)(2,1)} %bitcast.19), custom_call_target="tpu_custom_call" | custom-call | flops 3221225472 | bytes 23068672 | tf_op jit(solution)/shard_map/pallas_call | solution.py:65
  107.2 95.4 %all_to_all.20 = f32[16,512,256]{2,1,0:T(8,128)} all-to-all(f32[16,512,256]{2,1,0:T(8,128)} %bitcast.18), channel_id=1, replica_groups=mesh['row'=8,'col'=16] {'col'}, dimensions={0} | all-to-all | bytes 16777216 | tf_op jit(solution)/shard_map/all_to_all | solution.py:104
  202.6 4.0 reduce_sum.30
  206.6 1.1 convert_reduce_fusion
  207.8 0.2 convolution_convert_fusion
  208.0 2.4 broadcast_in_dim.8
  210.4 7.5 %all-to-all-start.2 = ((bf16[16,512,256]{2,1,0:T(8,128)(2,1)}), bf16[16,512,256]{2,1,0:T(8,128)(2,1)}, u32[]{:S(2)}, u32[]{:S(2)}) async-start(bf16[16,512,256]{2,1,0:T(8,128)(2,1)} %broadcast_in_dim.8), calls=%async_computation.2 | async-start | bytes 8388608 | tf_op jit(solution)/shard_map/all_to_all | solution.py:98
  217.9 0.3 fusion.4
  218.5 1.4 collective-permute-done
  219.9 0.4 collective-permute-start.1
  220.3 54.9 %all-to-all-done.2 = bf16[16,512,256]{2,1,0:T(8,128)(2,1)} async-done(((bf16[16,512,256]{2,1,0:T(8,128)(2,1)}), bf16[16,512,256]{2,1,0:T(8,128)(2,1)}, u32[]{:S(2)}, u32[]{:S(2)}) %all-to-all-start.2) | async-done | bytes 4194336 | tf_op jit(solution)/shard_map/all_to_all | solution.py:98
  275.2 82.5 %shard_map.112 = f32[32,128,256]{2,1,0:T(8,128)} custom-call(s32[384]{0:T(512)} %reduce.1.dest_ref, s32[384]{0:T(512)} %reduce.2.source_ref, s32[1]{0:T(128)} %bitcast.15.count_ref, bf16[384,128,128]{2,1,0:T(8,128)(2,1)} %bitcast.17, bf16[64,128,256]{2,1,0:T(8,128)(2,1)} %bitcast.6.panel_ref), custom_call_target="tpu_custom_call" | custom-call | flops 3221225472 | bytes 20971520 | tf_op jit(solution)/shard_map/pallas_call | solution.py:65
  357.7 3.8 convert_element_type.33
  361.5 3.6 all-to-all-start.3
  365.3 8.0 %collective-permute-done.2 = f32[257,256]{1,0:T(8,128)S(1)} collective-permute-done((f32[257,256]{1,0:T(8,128)S(1)}, f32[257,256]{1,0:T(8,128)S(1)}, u32[]{:S(2)}, u32[]{:S(2)}) %collective-permute-start.2) | collective-permute-done | bytes 263200 | tf_op jit(solution)/shard_map/ppermute | solution.py:91
  373.3 0.7 collective-permute-start.3
  373.9 19.0 %collective-permute-done.3 = f32[257,256]{1,0:T(8,128)S(1)} collective-permute-done((f32[257,256]{1,0:T(8,128)S(1)}, f32[257,256]{1,0:T(8,128)S(1)}, u32[]{:S(2)}, u32[]{:S(2)}) %collective-permute-start.3) | collective-permute-done | bytes 263200 | tf_op jit(solution)/shard_map/ppermute | solution.py:91
  393.0 2.1 collective-permute-start.4
  395.1 5.9 %collective-permute-done.4 = f32[257,256]{1,0:T(8,128)S(1)} collective-permute-done((f32[257,256]{1,0:T(8,128)S(1)}, f32[257,256]{1,0:T(8,128)S(1)}, u32[]{:S(2)}, u32[]{:S(2)}) %collective-permute-start.4) | collective-permute-done | bytes 263200 | tf_op jit(solution)/shard_map/ppermute | solution.py:91
  401.0 3.2 collective-permute-start.5
  404.2 5.6 %collective-permute-done.5 = f32[257,256]{1,0:T(8,128)S(1)} collective-permute-done((f32[257,256]{1,0:T(8,128)S(1)}, f32[257,256]{1,0:T(8,128)S(1)}, u32[]{:S(2)}, u32[]{:S(2)}) %collective-permute-start.5) | collective-permute-done | bytes 263200 | tf_op jit(solution)/shard_map/ppermute | solution.py:91
  409.8 4.2 collective-permute-start.6
  414.0 4.9 %collective-permute-done.6 = f32[257,256]{1,0:T(8,128)S(1)} collective-permute-done((f32[257,256]{1,0:T(8,128)S(1)}, f32[257,256]{1,0:T(8,128)S(1)}, u32[]{:S(2)}, u32[]{:S(2)}) %collective-permute-start.6) | collective-permute-done | bytes 263200 | tf_op jit(solution)/shard_map/ppermute | solution.py:91
  418.9 0.6 slice_multiply_fusion.1
  419.5 0.7 slice_multiply_fusion
  420.2 1.0 reduce_sum.32
  (23 shorter events, 0.6 us)
Async XLA Ops:
  0.6 206.0 %copy-start = (bf16[256,256]{1,0:T(8,128)(2,1)S(1)}, bf16[256,256]{1,0:T(8,128)(2,1)}, u32[]{:S(2)}) copy-start(bf16[256,256]{1,0:T(8,128)(2,1)} %param.9) | copy-start | bytes 393220
  0.6 10.9 %copy-start.2 = (s32[1,1,384]{2,1,0:T(1,128)S(1)}, s32[1,1,384]{2,1,0:T(1,128)}, u32[]{:S(2)}) copy-start(s32[1,1,384]{2,1,0:T(1,128)} %param.13) | copy-start | bytes 4612
  0.7 11.5 %copy-start.3 = (s32[1,1,384]{2,1,0:T(1,128)S(1)}, s32[1,1,384]{2,1,0:T(1,128)}, u32[]{:S(2)}) copy-start(s32[1,1,384]{2,1,0:T(1,128)} %param.14) | copy-start | bytes 4612
  3.1 36.2 %all-to-all-start = ((bf16[8,512,256]{2,1,0:T(8,128)(2,1)}), bf16[8,512,256]{2,1,0:T(8,128)(2,1)S(1)}, u32[]{:S(2)}, u32[]{:S(2)}) async-start(bf16[8,512,256]{2,1,0:T(8,128)(2,1)} %broadcast_in_dim.6), calls=%async_computation | async-start | bytes 4194304 | tf_op jit(solution)/shard_map/all_to_all | solution.py:98
  39.3 1.4 copy-start.1
  202.6 4.0 copy-start.4
  202.6 4.0 copy-start.5
  210.4 64.8 %all-to-all-start.2 = ((bf16[16,512,256]{2,1,0:T(8,128)(2,1)}), bf16[16,512,256]{2,1,0:T(8,128)(2,1)}, u32[]{:S(2)}, u32[]{:S(2)}) async-start(bf16[16,512,256]{2,1,0:T(8,128)(2,1)} %broadcast_in_dim.8), calls=%async_computation.2 | async-start | bytes 8388608 | tf_op jit(solution)/shard_map/all_to_all | solution.py:98
  218.2 1.6 collective-permute-start
  219.9 145.2 %collective-permute-start.1 = (f32[257,256]{1,0:T(8,128)S(1)}, f32[257,256]{1,0:T(8,128)S(1)}, u32[]{:S(2)}, u32[]{:S(2)}) collective-permute-start(f32[257,256]{1,0:T(8,128)S(1)} %fusion.3), channel_id=1, source_target_pairs={{0,2},{1,3},{2,0},{3,1},{4,6},{5,7},{6,4},{7,5},{8,10},{9,11},{10,... | collective-permute-start | bytes 789512 | tf_op jit(solution)/shard_map/ppermute | solution.py:91
  361.5 58.7 %all-to-all-start.3 = ((bf16[8,512,256]{2,1,0:T(8,128)(2,1)}), bf16[8,512,256]{2,1,0:T(8,128)(2,1)S(1)}, u32[]{:S(2)}, u32[]{:S(2)}) async-start(bf16[8,512,256]{2,1,0:T(8,128)(2,1)} %bitcast.7), calls=%async_computation.3 | async-start | bytes 4194304 | tf_op jit(solution)/shard_map/all_to_all | solution.py:104
  365.2 8.0 %collective-permute-start.2 = (f32[257,256]{1,0:T(8,128)S(1)}, f32[257,256]{1,0:T(8,128)S(1)}, u32[]{:S(2)}, u32[]{:S(2)}) collective-permute-start(f32[257,256]{1,0:T(8,128)S(1)} %add.42), channel_id=1, source_target_pairs={{0,4},{1,5},{2,6},{3,7},{4,0},{5,1},{6,2},{7,3},{8,12},{9,13},{10,... | collective-permute-start | bytes 789512 | tf_op jit(solution)/shard_map/ppermute | solution.py:91
  373.3 19.7 %collective-permute-start.3 = (f32[257,256]{1,0:T(8,128)S(1)}, f32[257,256]{1,0:T(8,128)S(1)}, u32[]{:S(2)}, u32[]{:S(2)}) collective-permute-start(f32[257,256]{1,0:T(8,128)S(1)} %add.43), channel_id=1, source_target_pairs={{0,8},{1,9},{2,10},{3,11},{4,12},{5,13},{6,14},{7,15},{8,0},{9,1},... | collective-permute-start | bytes 789512 | tf_op jit(solution)/shard_map/ppermute | solution.py:91
  393.0 8.0 %collective-permute-start.4 = (f32[257,256]{1,0:T(8,128)S(1)}, f32[257,256]{1,0:T(8,128)S(1)}, u32[]{:S(2)}, u32[]{:S(2)}) collective-permute-start(f32[257,256]{1,0:T(8,128)S(1)} %add.44), channel_id=1, source_target_pairs={{0,16},{16,0},{32,48},{48,32},{64,80},{80,64},{96,112},{112,96},{1... | collective-permute-start | bytes 789512 | tf_op jit(solution)/shard_map/ppermute | solution.py:91
  401.0 8.8 %collective-permute-start.5 = (f32[257,256]{1,0:T(8,128)S(1)}, f32[257,256]{1,0:T(8,128)S(1)}, u32[]{:S(2)}, u32[]{:S(2)}) collective-permute-start(f32[257,256]{1,0:T(8,128)S(1)} %add.45), channel_id=1, source_target_pairs={{0,32},{16,48},{32,0},{48,16},{64,96},{80,112},{96,64},{112,80},{1... | collective-permute-start | bytes 789512 | tf_op jit(solution)/shard_map/ppermute | solution.py:91
  409.8 9.1 %collective-permute-start.6 = (f32[257,256]{1,0:T(8,128)S(1)}, f32[257,256]{1,0:T(8,128)S(1)}, u32[]{:S(2)}, u32[]{:S(2)}) collective-permute-start(f32[257,256]{1,0:T(8,128)S(1)} %add.46), channel_id=1, source_target_pairs={{0,64},{16,80},{32,96},{48,112},{64,0},{80,16},{96,32},{112,48},{1... | collective-permute-start | bytes 789512 | tf_op jit(solution)/shard_map/ppermute | solution.py:91

commit v4 on v3

--- a/solution.py
+++ b/solution.py
@@ -124,7 +124,7 @@
         tile_set, dest_ids, source_ids, live_count, panel_blocks, blocks_down, False
     )
     term = partial_value.reshape(blocks_down * block, width)
-    summed = scatter_sum(term, "col", col_count)
+    summed = scatter_sum(term.astype(jnp.bfloat16), "col", col_count)
     aggregated = summed.astype(jnp.bfloat16)
     preact = jnp.dot(aggregated, weight, preferred_element_type=jnp.float32) + bias
     hidden = jax.nn.silu(preact).astype(jnp.bfloat16)
@@ -134,7 +134,10 @@
     local_weight = jnp.einsum("nf,ng->fg", aggregated, grad_pre, preferred_element_type=jnp.float32)
     local_bias = jnp.sum(grad_pre.astype(jnp.float32), axis=0)
     grad_agg = jnp.dot(grad_pre, weight.T, preferred_element_type=jnp.float32).astype(jnp.bfloat16)
-    grad_panel = gather_all(grad_agg, "col", col_count)
+    packed = jnp.concatenate([local_weight, local_bias[None, :]], axis=0)
+    grad_panel = lax.all_gather(grad_agg, "col", axis=0, tiled=True)
+    packed = butterfly_sum(butterfly_sum(packed, "col"), "row")
+    grad_panel, packed = lax.optimization_barrier((grad_panel, packed))
     grad_blocks = grad_panel.reshape(blocks_down, block, width)
     partial_back = accumulate(
         tile_set, dest_ids, source_ids, live_count, grad_blocks, blocks_across, True
@@ -143,8 +146,6 @@
     grad_features = scatter_sum(term_back.astype(jnp.bfloat16), "row", row_count).astype(
         jnp.bfloat16
     )
-    packed = jnp.concatenate([local_weight, local_bias[None, :]], axis=0)
-    packed = butterfly_sum(butterfly_sum(packed, "col"), "row")
     grad_weight = packed[:width] * factor
     grad_bias = packed[width] * factor
     return (hidden, grad_weight, grad_bias, grad_features)

time: 422 us -> 361 us (0.86)
  the two profiles are of different devices: /device:TPU:2 before, /device:TPU:0 now
where the time goes in v4:
time: 361 us
  waiting for transfers between devices  101 us (28%)
  blocking collectives  88 us (24%)
  Pallas kernels  69.2 us (19%)
  starting transfers between devices  66.7 us (18%)
  between operations  14.8 us (4%)
  other arithmetic  14.4 us (4%)
  local copies, waits for them, and re-layouts  3.85 us (1%)
    all_to_all x1, blocking collectives, scatter_sum(): got = lax.all_to_all(parts, axis, 0, 0, tiled=False)  88 us
    pallas_call x2, Pallas kernels, accumulate(): pl.pallas_call(functools.partial(accumulate_kernel, backward), out_shape=...  69.2 us
    ppermute x7, waiting for transfers between devices, butterfly_sum(): value = value + lax.ppermute(value, axis, pairs)  57.4 us
    all_to_all x1, starting transfers between devices, scatter_sum(): got = lax.all_to_all(parts, axis, 0, 0, tiled=False)  51 us
    all_to_all x1, waiting for transfers between devices, gather_all(): got = lax.all_to_all(spread, axis, 0, 0, tiled=False)  26.6 us
    all_to_all x1, waiting for transfers between devices, scatter_sum(): got = lax.all_to_all(parts, axis, 0, 0, tiled=False)  17.3 us
    all_to_all x1, starting transfers between devices, gather_all(): got = lax.all_to_all(spread, axis, 0, 0, tiled=False)  7.87 us
    ppermute x7, starting transfers between devices, butterfly_sum(): value = value + lax.ppermute(value, axis, pairs)  7.76 us
  transfers between devices with their start and end apart: 10, of which 9 were waited for; matrix products, arithmetic and copies ran while one was open for 1% of the time, Pallas kernels for 0%

profile of v4, /device:TPU:0, one launch (start us, length us, event | category | flops | bytes accessed | tf_op | source)
XLA Modules:
  0.0 360.8 jit_solution(2809821798634820102)
XLA Ops:
  7.2 2.5 broadcast_in_dim.4
  9.7 7.9 %all-to-all-start = ((bf16[8,512,256]{2,1,0:T(8,128)(2,1)}), bf16[8,512,256]{2,1,0:T(8,128)(2,1)S(1)}, u32[]{:S(2)}, u32[]{:S(2)}) async-start(bf16[8,512,256]{2,1,0:T(8,128)(2,1)} %broadcast_in_dim.4), calls=%async_computation | async-start | bytes 4194304 | tf_op jit(solution)/shard_map/all_to_all | solution.py:98
  18.2 0.6 reduce.2.dest_ref
  18.8 0.6 reduce.3.source_ref
  19.4 26.6 %all-to-all-done = bf16[8,512,256]{2,1,0:T(8,128)(2,1)S(1)} async-done(((bf16[8,512,256]{2,1,0:T(8,128)(2,1)}), bf16[8,512,256]{2,1,0:T(8,128)(2,1)S(1)}, u32[]{:S(2)}, u32[]{:S(2)}) %all-to-all-start) | async-done | bytes 2097184 | tf_op jit(solution)/shard_map/all_to_all | solution.py:98
  46.0 1.4 copy-done.1
  47.3 31.9 %shard_map.111 = f32[64,128,256]{2,1,0:T(8,128)} custom-call(s32[384]{0:T(512)} %reduce.2.dest_ref, s32[384]{0:T(512)} %reduce.3.source_ref, s32[1]{0:T(128)} %bitcast.14.count_ref, bf16[384,128,128]{2,1,0:T(8,128)(2,1)} %bitcast.16, bf16[32,128,256]{2,1,0:T(8,128)(2,1)} %bitcast.19), custom_call_target="tpu_custom_call" | custom-call | flops 3221225472 | bytes 23068672 | tf_op jit(solution)/shard_map/pallas_call | solution.py:65
  79.3 4.0 %convert_element_type.33 = bf16[64,128,256]{2,1,0:T(8,128)(2,1)S(1)} convert(f32[64,128,256]{2,1,0:T(8,128)} %shard_map.111) | non-fusion elementwise | flops 2097152 | bytes 12582912 | tf_op jit(solution)/shard_map/convert_element_type | solution.py:127
  83.3 88.0 %all_to_all.15 = bf16[16,512,256]{2,1,0:T(8,128)(2,1)} all-to-all(bf16[16,512,256]{2,1,0:T(8,128)(2,1)S(1)} %bitcast.18), channel_id=1, replica_groups=mesh['row'=8,'col'=16] {'col'}, dimensions={0} | all-to-all | bytes 8388608 | tf_op jit(solution)/shard_map/all_to_all | solution.py:104
  171.3 2.9 reduce_sum.33
  174.2 1.1 convert_reduce_fusion
  175.3 1.0 convolution_convert_fusion
  176.3 0.3 fusion.1
  176.6 0.1 collective-permute-start
  176.7 1.5 collective-permute-done
  178.4 10.1 %collective-permute-done.1 = f32[257,256]{1,0:T(8,128)S(1)} collective-permute-done((f32[257,256]{1,0:T(8,128)S(1)}, f32[257,256]{1,0:T(8,128)S(1)}, u32[]{:S(2)}, u32[]{:S(2)}) %collective-permute-start.1) | collective-permute-done | bytes 263200 | tf_op jit(solution)/shard_map/ppermute | solution.py:91
  188.5 0.1 collective-permute-start.2
  188.6 15.5 %collective-permute-done.2 = f32[257,256]{1,0:T(8,128)S(1)} collective-permute-done((f32[257,256]{1,0:T(8,128)S(1)}, f32[257,256]{1,0:T(8,128)S(1)}, u32[]{:S(2)}, u32[]{:S(2)}) %collective-permute-start.2) | collective-permute-done | bytes 263200 | tf_op jit(solution)/shard_map/ppermute | solution.py:91
  204.1 0.1 collective-permute-start.3
  204.2 13.6 %collective-permute-done.3 = f32[257,256]{1,0:T(8,128)S(1)} collective-permute-done((f32[257,256]{1,0:T(8,128)S(1)}, f32[257,256]{1,0:T(8,128)S(1)}, u32[]{:S(2)}, u32[]{:S(2)}) %collective-permute-start.3) | collective-permute-done | bytes 263200 | tf_op jit(solution)/shard_map/ppermute | solution.py:91
  218.0 6.4 %collective-permute-done.4 = f32[257,256]{1,0:T(8,128)S(1)} collective-permute-done((f32[257,256]{1,0:T(8,128)S(1)}, f32[257,256]{1,0:T(8,128)S(1)}, u32[]{:S(2)}, u32[]{:S(2)}) %collective-permute-start.4) | collective-permute-done | bytes 263200 | tf_op jit(solution)/shard_map/ppermute | solution.py:91
  224.4 5.1 %collective-permute-start.5 = (f32[257,256]{1,0:T(8,128)S(1)}, f32[257,256]{1,0:T(8,128)S(1)}, u32[]{:S(2)}, u32[]{:S(2)}) collective-permute-start(f32[257,256]{1,0:T(8,128)S(1)} %add.45), channel_id=1, source_target_pairs={{0,32},{16,48},{32,0},{48,16},{64,96},{80,112},{96,64},{112,80},{1... | collective-permute-start | bytes 789512 | tf_op jit(solution)/shard_map/ppermute | solution.py:91
  229.6 4.4 %collective-permute-done.5 = f32[257,256]{1,0:T(8,128)S(1)} collective-permute-done((f32[257,256]{1,0:T(8,128)S(1)}, f32[257,256]{1,0:T(8,128)S(1)}, u32[]{:S(2)}, u32[]{:S(2)}) %collective-permute-start.5) | collective-permute-done | bytes 263200 | tf_op jit(solution)/shard_map/ppermute | solution.py:91
  234.0 2.2 collective-permute-start.6
  236.3 5.8 %collective-permute-done.6 = f32[257,256]{1,0:T(8,128)S(1)} collective-permute-done((f32[257,256]{1,0:T(8,128)S(1)}, f32[257,256]{1,0:T(8,128)S(1)}, u32[]{:S(2)}, u32[]{:S(2)}) %collective-permute-start.6) | collective-permute-done | bytes 263200 | tf_op jit(solution)/shard_map/ppermute | solution.py:91
  242.2 37.3 %shard_map.112 = f32[32,128,256]{2,1,0:T(8,128)} custom-call(s32[384]{0:T(512)} %reduce.2.dest_ref, s32[384]{0:T(512)} %reduce.3.source_ref, s32[1]{0:T(128)} %bitcast.15.count_ref, bf16[384,128,128]{2,1,0:T(8,128)(2,1)} %bitcast.17, bf16[64,128,256]{2,1,0:T(8,128)(2,1)} %bitcast.20), custom_call_target="tpu_custom_call" | custom-call | flops 3221225472 | bytes 20971520 | tf_op jit(solution)/shard_map/pallas_call | solution.py:65
  279.5 3.8 %convert_element_type.40 = bf16[32,128,256]{2,1,0:T(8,128)(2,1)} convert(f32[32,128,256]{2,1,0:T(8,128)} %shard_map.112) | non-fusion elementwise | flops 1048576 | bytes 6291456 | tf_op jit(solution)/shard_map/convert_element_type | solution.py:146
  283.3 51.0 %all-to-all-start.2 = ((bf16[8,512,256]{2,1,0:T(8,128)(2,1)}), bf16[8,512,256]{2,1,0:T(8,128)(2,1)S(1)}, u32[]{:S(2)}, u32[]{:S(2)}) async-start(bf16[8,512,256]{2,1,0:T(8,128)(2,1)} %bitcast.7), calls=%async_computation.2 | async-start | bytes 4194304 | tf_op jit(solution)/shard_map/all_to_all | solution.py:104
  334.3 0.6 slice_multiply_fusion.1
  334.8 0.7 slice_multiply_fusion
  335.6 17.3 %all-to-all-done.2 = bf16[8,512,256]{2,1,0:T(8,128)(2,1)S(1)} async-done(((bf16[8,512,256]{2,1,0:T(8,128)(2,1)}), bf16[8,512,256]{2,1,0:T(8,128)(2,1)S(1)}, u32[]{:S(2)}, u32[]{:S(2)}) %all-to-all-start.2) | async-done | bytes 2097184 | tf_op jit(solution)/shard_map/all_to_all | solution.py:104
  352.9 1.0 reduce_sum.35
  (24 shorter events, 0.5 us)
Async XLA Ops:
  7.2 167.0 %copy-start = (bf16[256,256]{1,0:T(8,128)(2,1)S(1)}, bf16[256,256]{1,0:T(8,128)(2,1)}, u32[]{:S(2)}) copy-start(bf16[256,256]{1,0:T(8,128)(2,1)} %param.9) | copy-start | bytes 393220
  7.2 11.1 %copy-start.2 = (s32[1,1,384]{2,1,0:T(1,128)S(1)}, s32[1,1,384]{2,1,0:T(1,128)}, u32[]{:S(2)}) copy-start(s32[1,1,384]{2,1,0:T(1,128)} %param.13) | copy-start | bytes 4612
  7.2 11.6 %copy-start.3 = (s32[1,1,384]{2,1,0:T(1,128)S(1)}, s32[1,1,384]{2,1,0:T(1,128)}, u32[]{:S(2)}) copy-start(s32[1,1,384]{2,1,0:T(1,128)} %param.14) | copy-start | bytes 4612
  9.7 36.3 %all-to-all-start = ((bf16[8,512,256]{2,1,0:T(8,128)(2,1)}), bf16[8,512,256]{2,1,0:T(8,128)(2,1)S(1)}, u32[]{:S(2)}, u32[]{:S(2)}) async-start(bf16[8,512,256]{2,1,0:T(8,128)(2,1)} %broadcast_in_dim.4), calls=%async_computation | async-start | bytes 4194304 | tf_op jit(solution)/shard_map/all_to_all | solution.py:98
  17.5 224.6 %all-gather.2.cloned.1.call-start = ((), (), s32[]{:S(2)}) async-start(), calls=%async_computation.3 | async-start | bytes 4456448 | tf_op jit(solution)/shard_map/all_gather | solution.py:138
  46.0 1.4 copy-start.1
  171.3 2.9 copy-start.4
  171.3 2.9 copy-start.5
  176.6 1.6 collective-permute-start
  178.3 10.2 %collective-permute-start.1 = (f32[257,256]{1,0:T(8,128)S(1)}, f32[257,256]{1,0:T(8,128)S(1)}, u32[]{:S(2)}, u32[]{:S(2)}) collective-permute-start(f32[257,256]{1,0:T(8,128)S(1)} %fusion), channel_id=1, source_target_pairs={{0,2},{1,3},{2,0},{3,1},{4,6},{5,7},{6,4},{7,5},{8,10},{9,11},{10,... | collective-permute-start | bytes 789512 | tf_op jit(solution)/shard_map/ppermute | solution.py:91
  188.5 15.6 %collective-permute-start.2 = (f32[257,256]{1,0:T(8,128)S(1)}, f32[257,256]{1,0:T(8,128)S(1)}, u32[]{:S(2)}, u32[]{:S(2)}) collective-permute-start(f32[257,256]{1,0:T(8,128)S(1)} %add.42), channel_id=1, source_target_pairs={{0,4},{1,5},{2,6},{3,7},{4,0},{5,1},{6,2},{7,3},{8,12},{9,13},{10,... | collective-permute-start | bytes 789512 | tf_op jit(solution)/shard_map/ppermute | solution.py:91
  204.1 13.7 %collective-permute-start.3 = (f32[257,256]{1,0:T(8,128)S(1)}, f32[257,256]{1,0:T(8,128)S(1)}, u32[]{:S(2)}, u32[]{:S(2)}) collective-permute-start(f32[257,256]{1,0:T(8,128)S(1)} %add.43), channel_id=1, source_target_pairs={{0,8},{1,9},{2,10},{3,11},{4,12},{5,13},{6,14},{7,15},{8,0},{9,1},... | collective-permute-start | bytes 789512 | tf_op jit(solution)/shard_map/ppermute | solution.py:91
  217.9 6.5 %collective-permute-start.4 = (f32[257,256]{1,0:T(8,128)S(1)}, f32[257,256]{1,0:T(8,128)S(1)}, u32[]{:S(2)}, u32[]{:S(2)}) collective-permute-start(f32[257,256]{1,0:T(8,128)S(1)} %add.44), channel_id=1, source_target_pairs={{0,16},{16,0},{32,48},{48,32},{64,80},{80,64},{96,112},{112,96},{1... | collective-permute-start | bytes 789512 | tf_op jit(solution)/shard_map/ppermute | solution.py:91
  224.4 9.6 %collective-permute-start.5 = (f32[257,256]{1,0:T(8,128)S(1)}, f32[257,256]{1,0:T(8,128)S(1)}, u32[]{:S(2)}, u32[]{:S(2)}) collective-permute-start(f32[257,256]{1,0:T(8,128)S(1)} %add.45), channel_id=1, source_target_pairs={{0,32},{16,48},{32,0},{48,16},{64,96},{80,112},{96,64},{112,80},{1... | collective-permute-start | bytes 789512 | tf_op jit(solution)/shard_map/ppermute | solution.py:91
  234.0 8.0 %collective-permute-start.6 = (f32[257,256]{1,0:T(8,128)S(1)}, f32[257,256]{1,0:T(8,128)S(1)}, u32[]{:S(2)}, u32[]{:S(2)}) collective-permute-start(f32[257,256]{1,0:T(8,128)S(1)} %add.46), channel_id=1, source_target_pairs={{0,64},{16,80},{32,96},{48,112},{64,0},{80,16},{96,32},{112,48},{1... | collective-permute-start | bytes 789512 | tf_op jit(solution)/shard_map/ppermute | solution.py:91
  283.3 69.6 %all-to-all-start.2 = ((bf16[8,512,256]{2,1,0:T(8,128)(2,1)}), bf16[8,512,256]{2,1,0:T(8,128)(2,1)S(1)}, u32[]{:S(2)}, u32[]{:S(2)}) async-start(bf16[8,512,256]{2,1,0:T(8,128)(2,1)} %bitcast.7), calls=%async_computation.2 | async-start | bytes 4194304 | tf_op jit(solution)/shard_map/all_to_all | solution.py:104
Sparse Core Ops, SparseCore 0:
  176.4 43.2 all-gather.1

commit v5 on v4

--- a/solution.py
+++ b/solution.py
@@ -9,6 +9,7 @@
 from jax.sharding import PartitionSpec as P
 
 GROUP = 32
+UNROLL = 32
 
 
 def accumulate_kernel(backward, dest_ref, source_ref, count_ref, tiles_ref, panel_ref, out_ref):
@@ -24,29 +25,36 @@
     base = step * group
     live_count = count_ref[0]
 
-    def one_tile(i, carry):
+    def one_tile(i, checked):
         slot = base + i
+        if backward:
+            fetch = jnp.clip(dest_ref[slot], 0, in_blocks - 1)
+            target = jnp.clip(source_ref[slot], 0, out_blocks - 1)
+            contrib = lax.dot_general(
+                tiles_ref[i], panel_ref[fetch], (((0,), (0,)), ((), ())),
+                preferred_element_type=jnp.float32,
+            )
+        else:
+            fetch = jnp.clip(source_ref[slot], 0, in_blocks - 1)
+            target = jnp.clip(dest_ref[slot], 0, out_blocks - 1)
+            contrib = jnp.dot(
+                tiles_ref[i], panel_ref[fetch], preferred_element_type=jnp.float32
+            )
+        if checked:
+            contrib = jnp.where(slot < live_count, contrib, 0.0)
+        out_ref[target] += contrib
 
-        @pl.when(slot < live_count)
-        def _():
-            if backward:
-                fetch = jnp.clip(dest_ref[slot], 0, in_blocks - 1)
-                target = jnp.clip(source_ref[slot], 0, out_blocks - 1)
-                contrib = lax.dot_general(
-                    tiles_ref[i], panel_ref[fetch], (((0,), (0,)), ((), ())),
-                    preferred_element_type=jnp.float32,
-                )
-            else:
-                fetch = jnp.clip(source_ref[slot], 0, in_blocks - 1)
-                target = jnp.clip(dest_ref[slot], 0, out_blocks - 1)
-                contrib = jnp.dot(
-                    tiles_ref[i], panel_ref[fetch], preferred_element_type=jnp.float32
-                )
-            out_ref[target] += contrib
+    @pl.when(base + group <= live_count)
+    def _():
+        @pl.loop(0, group, unroll=UNROLL)
+        def _(i):
+            one_tile(i, False)
 
-        return carry
-
-    lax.fori_loop(0, group, one_tile, 0)
+    @pl.when((base < live_count) & (base + group > live_count))
+    def _():
+        @pl.loop(0, group)
+        def _(i):
+            one_tile(i, True)
 
 
 def accumulate(tiles, dest_ids, source_ids, live_count, source_blocks, out_blocks, backward):

time: 361 us -> 252 us (0.70)
  Pallas kernels: 69.2 us -> 23.7 us
  starting transfers between devices: 66.7 us -> 34.3 us
  blocking collectives: 88 us -> 56.9 us
    pallas_call x2, Pallas kernels: 69.2 us -> 23.7 us  [accumulate(): pl.pallas_call(functools.partial(accumulate_kernel, backward), out_shape=...]
    all_to_all x1, starting transfers between devices: 51 us -> 10.8 us  [scatter_sum(): got = lax.all_to_all(parts, axis, 0, 0, tiled=False)]
    all_to_all x1, blocking collectives: 88 us -> 56.9 us  [scatter_sum(): got = lax.all_to_all(parts, axis, 0, 0, tiled=False)]
    ppermute x7, starting transfers between devices: 7.76 us -> 15.6 us  [butterfly_sum(): value = value + lax.ppermute(value, axis, pairs)]
    ppermute x7, waiting for transfers between devices: 57.4 us -> 52 us  [butterfly_sum(): value = value + lax.ppermute(value, axis, pairs)]
    all_to_all x1, waiting for transfers between devices: 17.3 us -> 22.2 us  [scatter_sum(): got = lax.all_to_all(parts, axis, 0, 0, tiled=False)]
where the time goes in v5:
time: 252 us; the launch traced here: 251 us
  waiting for transfers between devices  101 us (40%)
  blocking collectives  56.9 us (23%)
  starting transfers between devices  34.3 us (14%)
  Pallas kernels  23.7 us (9%)
  between operations  14.8 us (6%)
  other arithmetic  14.4 us (6%)
  local copies, waits for them, and re-layouts  3.85 us (2%)
    all_to_all x1, blocking collectives, scatter_sum(): got = lax.all_to_all(parts, axis, 0, 0, tiled=False)  56.9 us
    ppermute x7, waiting for transfers between devices, butterfly_sum(): value = value + lax.ppermute(value, axis, pairs)  52 us
    all_to_all x1, waiting for transfers between devices, gather_all(): got = lax.all_to_all(spread, axis, 0, 0, tiled=False)  26.6 us
    pallas_call x2, Pallas kernels, accumulate(): pl.pallas_call(functools.partial(accumulate_kernel, backward), out_shape=...  23.7 us
    all_to_all x1, waiting for transfers between devices, scatter_sum(): got = lax.all_to_all(parts, axis, 0, 0, tiled=False)  22.2 us
    ppermute x7, starting transfers between devices, butterfly_sum(): value = value + lax.ppermute(value, axis, pairs)  15.6 us
    all_to_all x1, starting transfers between devices, scatter_sum(): got = lax.all_to_all(parts, axis, 0, 0, tiled=False)  10.8 us
    all_to_all x1, starting transfers between devices, gather_all(): got = lax.all_to_all(spread, axis, 0, 0, tiled=False)  7.87 us
  transfers between devices with their start and end apart: 10, of which 9 were waited for; matrix products, arithmetic and copies ran while one was open for 1% of the time, Pallas kernels for 0%

profile of v5, /device:TPU:0, one launch (start us, length us, event | category | flops | bytes accessed | tf_op | source)
XLA Modules:
  0.0 251.2 jit_solution(266941934234421946)
XLA Ops:
  7.2 2.5 broadcast_in_dim.4
  9.7 7.9 %all-to-all-start = ((bf16[8,512,256]{2,1,0:T(8,128)(2,1)}), bf16[8,512,256]{2,1,0:T(8,128)(2,1)S(1)}, u32[]{:S(2)}, u32[]{:S(2)}) async-start(bf16[8,512,256]{2,1,0:T(8,128)(2,1)} %broadcast_in_dim.4), calls=%async_computation | async-start | bytes 4194304 | tf_op jit(solution)/shard_map/all_to_all | solution.py:106
  18.2 0.6 reduce.2.dest_ref
  18.8 0.6 reduce.3.source_ref
  19.4 26.6 %all-to-all-done = bf16[8,512,256]{2,1,0:T(8,128)(2,1)S(1)} async-done(((bf16[8,512,256]{2,1,0:T(8,128)(2,1)}), bf16[8,512,256]{2,1,0:T(8,128)(2,1)S(1)}, u32[]{:S(2)}, u32[]{:S(2)}) %all-to-all-start) | async-done | bytes 2097184 | tf_op jit(solution)/shard_map/all_to_all | solution.py:106
  46.0 1.4 copy-done.1
  47.3 12.2 %shard_map.111 = f32[64,128,256]{2,1,0:T(8,128)} custom-call(s32[384]{0:T(512)} %reduce.2.dest_ref, s32[384]{0:T(512)} %reduce.3.source_ref, s32[1]{0:T(128)} %bitcast.14.count_ref, bf16[384,128,128]{2,1,0:T(8,128)(2,1)} %bitcast.16, bf16[32,128,256]{2,1,0:T(8,128)(2,1)} %bitcast.19), custom_call_target="tpu_custom_call" | custom-call | flops 3221225472 | bytes 23068672 | tf_op jit(solution)/shard_map/pallas_call | solution.py:73
  59.6 4.0 %convert_element_type.33 = bf16[64,128,256]{2,1,0:T(8,128)(2,1)S(1)} convert(f32[64,128,256]{2,1,0:T(8,128)} %shard_map.111) | non-fusion elementwise | flops 2097152 | bytes 12582912 | tf_op jit(solution)/shard_map/convert_element_type | solution.py:135
  63.6 56.9 %all_to_all.15 = bf16[16,512,256]{2,1,0:T(8,128)(2,1)} all-to-all(bf16[16,512,256]{2,1,0:T(8,128)(2,1)S(1)} %bitcast.18), channel_id=1, replica_groups=mesh['row'=8,'col'=16] {'col'}, dimensions={0} | all-to-all | bytes 8388608 | tf_op jit(solution)/shard_map/all_to_all | solution.py:112
  120.5 2.9 %reduce_sum.33 = bf16[512,256]{1,0:T(8,128)(2,1)S(1)} reduce(bf16[16,512,256]{2,1,0:T(8,128)(2,1)} %all_to_all.15, bf16[]{:T(256)} %constant.4.clone.1), dimensions={0}, to_apply=%region_0.0 | reduce | flops 1966080 | bytes 4456450 | tf_op jit(solution)/shard_map/reduce_sum | solution.py:113
  123.4 1.1 convert_reduce_fusion
  124.6 1.0 convolution_convert_fusion
  125.5 0.3 fusion.1
  125.9 1.5 collective-permute-done
  127.6 8.5 %collective-permute-done.1 = f32[257,256]{1,0:T(8,128)S(1)} collective-permute-done((f32[257,256]{1,0:T(8,128)S(1)}, f32[257,256]{1,0:T(8,128)S(1)}, u32[]{:S(2)}, u32[]{:S(2)}) %collective-permute-start.1) | collective-permute-done | bytes 263200 | tf_op jit(solution)/shard_map/ppermute | solution.py:99
  136.2 0.6 collective-permute-start.2
  136.8 14.6 %collective-permute-done.2 = f32[257,256]{1,0:T(8,128)S(1)} collective-permute-done((f32[257,256]{1,0:T(8,128)S(1)}, f32[257,256]{1,0:T(8,128)S(1)}, u32[]{:S(2)}, u32[]{:S(2)}) %collective-permute-start.2) | collective-permute-done | bytes 263200 | tf_op jit(solution)/shard_map/ppermute | solution.py:99
  151.4 0.3 collective-permute-start.3
  151.7 13.1 %collective-permute-done.3 = f32[257,256]{1,0:T(8,128)S(1)} collective-permute-done((f32[257,256]{1,0:T(8,128)S(1)}, f32[257,256]{1,0:T(8,128)S(1)}, u32[]{:S(2)}, u32[]{:S(2)}) %collective-permute-start.3) | collective-permute-done | bytes 263200 | tf_op jit(solution)/shard_map/ppermute | solution.py:99
  164.8 4.8 %collective-permute-start.4 = (f32[257,256]{1,0:T(8,128)S(1)}, f32[257,256]{1,0:T(8,128)S(1)}, u32[]{:S(2)}, u32[]{:S(2)}) collective-permute-start(f32[257,256]{1,0:T(8,128)S(1)} %add.44), channel_id=1, source_target_pairs={{0,16},{16,0},{32,48},{48,32},{64,80},{80,64},{96,112},{112,96},{1... | collective-permute-start | bytes 789512 | tf_op jit(solution)/shard_map/ppermute | solution.py:99
  169.6 4.4 %collective-permute-done.4 = f32[257,256]{1,0:T(8,128)S(1)} collective-permute-done((f32[257,256]{1,0:T(8,128)S(1)}, f32[257,256]{1,0:T(8,128)S(1)}, u32[]{:S(2)}, u32[]{:S(2)}) %collective-permute-start.4) | collective-permute-done | bytes 263200 | tf_op jit(solution)/shard_map/ppermute | solution.py:99
  174.1 2.6 %collective-permute-start.5 = (f32[257,256]{1,0:T(8,128)S(1)}, f32[257,256]{1,0:T(8,128)S(1)}, u32[]{:S(2)}, u32[]{:S(2)}) collective-permute-start(f32[257,256]{1,0:T(8,128)S(1)} %add.45), channel_id=1, source_target_pairs={{0,32},{16,48},{32,0},{48,16},{64,96},{80,112},{96,64},{112,80},{1... | collective-permute-start | bytes 789512 | tf_op jit(solution)/shard_map/ppermute | solution.py:99
  176.7 5.4 %collective-permute-done.5 = f32[257,256]{1,0:T(8,128)S(1)} collective-permute-done((f32[257,256]{1,0:T(8,128)S(1)}, f32[257,256]{1,0:T(8,128)S(1)}, u32[]{:S(2)}, u32[]{:S(2)}) %collective-permute-start.5) | collective-permute-done | bytes 263200 | tf_op jit(solution)/shard_map/ppermute | solution.py:99
  182.2 7.2 %collective-permute-start.6 = (f32[257,256]{1,0:T(8,128)S(1)}, f32[257,256]{1,0:T(8,128)S(1)}, u32[]{:S(2)}, u32[]{:S(2)}) collective-permute-start(f32[257,256]{1,0:T(8,128)S(1)} %add.46), channel_id=1, source_target_pairs={{0,64},{16,80},{32,96},{48,112},{64,0},{80,16},{96,32},{112,48},{1... | collective-permute-start | bytes 789512 | tf_op jit(solution)/shard_map/ppermute | solution.py:99
  189.4 4.4 %collective-permute-done.6 = f32[257,256]{1,0:T(8,128)S(1)} collective-permute-done((f32[257,256]{1,0:T(8,128)S(1)}, f32[257,256]{1,0:T(8,128)S(1)}, u32[]{:S(2)}, u32[]{:S(2)}) %collective-permute-start.6) | collective-permute-done | bytes 263200 | tf_op jit(solution)/shard_map/ppermute | solution.py:99
  193.9 11.4 %shard_map.112 = f32[32,128,256]{2,1,0:T(8,128)} custom-call(s32[384]{0:T(512)} %reduce.2.dest_ref, s32[384]{0:T(512)} %reduce.3.source_ref, s32[1]{0:T(128)} %bitcast.15.count_ref, bf16[384,128,128]{2,1,0:T(8,128)(2,1)} %bitcast.17, bf16[64,128,256]{2,1,0:T(8,128)(2,1)} %bitcast.20), custom_call_target="tpu_custom_call" | custom-call | flops 3221225472 | bytes 20971520 | tf_op jit(solution)/shard_map/pallas_call | solution.py:73
  205.3 3.8 %convert_element_type.40 = bf16[32,128,256]{2,1,0:T(8,128)(2,1)} convert(f32[32,128,256]{2,1,0:T(8,128)} %shard_map.112) | non-fusion elementwise | flops 1048576 | bytes 6291456 | tf_op jit(solution)/shard_map/convert_element_type | solution.py:154
  209.1 10.8 %all-to-all-start.2 = ((bf16[8,512,256]{2,1,0:T(8,128)(2,1)}), bf16[8,512,256]{2,1,0:T(8,128)(2,1)S(1)}, u32[]{:S(2)}, u32[]{:S(2)}) async-start(bf16[8,512,256]{2,1,0:T(8,128)(2,1)} %bitcast.7), calls=%async_computation.2 | async-start | bytes 4194304 | tf_op jit(solution)/shard_map/all_to_all | solution.py:112
  219.9 0.6 slice_multiply_fusion.1
  220.4 0.7 slice_multiply_fusion
  221.2 22.2 %all-to-all-done.2 = bf16[8,512,256]{2,1,0:T(8,128)(2,1)S(1)} async-done(((bf16[8,512,256]{2,1,0:T(8,128)(2,1)}), bf16[8,512,256]{2,1,0:T(8,128)(2,1)S(1)}, u32[]{:S(2)}, u32[]{:S(2)}) %all-to-all-start.2) | async-done | bytes 2097184 | tf_op jit(solution)/shard_map/all_to_all | solution.py:112
  243.3 1.0 reduce_sum.35
  (24 shorter events, 0.5 us)
Async XLA Ops:
  7.2 116.2 %copy-start = (bf16[256,256]{1,0:T(8,128)(2,1)S(1)}, bf16[256,256]{1,0:T(8,128)(2,1)}, u32[]{:S(2)}) copy-start(bf16[256,256]{1,0:T(8,128)(2,1)} %param.9) | copy-start | bytes 393220
  7.2 11.1 %copy-start.2 = (s32[1,1,384]{2,1,0:T(1,128)S(1)}, s32[1,1,384]{2,1,0:T(1,128)}, u32[]{:S(2)}) copy-start(s32[1,1,384]{2,1,0:T(1,128)} %param.13) | copy-start | bytes 4612
  7.2 11.6 %copy-start.3 = (s32[1,1,384]{2,1,0:T(1,128)S(1)}, s32[1,1,384]{2,1,0:T(1,128)}, u32[]{:S(2)}) copy-start(s32[1,1,384]{2,1,0:T(1,128)} %param.14) | copy-start | bytes 4612
  9.7 36.3 %all-to-all-start = ((bf16[8,512,256]{2,1,0:T(8,128)(2,1)}), bf16[8,512,256]{2,1,0:T(8,128)(2,1)S(1)}, u32[]{:S(2)}, u32[]{:S(2)}) async-start(bf16[8,512,256]{2,1,0:T(8,128)(2,1)} %broadcast_in_dim.4), calls=%async_computation | async-start | bytes 4194304 | tf_op jit(solution)/shard_map/all_to_all | solution.py:106
  17.5 176.3 %all-gather.2.cloned.1.call-start = ((), (), s32[]{:S(2)}) async-start(), calls=%async_computation.3 | async-start | bytes 4456448 | tf_op jit(solution)/shard_map/all_gather | solution.py:146
  46.0 1.4 copy-start.1
  120.5 2.9 %copy-start.4 = (bf16[512,256]{1,0:T(8,128)(2,1)S(1)}, bf16[512,256]{1,0:T(8,128)(2,1)}, u32[]{:S(2)}) copy-start(bf16[512,256]{1,0:T(8,128)(2,1)} %param.11) | copy-start | bytes 786436
  120.5 2.9 %copy-start.5 = (f32[256]{0:T(256)S(1)}, f32[256]{0:T(256)}, u32[]{:S(2)}) copy-start(f32[256]{0:T(256)} %param.10) | copy-start | bytes 3076
  125.9 1.6 collective-permute-start
  127.5 8.6 %collective-permute-start.1 = (f32[257,256]{1,0:T(8,128)S(1)}, f32[257,256]{1,0:T(8,128)S(1)}, u32[]{:S(2)}, u32[]{:S(2)}) collective-permute-start(f32[257,256]{1,0:T(8,128)S(1)} %fusion), channel_id=1, source_target_pairs={{0,2},{1,3},{2,0},{3,1},{4,6},{5,7},{6,4},{7,5},{8,10},{9,11},{10,... | collective-permute-start | bytes 789512 | tf_op jit(solution)/shard_map/ppermute | solution.py:99
  136.2 15.2 %collective-permute-start.2 = (f32[257,256]{1,0:T(8,128)S(1)}, f32[257,256]{1,0:T(8,128)S(1)}, u32[]{:S(2)}, u32[]{:S(2)}) collective-permute-start(f32[257,256]{1,0:T(8,128)S(1)} %add.42), channel_id=1, source_target_pairs={{0,4},{1,5},{2,6},{3,7},{4,0},{5,1},{6,2},{7,3},{8,12},{9,13},{10,... | collective-permute-start | bytes 789512 | tf_op jit(solution)/shard_map/ppermute | solution.py:99
  151.4 13.4 %collective-permute-start.3 = (f32[257,256]{1,0:T(8,128)S(1)}, f32[257,256]{1,0:T(8,128)S(1)}, u32[]{:S(2)}, u32[]{:S(2)}) collective-permute-start(f32[257,256]{1,0:T(8,128)S(1)} %add.43), channel_id=1, source_target_pairs={{0,8},{1,9},{2,10},{3,11},{4,12},{5,13},{6,14},{7,15},{8,0},{9,1},... | collective-permute-start | bytes 789512 | tf_op jit(solution)/shard_map/ppermute | solution.py:99
  164.8 9.2 %collective-permute-start.4 = (f32[257,256]{1,0:T(8,128)S(1)}, f32[257,256]{1,0:T(8,128)S(1)}, u32[]{:S(2)}, u32[]{:S(2)}) collective-permute-start(f32[257,256]{1,0:T(8,128)S(1)} %add.44), channel_id=1, source_target_pairs={{0,16},{16,0},{32,48},{48,32},{64,80},{80,64},{96,112},{112,96},{1... | collective-permute-start | bytes 789512 | tf_op jit(solution)/shard_map/ppermute | solution.py:99
  174.1 8.0 %collective-permute-start.5 = (f32[257,256]{1,0:T(8,128)S(1)}, f32[257,256]{1,0:T(8,128)S(1)}, u32[]{:S(2)}, u32[]{:S(2)}) collective-permute-start(f32[257,256]{1,0:T(8,128)S(1)} %add.45), channel_id=1, source_target_pairs={{0,32},{16,48},{32,0},{48,16},{64,96},{80,112},{96,64},{112,80},{1... | collective-permute-start | bytes 789512 | tf_op jit(solution)/shard_map/ppermute | solution.py:99
  182.2 11.6 %collective-permute-start.6 = (f32[257,256]{1,0:T(8,128)S(1)}, f32[257,256]{1,0:T(8,128)S(1)}, u32[]{:S(2)}, u32[]{:S(2)}) collective-permute-start(f32[257,256]{1,0:T(8,128)S(1)} %add.46), channel_id=1, source_target_pairs={{0,64},{16,80},{32,96},{48,112},{64,0},{80,16},{96,32},{112,48},{1... | collective-permute-start | bytes 789512 | tf_op jit(solution)/shard_map/ppermute | solution.py:99
  209.1 34.2 %all-to-all-start.2 = ((bf16[8,512,256]{2,1,0:T(8,128)(2,1)}), bf16[8,512,256]{2,1,0:T(8,128)(2,1)S(1)}, u32[]{:S(2)}, u32[]{:S(2)}) async-start(bf16[8,512,256]{2,1,0:T(8,128)(2,1)} %bitcast.7), calls=%async_computation.2 | async-start | bytes 4194304 | tf_op jit(solution)/shard_map/all_to_all | solution.py:112
Sparse Core Ops, SparseCore 0:
  125.7 45.7 all-gather.1

commit v6 on v5

--- a/solution.py
+++ b/solution.py
@@ -101,15 +101,64 @@
     return value
 
 
-def gather_all(value, axis, size):
-    spread = jnp.broadcast_to(value[None], (size,) + value.shape)
-    got = lax.all_to_all(spread, axis, 0, 0, tiled=False)
+def exchange_kernel(axis, size, spread, parts_ref, out_ref, local_sem, send_sems, recv_sems):
+    me = lax.axis_index(axis)
+    barrier = pltpu.get_barrier_semaphore()
+    for shift in range(1, size):
+        pl.semaphore_signal(
+            barrier, 1, device_id={axis: lax.rem(me + shift, size)},
+            device_id_type=pl.DeviceIdType.MESH,
+        )
+    pl.semaphore_wait(barrier, size - 1)
+    copies = []
+    for shift in range(1, size):
+        peer = lax.rem(me + shift, size)
+        copy = pltpu.make_async_remote_copy(
+            src_ref=parts_ref if spread else parts_ref.at[peer],
+            dst_ref=out_ref.at[me],
+            send_sem=send_sems.at[shift],
+            recv_sem=recv_sems.at[shift],
+            device_id={axis: peer},
+            device_id_type=pl.DeviceIdType.MESH,
+        )
+        copy.start()
+        copies.append(copy)
+    local = pltpu.make_async_copy(
+        parts_ref if spread else parts_ref.at[me], out_ref.at[me], local_sem
+    )
+    local.start()
+    local.wait()
+    for copy in copies:
+        copy.wait_send()
+        copy.wait_recv()
+
+
+def exchange(parts, axis, size, spread, tag):
+    shape = (size,) + parts.shape[1 - spread:]
+    nbytes = math.prod(shape) * parts.dtype.itemsize
+    return pl.pallas_call(
+        functools.partial(exchange_kernel, axis, size, spread),
+        out_shape=jax.ShapeDtypeStruct(shape, parts.dtype),
+        in_specs=[pl.BlockSpec(memory_space=pl.ANY)],
+        out_specs=pl.BlockSpec(memory_space=pl.ANY),
+        scratch_shapes=[
+            pltpu.SemaphoreType.DMA,
+            pltpu.SemaphoreType.DMA((size,)),
+            pltpu.SemaphoreType.DMA((size,)),
+        ],
+        compiler_params=pltpu.CompilerParams(collective_id=tag, has_side_effects=True),
+        cost_estimate=pl.CostEstimate(flops=0, transcendentals=0, bytes_accessed=2 * nbytes),
+    )(parts)
+
+
+def gather_all(value, axis, size, tag):
+    got = exchange(value, axis, size, True, tag)
     return got.reshape((size * value.shape[0],) + value.shape[1:])
 
 
-def scatter_sum(value, axis, size):
+def scatter_sum(value, axis, size, tag):
     parts = value.reshape((size, value.shape[0] // size) + value.shape[1:])
-    got = lax.all_to_all(parts, axis, 0, 0, tiled=False)
+    got = exchange(parts, axis, size, False, tag)
     return jnp.sum(got.astype(jnp.float32), axis=0)
 
 
@@ -126,13 +175,13 @@
     blocks_down = own_nodes * col_count // block
     blocks_across = own_nodes * row_count // block
     factor = 1.0 / math.sqrt(own_nodes * row_count * col_count)
-    panel = gather_all(features, "row", row_count)
+    panel = gather_all(features, "row", row_count, 0)
     panel_blocks = panel.reshape(blocks_across, block, width)
     partial_value = accumulate(
         tile_set, dest_ids, source_ids, live_count, panel_blocks, blocks_down, False
     )
     term = partial_value.reshape(blocks_down * block, width)
-    summed = scatter_sum(term.astype(jnp.bfloat16), "col", col_count)
+    summed = scatter_sum(term.astype(jnp.bfloat16), "col", col_count, 1)
     aggregated = summed.astype(jnp.bfloat16)
     preact = jnp.dot(aggregated, weight, preferred_element_type=jnp.float32) + bias
     hidden = jax.nn.silu(preact).astype(jnp.bfloat16)
@@ -151,7 +200,7 @@
         tile_set, dest_ids, source_ids, live_count, grad_blocks, blocks_across, True
     )
     term_back = partial_back.reshape(blocks_across * block, width)
-    grad_features = scatter_sum(term_back.astype(jnp.bfloat16), "row", row_count).astype(
+    grad_features = scatter_sum(term_back.astype(jnp.bfloat16), "row", row_count, 2).astype(
         jnp.bfloat16
     )
     grad_weight = packed[:width] * factor

time: 252 us -> 269 us (1.067)
  Pallas kernels: 23.7 us -> 162 us
  blocking collectives: 56.9 us -> 0 us
  waiting for transfers between devices: 101 us -> 56.7 us
  starting transfers between devices: 34.3 us -> 12.9 us
  other arithmetic: 14.4 us -> 19.5 us
  local copies, waits for them, and re-layouts: 3.85 us -> 0.02 us
    pallas_call x0 -> x3, Pallas kernels: none -> 138 us  [exchange(): pl.pallas_call(functools.partial(exchange_kernel, axis, size, spread), ou...]
    all_to_all x1 -> x0, blocking collectives: 56.9 us -> none  [scatter_sum(): got = lax.all_to_all(parts, axis, 0, 0, tiled=False)]
    all_to_all x2 -> x0, waiting for transfers between devices: 48.7 us -> none  [the longest x1 26.6 us: gather_all(): got = lax.all_to_all(spread, axis, 0, 0, tiled=False)]
    all_to_all x2 -> x0, starting transfers between devices: 18.6 us -> none  [the longest x1 10.8 us: scatter_sum(): got = lax.all_to_all(parts, axis, 0, 0, tiled=False)]
    ppermute x7, waiting for transfers between devices: 52 us -> 56.7 us  [butterfly_sum(): value = value + lax.ppermute(value, axis, pairs)]
    ppermute x7, starting transfers between devices: 15.6 us -> 12.9 us  [butterfly_sum(): value = value + lax.ppermute(value, axis, pairs)]
  transfers between devices with their start and end apart: 10 -> 8, of which waited for: 9 -> 7; matrix products, arithmetic and copies ran while one was open for 1% -> 0% of each run, Pallas kernels for 0% -> 0%
where the time goes in v6:
time: 269 us; the launch traced here: 268 us
  Pallas kernels  162 us (60%)
  waiting for transfers between devices  56.7 us (21%)
  other arithmetic  19.5 us (7%)
  between operations  14.8 us (6%)
  starting transfers between devices  12.9 us (5%)
    pallas_call x3, Pallas kernels, exchange(): pl.pallas_call(functools.partial(exchange_kernel, axis, size, spread), ou...  138 us
    ppermute x7, waiting for transfers between devices, butterfly_sum(): value = value + lax.ppermute(value, axis, pairs)  56.7 us
    pallas_call x2, Pallas kernels, accumulate(): pl.pallas_call(functools.partial(accumulate_kernel, backward), out_shape=...  24.2 us
    ppermute x7, starting transfers between devices, butterfly_sum(): value = value + lax.ppermute(value, axis, pairs)  12.9 us
    convert_element_type x1, other arithmetic, per_device(): summed = scatter_sum(term.astype(jnp.bfloat16), 'col', col_count, 1)  5.97 us
    reduce_sum x2, other arithmetic, scatter_sum(): return jnp.sum(got.astype(jnp.float32), axis=0)  5.54 us
  transfers between devices with their start and end apart: 8, of which 7 were waited for; matrix products, arithmetic and copies ran while one was open for 0% of the time, Pallas kernels for 0%

profile of v6, /device:TPU:0, one launch (start us, length us, event | category | flops | bytes accessed | tf_op | source)
XLA Modules:
  0.0 268.0 jit_solution(7353205826811526043)
XLA Ops:
  7.2 0.0 all-gather.2.cloned.1.call-start
  7.9 1.3 reduce.2.dest_ref
  9.2 1.3 reduce.3.source_ref
  10.5 37.1 %shard_map.111 = bf16[8,512,256]{2,1,0:T(8,128)(2,1)} custom-call(bf16[512,256]{1,0:T(8,128)(2,1)} %parts_ref.1), custom_call_target="tpu_custom_call" | custom-call | bytes 4194304 | tf_op jit(solution)/shard_map/pallas_call | solution.py:139
  47.6 11.8 %shard_map.112 = f32[64,128,256]{2,1,0:T(8,128)} custom-call(s32[384]{0:T(512)} %reduce.2.dest_ref, s32[384]{0:T(512)} %reduce.3.source_ref, s32[1]{0:T(128)} %bitcast.14.count_ref, bf16[384,128,128]{2,1,0:T(8,128)(2,1)} %bitcast.16, bf16[32,128,256]{2,1,0:T(8,128)(2,1)} %bitcast.20), custom_call_target="tpu_custom_call" | custom-call | flops 3221225472 | bytes 23068672 | tf_op jit(solution)/shard_map/pallas_call | solution.py:73
  59.4 6.0 %convert_element_type.33 = bf16[64,128,256]{2,1,0:T(8,128)(2,1)} convert(f32[64,128,256]{2,1,0:T(8,128)} %shard_map.112) | non-fusion elementwise | flops 2097152 | bytes 12582912 | tf_op jit(solution)/shard_map/convert_element_type | solution.py:184
  65.4 70.8 %shard_map.113 = bf16[16,512,256]{2,1,0:T(8,128)(2,1)} custom-call(bf16[16,512,256]{2,1,0:T(8,128)(2,1)} %bitcast.18), custom_call_target="tpu_custom_call" | custom-call | bytes 8388608 | tf_op jit(solution)/shard_map/pallas_call | solution.py:139
  136.2 2.9 %reduce_sum.33 = bf16[512,256]{1,0:T(8,128)(2,1)S(1)} reduce(bf16[16,512,256]{2,1,0:T(8,128)(2,1)} %shard_map.113, bf16[]{:T(256)} %constant.4.clone.1), dimensions={0}, to_apply=%region_0.0 | reduce | flops 1966080 | bytes 4456450 | tf_op jit(solution)/shard_map/reduce_sum | solution.py:162
  139.2 1.1 convert_reduce_fusion
  140.3 1.0 convolution_convert_fusion
  141.3 0.3 fusion.1
  141.6 5.1 %collective-permute-start = (f32[257,256]{1,0:T(8,128)S(1)}, f32[257,256]{1,0:T(8,128)S(1)}, u32[]{:S(2)}, u32[]{:S(2)}) collective-permute-start(f32[257,256]{1,0:T(8,128)S(1)} %pad_maximum_fusion), channel_id=1, source_target_pairs={{0,1},{1,0},{2,3},{3,2},{4,5},{5,4},{6,7},{7,6},{8,9},{9,8},{10,11... | collective-permute-start | bytes 789512 | tf_op jit(solution)/shard_map/ppermute | solution.py:99
  146.6 1.2 collective-permute-done
  147.8 0.1 fusion
  147.8 0.1 collective-permute-start.1
  147.9 11.0 %collective-permute-done.1 = f32[257,256]{1,0:T(8,128)S(1)} collective-permute-done((f32[257,256]{1,0:T(8,128)S(1)}, f32[257,256]{1,0:T(8,128)S(1)}, u32[]{:S(2)}, u32[]{:S(2)}) %collective-permute-start.1) | collective-permute-done | bytes 263200 | tf_op jit(solution)/shard_map/ppermute | solution.py:99
  158.9 0.1 collective-permute-start.2
  159.0 14.6 %collective-permute-done.2 = f32[257,256]{1,0:T(8,128)S(1)} collective-permute-done((f32[257,256]{1,0:T(8,128)S(1)}, f32[257,256]{1,0:T(8,128)S(1)}, u32[]{:S(2)}, u32[]{:S(2)}) %collective-permute-start.2) | collective-permute-done | bytes 263200 | tf_op jit(solution)/shard_map/ppermute | solution.py:99
  173.7 2.4 collective-permute-start.3
  176.1 12.0 %collective-permute-done.3 = f32[257,256]{1,0:T(8,128)S(1)} collective-permute-done((f32[257,256]{1,0:T(8,128)S(1)}, f32[257,256]{1,0:T(8,128)S(1)}, u32[]{:S(2)}, u32[]{:S(2)}) %collective-permute-start.3) | collective-permute-done | bytes 263200 | tf_op jit(solution)/shard_map/ppermute | solution.py:99
  188.2 0.8 collective-permute-start.4
  188.9 6.3 %collective-permute-done.4 = f32[257,256]{1,0:T(8,128)S(1)} collective-permute-done((f32[257,256]{1,0:T(8,128)S(1)}, f32[257,256]{1,0:T(8,128)S(1)}, u32[]{:S(2)}, u32[]{:S(2)}) %collective-permute-start.4) | collective-permute-done | bytes 263200 | tf_op jit(solution)/shard_map/ppermute | solution.py:99
  195.2 1.7 collective-permute-start.5
  197.0 6.3 %collective-permute-done.5 = f32[257,256]{1,0:T(8,128)S(1)} collective-permute-done((f32[257,256]{1,0:T(8,128)S(1)}, f32[257,256]{1,0:T(8,128)S(1)}, u32[]{:S(2)}, u32[]{:S(2)}) %collective-permute-start.5) | collective-permute-done | bytes 263200 | tf_op jit(solution)/shard_map/ppermute | solution.py:99
  203.3 2.7 %collective-permute-start.6 = (f32[257,256]{1,0:T(8,128)S(1)}, f32[257,256]{1,0:T(8,128)S(1)}, u32[]{:S(2)}, u32[]{:S(2)}) collective-permute-start(f32[257,256]{1,0:T(8,128)S(1)} %add.46), channel_id=1, source_target_pairs={{0,64},{16,80},{32,96},{48,112},{64,0},{80,16},{96,32},{112,48},{1... | collective-permute-start | bytes 789512 | tf_op jit(solution)/shard_map/ppermute | solution.py:99
  206.0 5.3 %collective-permute-done.6 = f32[257,256]{1,0:T(8,128)S(1)} collective-permute-done((f32[257,256]{1,0:T(8,128)S(1)}, f32[257,256]{1,0:T(8,128)S(1)}, u32[]{:S(2)}, u32[]{:S(2)}) %collective-permute-start.6) | collective-permute-done | bytes 263200 | tf_op jit(solution)/shard_map/ppermute | solution.py:99
  211.4 0.6 slice_multiply_fusion.1
  212.0 0.7 slice_multiply_fusion
  212.7 12.4 %shard_map.114 = f32[32,128,256]{2,1,0:T(8,128)} custom-call(s32[384]{0:T(512)} %reduce.2.dest_ref, s32[384]{0:T(512)} %reduce.3.source_ref, s32[1]{0:T(128)} %bitcast.15.count_ref, bf16[384,128,128]{2,1,0:T(8,128)(2,1)} %bitcast.17, bf16[64,128,256]{2,1,0:T(8,128)(2,1)} %bitcast.21), custom_call_target="tpu_custom_call" | custom-call | flops 3221225472 | bytes 20971520 | tf_op jit(solution)/shard_map/pallas_call | solution.py:73
  225.1 3.8 %convert_element_type.40 = bf16[32,128,256]{2,1,0:T(8,128)(2,1)} convert(f32[32,128,256]{2,1,0:T(8,128)} %shard_map.114) | non-fusion elementwise | flops 1048576 | bytes 6291456 | tf_op jit(solution)/shard_map/convert_element_type | solution.py:203
  228.9 29.6 %shard_map.115 = bf16[8,512,256]{2,1,0:T(8,128)(2,1)} custom-call(bf16[8,512,256]{2,1,0:T(8,128)(2,1)} %bitcast.19), custom_call_target="tpu_custom_call" | custom-call | bytes 4194304 | tf_op jit(solution)/shard_map/pallas_call | solution.py:139
  258.5 2.7 reduce_sum.35
  (15 shorter events, 0.3 us)
Async XLA Ops:
  7.2 132.0 %copy-start = (bf16[256,256]{1,0:T(8,128)(2,1)S(1)}, bf16[256,256]{1,0:T(8,128)(2,1)}, u32[]{:S(2)}) copy-start(bf16[256,256]{1,0:T(8,128)(2,1)} %param.9) | copy-start | bytes 393220
  7.2 204.2 %all-gather.2.cloned.1.call-start = ((), (), s32[]{:S(2)}) async-start(), calls=%async_computation | async-start | bytes 4456448 | tf_op jit(solution)/shard_map/all_gather | solution.py:195
  136.2 2.9 %copy-start.1 = (bf16[512,256]{1,0:T(8,128)(2,1)S(1)}, bf16[512,256]{1,0:T(8,128)(2,1)}, u32[]{:S(2)}) copy-start(bf16[512,256]{1,0:T(8,128)(2,1)} %param.11) | copy-start | bytes 786436
  136.2 2.9 %copy-start.2 = (f32[256]{0:T(256)S(1)}, f32[256]{0:T(256)}, u32[]{:S(2)}) copy-start(f32[256]{0:T(256)} %param.10) | copy-start | bytes 3076
  141.6 6.2 %collective-permute-start = (f32[257,256]{1,0:T(8,128)S(1)}, f32[257,256]{1,0:T(8,128)S(1)}, u32[]{:S(2)}, u32[]{:S(2)}) collective-permute-start(f32[257,256]{1,0:T(8,128)S(1)} %pad_maximum_fusion), channel_id=1, source_target_pairs={{0,1},{1,0},{2,3},{3,2},{4,5},{5,4},{6,7},{7,6},{8,9},{9,8},{10,11... | collective-permute-start | bytes 789512 | tf_op jit(solution)/shard_map/ppermute | solution.py:99
  147.8 11.1 %collective-permute-start.1 = (f32[257,256]{1,0:T(8,128)S(1)}, f32[257,256]{1,0:T(8,128)S(1)}, u32[]{:S(2)}, u32[]{:S(2)}) collective-permute-start(f32[257,256]{1,0:T(8,128)S(1)} %fusion), channel_id=1, source_target_pairs={{0,2},{1,3},{2,0},{3,1},{4,6},{5,7},{6,4},{7,5},{8,10},{9,11},{10,... | collective-permute-start | bytes 789512 | tf_op jit(solution)/shard_map/ppermute | solution.py:99
  158.9 14.7 %collective-permute-start.2 = (f32[257,256]{1,0:T(8,128)S(1)}, f32[257,256]{1,0:T(8,128)S(1)}, u32[]{:S(2)}, u32[]{:S(2)}) collective-permute-start(f32[257,256]{1,0:T(8,128)S(1)} %add.42), channel_id=1, source_target_pairs={{0,4},{1,5},{2,6},{3,7},{4,0},{5,1},{6,2},{7,3},{8,12},{9,13},{10,... | collective-permute-start | bytes 789512 | tf_op jit(solution)/shard_map/ppermute | solution.py:99
  173.7 14.4 %collective-permute-start.3 = (f32[257,256]{1,0:T(8,128)S(1)}, f32[257,256]{1,0:T(8,128)S(1)}, u32[]{:S(2)}, u32[]{:S(2)}) collective-permute-start(f32[257,256]{1,0:T(8,128)S(1)} %add.43), channel_id=1, source_target_pairs={{0,8},{1,9},{2,10},{3,11},{4,12},{5,13},{6,14},{7,15},{8,0},{9,1},... | collective-permute-start | bytes 789512 | tf_op jit(solution)/shard_map/ppermute | solution.py:99
  188.2 7.0 %collective-permute-start.4 = (f32[257,256]{1,0:T(8,128)S(1)}, f32[257,256]{1,0:T(8,128)S(1)}, u32[]{:S(2)}, u32[]{:S(2)}) collective-permute-start(f32[257,256]{1,0:T(8,128)S(1)} %add.44), channel_id=1, source_target_pairs={{0,16},{16,0},{32,48},{48,32},{64,80},{80,64},{96,112},{112,96},{1... | collective-permute-start | bytes 789512 | tf_op jit(solution)/shard_map/ppermute | solution.py:99
  195.2 8.0 %collective-permute-start.5 = (f32[257,256]{1,0:T(8,128)S(1)}, f32[257,256]{1,0:T(8,128)S(1)}, u32[]{:S(2)}, u32[]{:S(2)}) collective-permute-start(f32[257,256]{1,0:T(8,128)S(1)} %add.45), channel_id=1, source_target_pairs={{0,32},{16,48},{32,0},{48,16},{64,96},{80,112},{96,64},{112,80},{1... | collective-permute-start | bytes 789512 | tf_op jit(solution)/shard_map/ppermute | solution.py:99
  203.3 8.0 %collective-permute-start.6 = (f32[257,256]{1,0:T(8,128)S(1)}, f32[257,256]{1,0:T(8,128)S(1)}, u32[]{:S(2)}, u32[]{:S(2)}) collective-permute-start(f32[257,256]{1,0:T(8,128)S(1)} %add.46), channel_id=1, source_target_pairs={{0,64},{16,80},{32,96},{48,112},{64,0},{80,16},{96,32},{112,48},{1... | collective-permute-start | bytes 789512 | tf_op jit(solution)/shard_map/ppermute | solution.py:99
Sparse Core Ops, SparseCore 0:
  141.4 48.8 all-gather.1

commit v7 on v6

--- a/solution.py
+++ b/solution.py
@@ -91,14 +91,54 @@
     )(dest_ids, source_ids, live_count.reshape(1), tiles, source_blocks)
 
 
-def butterfly_sum(value, axis):
-    size = lax.axis_size(axis)
-    distance = 1
-    while distance < size:
-        pairs = [(i, i ^ distance) for i in range(size)]
-        value = value + lax.ppermute(value, axis, pairs)
-        distance *= 2
-    return value
+def butterfly_kernel(steps, value_ref, out_ref, slots, send_sems, recv_sems):
+    partners = []
+    for axis, distance in steps:
+        me = lax.axis_index(axis)
+        bit = (me // distance) % 2
+        partners.append((axis, me + distance - 2 * distance * bit))
+    barrier = pltpu.get_barrier_semaphore()
+    for axis, partner in partners:
+        pl.semaphore_signal(
+            barrier, 1, device_id={axis: partner}, device_id_type=pl.DeviceIdType.MESH
+        )
+    pl.semaphore_wait(barrier, len(partners))
+    out_ref[...] = value_ref[...]
+    for index, (axis, partner) in enumerate(partners):
+        copy = pltpu.make_async_remote_copy(
+            src_ref=out_ref,
+            dst_ref=slots.at[index],
+            send_sem=send_sems.at[index],
+            recv_sem=recv_sems.at[index],
+            device_id={axis: partner},
+            device_id_type=pl.DeviceIdType.MESH,
+        )
+        copy.start()
+        copy.wait_send()
+        copy.wait_recv()
+        out_ref[...] = out_ref[...] + slots[index]
+
+
+def butterfly_sum(value, axes, tag):
+    steps = []
+    for axis, size in axes:
+        distance = 1
+        while distance < size:
+            steps.append((axis, distance))
+            distance *= 2
+    count = len(steps)
+    return pl.pallas_call(
+        functools.partial(butterfly_kernel, tuple(steps)),
+        out_shape=jax.ShapeDtypeStruct(value.shape, value.dtype),
+        in_specs=[pl.BlockSpec(memory_space=pltpu.VMEM)],
+        out_specs=pl.BlockSpec(memory_space=pltpu.VMEM),
+        scratch_shapes=[
+            pltpu.VMEM((count,) + value.shape, value.dtype),
+            pltpu.SemaphoreType.DMA((count,)),
+            pltpu.SemaphoreType.DMA((count,)),
+        ],
+        compiler_params=pltpu.CompilerParams(collective_id=tag, has_side_effects=True),
+    )(value)
 
 
 def exchange_kernel(axis, size, spread, parts_ref, out_ref, local_sem, send_sems, recv_sems):
@@ -151,9 +191,16 @@
     )(parts)
 
 
-def gather_all(value, axis, size, tag):
-    got = exchange(value, axis, size, True, tag)
+def gather_all(value, axis, size):
+    spread = jnp.broadcast_to(value[None], (size,) + value.shape)
+    got = lax.all_to_all(spread, axis, 0, 0, tiled=False)
     return got.reshape((size * value.shape[0],) + value.shape[1:])
+
+
+def scatter_sum_native(value, axis, size):
+    parts = value.reshape((size, value.shape[0] // size) + value.shape[1:])
+    got = lax.all_to_all(parts, axis, 0, 0, tiled=False)
+    return jnp.sum(got.astype(jnp.float32), axis=0)
 
 
 def scatter_sum(value, axis, size, tag):
@@ -175,13 +222,13 @@
     blocks_down = own_nodes * col_count // block
     blocks_across = own_nodes * row_count // block
     factor = 1.0 / math.sqrt(own_nodes * row_count * col_count)
-    panel = gather_all(features, "row", row_count, 0)
+    panel = gather_all(features, "row", row_count)
     panel_blocks = panel.reshape(blocks_across, block, width)
     partial_value = accumulate(
         tile_set, dest_ids, source_ids, live_count, panel_blocks, blocks_down, False
     )
     term = partial_value.reshape(blocks_down * block, width)
-    summed = scatter_sum(term.astype(jnp.bfloat16), "col", col_count, 1)
+    summed = scatter_sum_native(term.astype(jnp.bfloat16), "col", col_count)
     aggregated = summed.astype(jnp.bfloat16)
     preact = jnp.dot(aggregated, weight, preferred_element_type=jnp.float32) + bias
     hidden = jax.nn.silu(preact).astype(jnp.bfloat16)
@@ -193,14 +240,14 @@
     grad_agg = jnp.dot(grad_pre, weight.T, preferred_element_type=jnp.float32).astype(jnp.bfloat16)
     packed = jnp.concatenate([local_weight, local_bias[None, :]], axis=0)
     grad_panel = lax.all_gather(grad_agg, "col", axis=0, tiled=True)
-    packed = butterfly_sum(butterfly_sum(packed, "col"), "row")
+    packed = butterfly_sum(packed, (("col", col_count), ("row", row_count)), 1)
     grad_panel, packed = lax.optimization_barrier((grad_panel, packed))
     grad_blocks = grad_panel.reshape(blocks_down, block, width)
     partial_back = accumulate(
         tile_set, dest_ids, source_ids, live_count, grad_blocks, blocks_across, True
     )
     term_back = partial_back.reshape(blocks_across * block, width)
-    grad_features = scatter_sum(term_back.astype(jnp.bfloat16), "row", row_count, 2).astype(
+    grad_features = scatter_sum(term_back.astype(jnp.bfloat16), "row", row_count, 0).astype(
         jnp.bfloat16
     )
     grad_weight = packed[:width] * factor

time: 269 us -> 252 us (0.937)
  blocking collectives: 0 us -> 62.1 us
  Pallas kernels: 162 us -> 115 us
  waiting for transfers between devices: 56.7 us -> 26.6 us
  starting transfers between devices: 12.9 us -> 7.9 us
  local copies, waits for them, and re-layouts: 0.02 us -> 3.89 us
    pallas_call x3 -> x1, Pallas kernels: 138 us -> 34.2 us  [exchange(): pl.pallas_call(functools.partial(exchange_kernel, axis, size, spread), ou...]
    pallas_call x0 -> x1, Pallas kernels: none -> 62.6 us  [butterfly_sum(): pl.pallas_call(functools.partial(butterfly_kernel, tuple(steps)), out_sha...]
    all_to_all x0 -> x1, blocking collectives: none -> 62.1 us  [scatter_sum_native(): got = lax.all_to_all(parts, axis, 0, 0, tiled=False)]
    ppermute x7 -> x0, waiting for transfers between devices: 56.7 us -> none  [butterfly_sum(): value = value + lax.ppermute(value, axis, pairs)]
    all_to_all x0 -> x1, waiting for transfers between devices: none -> 26.6 us  [gather_all(): got = lax.all_to_all(spread, axis, 0, 0, tiled=False)]
    ppermute x7 -> x0, starting transfers between devices: 12.9 us -> none  [butterfly_sum(): value = value + lax.ppermute(value, axis, pairs)]
    all_to_all x0 -> x1, starting transfers between devices: none -> 7.87 us  [gather_all(): got = lax.all_to_all(spread, axis, 0, 0, tiled=False)]
    pallas_call x2, Pallas kernels: 24.2 us -> 18.2 us  [accumulate(): pl.pallas_call(functools.partial(accumulate_kernel, backward), out_shape=...]
  transfers between devices with their start and end apart: 8 -> 2, of which waited for: 7 -> 1; matrix products, arithmetic and copies ran while one was open for 0% -> 1% of each run, Pallas kernels for 0% -> 25%
where the time goes in v7:
time: 252 us; the launch traced here: 251 us
  Pallas kernels  115 us (46%)
  blocking collectives  62.1 us (25%)
  waiting for transfers between devices  26.6 us (11%)
  other arithmetic  18.1 us (7%)
  between operations  14.8 us (6%)
  starting transfers between devices  7.9 us (3%)
  local copies, waits for them, and re-layouts  3.89 us (2%)
    pallas_call x1, Pallas kernels, butterfly_sum(): pl.pallas_call(functools.partial(butterfly_kernel, tuple(steps)), out_sha...  62.6 us
    all_to_all x1, blocking collectives, scatter_sum_native(): got = lax.all_to_all(parts, axis, 0, 0, tiled=False)  62.1 us
    pallas_call x1, Pallas kernels, exchange(): pl.pallas_call(functools.partial(exchange_kernel, axis, size, spread), ou...  34.2 us
    all_to_all x1, waiting for transfers between devices, gather_all(): got = lax.all_to_all(spread, axis, 0, 0, tiled=False)  26.6 us
    pallas_call x2, Pallas kernels, accumulate(): pl.pallas_call(functools.partial(accumulate_kernel, backward), out_shape=...  18.2 us
    all_to_all x1, starting transfers between devices, gather_all(): got = lax.all_to_all(spread, axis, 0, 0, tiled=False)  7.87 us
  transfers between devices with their start and end apart: 2, of which 1 were waited for; matrix products, arithmetic and copies ran while one was open for 1% of the time, Pallas kernels for 25%

profile of v7, /device:TPU:0, one launch (start us, length us, event | category | flops | bytes accessed | tf_op | source)
XLA Modules:
  0.0 250.8 jit_solution(10504392446538956809)
XLA Ops:
  7.2 0.0 copy-start
  7.2 0.0 copy-start.2
  7.2 0.0 copy-start.3
  7.2 2.5 broadcast_in_dim.4
  9.7 7.9 %all-to-all-start = ((bf16[8,512,256]{2,1,0:T(8,128)(2,1)}), bf16[8,512,256]{2,1,0:T(8,128)(2,1)S(1)}, u32[]{:S(2)}, u32[]{:S(2)}) async-start(bf16[8,512,256]{2,1,0:T(8,128)(2,1)} %broadcast_in_dim.4), calls=%async_computation | async-start | bytes 4194304 | tf_op jit(solution)/shard_map/all_to_all | solution.py:196
  17.5 0.0 all-gather.2.cloned.1.call-start
  18.2 0.0 copy-done.2
  18.2 0.6 reduce.2.dest_ref
  18.8 0.0 copy-done.3
  18.8 0.5 reduce.3.source_ref
  19.4 26.6 %all-to-all-done = bf16[8,512,256]{2,1,0:T(8,128)(2,1)S(1)} async-done(((bf16[8,512,256]{2,1,0:T(8,128)(2,1)}), bf16[8,512,256]{2,1,0:T(8,128)(2,1)S(1)}, u32[]{:S(2)}, u32[]{:S(2)}) %all-to-all-start) | async-done | bytes 2097184 | tf_op jit(solution)/shard_map/all_to_all | solution.py:196
  46.0 1.4 copy-done.1
  47.4 9.5 %shard_map.111 = f32[64,128,256]{2,1,0:T(8,128)} custom-call(s32[384]{0:T(512)} %reduce.2.dest_ref, s32[384]{0:T(512)} %reduce.3.source_ref, s32[1]{0:T(128)} %bitcast.14.count_ref, bf16[384,128,128]{2,1,0:T(8,128)(2,1)} %bitcast.16, bf16[32,128,256]{2,1,0:T(8,128)(2,1)} %bitcast.20), custom_call_target="tpu_custom_call" | custom-call | flops 3221225472 | bytes 23068672 | tf_op jit(solution)/shard_map/pallas_call | solution.py:73
  56.9 4.0 %convert_element_type.33 = bf16[64,128,256]{2,1,0:T(8,128)(2,1)S(1)} convert(f32[64,128,256]{2,1,0:T(8,128)} %shard_map.111) | non-fusion elementwise | flops 2097152 | bytes 12582912 | tf_op jit(solution)/shard_map/convert_element_type | solution.py:231
  60.9 62.1 %all_to_all.10 = bf16[16,512,256]{2,1,0:T(8,128)(2,1)} all-to-all(bf16[16,512,256]{2,1,0:T(8,128)(2,1)S(1)} %bitcast.18), channel_id=1, replica_groups=mesh['row'=8,'col'=16] {'col'}, dimensions={0} | all-to-all | bytes 8388608 | tf_op jit(solution)/shard_map/all_to_all | solution.py:202
  123.0 2.9 %reduce_sum.33 = bf16[512,256]{1,0:T(8,128)(2,1)S(1)} reduce(bf16[16,512,256]{2,1,0:T(8,128)(2,1)} %all_to_all.10, bf16[]{:T(256)} %constant.4.clone.1), dimensions={0}, to_apply=%region_0.0 | reduce | flops 1966080 | bytes 4456450 | tf_op jit(solution)/shard_map/reduce_sum | solution.py:203
  125.9 0.0 copy-done
  125.9 0.0 copy-done.4
  125.9 0.0 copy-done.5
  126.0 1.1 convert_reduce_fusion
  127.1 1.0 convolution_convert_fusion
  128.0 0.0 all-gather.2.cloned.1.call-update
  128.1 0.3 fusion
  128.3 0.7 pad_maximum_fusion.value_ref
  129.1 62.6 %shard_map.112 = f32[257,256]{1,0:T(8,128)} custom-call(f32[257,256]{1,0:T(8,128)} %pad_maximum_fusion.value_ref), custom_call_target="tpu_custom_call" | custom-call | tf_op jit(solution)/shard_map/pallas_call | solution.py:130
  191.7 0.0 all-gather.2.cloned.1.call-done
  191.7 1.3 slice_multiply_fusion.1
  193.0 1.7 slice_multiply_fusion
  194.7 8.7 %shard_map.113 = f32[32,128,256]{2,1,0:T(8,128)} custom-call(s32[384]{0:T(512)} %reduce.2.dest_ref, s32[384]{0:T(512)} %reduce.3.source_ref, s32[1]{0:T(128)} %bitcast.15.count_ref, bf16[384,128,128]{2,1,0:T(8,128)(2,1)} %bitcast.17, bf16[64,128,256]{2,1,0:T(8,128)(2,1)} %bitcast.21), custom_call_target="tpu_custom_call" | custom-call | flops 3221225472 | bytes 20971520 | tf_op jit(solution)/shard_map/pallas_call | solution.py:73
  203.3 3.8 %convert_element_type.40 = bf16[32,128,256]{2,1,0:T(8,128)(2,1)} convert(f32[32,128,256]{2,1,0:T(8,128)} %shard_map.113) | non-fusion elementwise | flops 1048576 | bytes 6291456 | tf_op jit(solution)/shard_map/convert_element_type | solution.py:250
  207.2 34.2 %shard_map.114 = bf16[8,512,256]{2,1,0:T(8,128)(2,1)} custom-call(bf16[8,512,256]{2,1,0:T(8,128)(2,1)} %bitcast.19), custom_call_target="tpu_custom_call" | custom-call | bytes 4194304 | tf_op jit(solution)/shard_map/pallas_call | solution.py:179
  241.3 2.7 %reduce_sum.35 = bf16[512,256]{1,0:T(8,128)(2,1)} reduce(bf16[8,512,256]{2,1,0:T(8,128)(2,1)} %shard_map.114, bf16[]{:T(256)} %constant.4.clone.1), dimensions={0}, to_apply=%region_2.3 | reduce | flops 917504 | bytes 2359298 | tf_op jit(solution)/shard_map/reduce_sum | solution.py:209
  (3 shorter events, 0.0 us)
Async XLA Ops:
  7.2 118.8 %copy-start = (bf16[256,256]{1,0:T(8,128)(2,1)S(1)}, bf16[256,256]{1,0:T(8,128)(2,1)}, u32[]{:S(2)}) copy-start(bf16[256,256]{1,0:T(8,128)(2,1)} %param.9) | copy-start | bytes 393220
  7.2 11.1 %copy-start.2 = (s32[1,1,384]{2,1,0:T(1,128)S(1)}, s32[1,1,384]{2,1,0:T(1,128)}, u32[]{:S(2)}) copy-start(s32[1,1,384]{2,1,0:T(1,128)} %param.13) | copy-start | bytes 4612
  7.2 11.6 %copy-start.3 = (s32[1,1,384]{2,1,0:T(1,128)S(1)}, s32[1,1,384]{2,1,0:T(1,128)}, u32[]{:S(2)}) copy-start(s32[1,1,384]{2,1,0:T(1,128)} %param.14) | copy-start | bytes 4612
  9.7 36.3 %all-to-all-start = ((bf16[8,512,256]{2,1,0:T(8,128)(2,1)}), bf16[8,512,256]{2,1,0:T(8,128)(2,1)S(1)}, u32[]{:S(2)}, u32[]{:S(2)}) async-start(bf16[8,512,256]{2,1,0:T(8,128)(2,1)} %broadcast_in_dim.4), calls=%async_computation | async-start | bytes 4194304 | tf_op jit(solution)/shard_map/all_to_all | solution.py:196
  17.5 174.2 %all-gather.2.cloned.1.call-start = ((), (), s32[]{:S(2)}) async-start(), calls=%async_computation.2 | async-start | bytes 4456448 | tf_op jit(solution)/shard_map/all_gather | solution.py:242
  46.0 1.4 copy-start.1
  123.0 2.9 %copy-start.4 = (bf16[512,256]{1,0:T(8,128)(2,1)S(1)}, bf16[512,256]{1,0:T(8,128)(2,1)}, u32[]{:S(2)}) copy-start(bf16[512,256]{1,0:T(8,128)(2,1)} %param.11) | copy-start | bytes 786436
  123.0 2.9 %copy-start.5 = (f32[256]{0:T(256)S(1)}, f32[256]{0:T(256)}, u32[]{:S(2)}) copy-start(f32[256]{0:T(256)} %param.10) | copy-start | bytes 3076
Sparse Core Ops, SparseCore 0:
  128.2 43.4 all-gather.1

commit v8 on v7

--- a/solution.py
+++ b/solution.py
@@ -141,7 +141,8 @@
     )(value)
 
 
-def exchange_kernel(axis, size, spread, parts_ref, out_ref, local_sem, send_sems, recv_sems):
+def exchange_kernel(axis, size, spread, parts_ref, value_ref, out_ref, sum_ref, local_sem,
+                    send_sems, recv_sems, slots, sum_send_sems, sum_recv_sems):
     me = lax.axis_index(axis)
     barrier = pltpu.get_barrier_semaphore()
     for shift in range(1, size):
@@ -167,28 +168,55 @@
         parts_ref if spread else parts_ref.at[me], out_ref.at[me], local_sem
     )
     local.start()
+    sum_ref[...] = value_ref[...]
+    distance = 1
+    index = 0
+    while distance < size:
+        bit = (me // distance) % 2
+        partner = me + distance - 2 * distance * bit
+        step = pltpu.make_async_remote_copy(
+            src_ref=sum_ref,
+            dst_ref=slots.at[index],
+            send_sem=sum_send_sems.at[index],
+            recv_sem=sum_recv_sems.at[index],
+            device_id={axis: partner},
+            device_id_type=pl.DeviceIdType.MESH,
+        )
+        step.start()
+        step.wait_send()
+        step.wait_recv()
+        sum_ref[...] = sum_ref[...] + slots[index]
+        distance *= 2
+        index += 1
     local.wait()
     for copy in copies:
         copy.wait_send()
         copy.wait_recv()
 
 
-def exchange(parts, axis, size, spread, tag):
+def exchange(parts, value, axis, size, spread, tag):
     shape = (size,) + parts.shape[1 - spread:]
     nbytes = math.prod(shape) * parts.dtype.itemsize
+    steps = max(size.bit_length() - 1, 1)
     return pl.pallas_call(
         functools.partial(exchange_kernel, axis, size, spread),
-        out_shape=jax.ShapeDtypeStruct(shape, parts.dtype),
-        in_specs=[pl.BlockSpec(memory_space=pl.ANY)],
-        out_specs=pl.BlockSpec(memory_space=pl.ANY),
+        out_shape=(
+            jax.ShapeDtypeStruct(shape, parts.dtype),
+            jax.ShapeDtypeStruct(value.shape, value.dtype),
+        ),
+        in_specs=[pl.BlockSpec(memory_space=pl.ANY), pl.BlockSpec(memory_space=pltpu.VMEM)],
+        out_specs=(pl.BlockSpec(memory_space=pl.ANY), pl.BlockSpec(memory_space=pltpu.VMEM)),
         scratch_shapes=[
             pltpu.SemaphoreType.DMA,
             pltpu.SemaphoreType.DMA((size,)),
             pltpu.SemaphoreType.DMA((size,)),
+            pltpu.VMEM((steps,) + value.shape, value.dtype),
+            pltpu.SemaphoreType.DMA((steps,)),
+            pltpu.SemaphoreType.DMA((steps,)),
         ],
         compiler_params=pltpu.CompilerParams(collective_id=tag, has_side_effects=True),
         cost_estimate=pl.CostEstimate(flops=0, transcendentals=0, bytes_accessed=2 * nbytes),
-    )(parts)
+    )(parts, value)
 
 
 def gather_all(value, axis, size):
@@ -203,10 +231,10 @@
     return jnp.sum(got.astype(jnp.float32), axis=0)
 
 
-def scatter_sum(value, axis, size, tag):
+def scatter_sum(value, extra, axis, size, tag):
     parts = value.reshape((size, value.shape[0] // size) + value.shape[1:])
-    got = exchange(parts, axis, size, False, tag)
-    return jnp.sum(got.astype(jnp.float32), axis=0)
+    got, extra = exchange(parts, extra, axis, size, False, tag)
+    return jnp.sum(got.astype(jnp.float32), axis=0), extra
 
 
 def per_device(features, weight, bias, cotangent, tiles, tile_rows, tile_cols, tile_counts):
@@ -240,16 +268,17 @@
     grad_agg = jnp.dot(grad_pre, weight.T, preferred_element_type=jnp.float32).astype(jnp.bfloat16)
     packed = jnp.concatenate([local_weight, local_bias[None, :]], axis=0)
     grad_panel = lax.all_gather(grad_agg, "col", axis=0, tiled=True)
-    packed = butterfly_sum(packed, (("col", col_count), ("row", row_count)), 1)
+    packed = butterfly_sum(packed, (("col", col_count),), 1)
     grad_panel, packed = lax.optimization_barrier((grad_panel, packed))
     grad_blocks = grad_panel.reshape(blocks_down, block, width)
     partial_back = accumulate(
         tile_set, dest_ids, source_ids, live_count, grad_blocks, blocks_across, True
     )
     term_back = partial_back.reshape(blocks_across * block, width)
-    grad_features = scatter_sum(term_back.astype(jnp.bfloat16), "row", row_count, 0).astype(
-        jnp.bfloat16
-    )
+    grad_features, packed = scatter_sum(
+        term_back.astype(jnp.bfloat16), packed, "row", row_count, 0
+    )
+    grad_features = grad_features.astype(jnp.bfloat16)
     grad_weight = packed[:width] * factor
     grad_bias = packed[width] * factor
     return (hidden, grad_weight, grad_bias, grad_features)

time: 252 us -> 264 us (1.048)
  Pallas kernels: 115 us -> 133 us
  blocking collectives: 62.1 us -> 55.1 us
    pallas_call x1, Pallas kernels: 34.2 us -> 56 us  [exchange(): pl.pallas_call(functools.partial(exchange_kernel, axis, size, spread), ou...]
    pallas_call x1, Pallas kernels: 62.6 us -> 41.2 us  [butterfly_sum(): pl.pallas_call(functools.partial(butterfly_kernel, tuple(steps)), out_sha...]
    pallas_call x2, Pallas kernels: 18.2 us -> 35.6 us  [accumulate(): pl.pallas_call(functools.partial(accumulate_kernel, backward), out_shape=...]
    all_to_all x1, blocking collectives: 62.1 us -> 55.1 us  [scatter_sum_native(): got = lax.all_to_all(parts, axis, 0, 0, tiled=False)]
  transfers between devices with their start and end apart: 2 -> 2, of which waited for: 1 -> 2; matrix products, arithmetic and copies ran while one was open for 1% -> 1% of each run, Pallas kernels for 25% -> 16%
where the time goes in v8:
time: 264 us; the launch traced here: 263 us
  Pallas kernels  133 us (50%)
  blocking collectives  55.1 us (21%)
  waiting for transfers between devices  28 us (11%)
  other arithmetic  18.2 us (7%)
  between operations  14.8 us (6%)
  starting transfers between devices  7.9 us (3%)
  local copies, waits for them, and re-layouts  3.89 us (1%)
    pallas_call x1, Pallas kernels, exchange(): pl.pallas_call(functools.partial(exchange_kernel, axis, size, spread), ou...  56 us
    all_to_all x1, blocking collectives, scatter_sum_native(): got = lax.all_to_all(parts, axis, 0, 0, tiled=False)  55.1 us
    pallas_call x1, Pallas kernels, butterfly_sum(): pl.pallas_call(functools.partial(butterfly_kernel, tuple(steps)), out_sha...  41.2 us
    pallas_call x2, Pallas kernels, accumulate(): pl.pallas_call(functools.partial(accumulate_kernel, backward), out_shape=...  35.6 us
    all_to_all x1, waiting for transfers between devices, gather_all(): got = lax.all_to_all(spread, axis, 0, 0, tiled=False)  26.5 us
    all_to_all x1, starting transfers between devices, gather_all(): got = lax.all_to_all(spread, axis, 0, 0, tiled=False)  7.87 us
  transfers between devices with their start and end apart: 2, of which 2 were waited for; matrix products, arithmetic and copies ran while one was open for 1% of the time, Pallas kernels for 16%

profile of v8, /device:TPU:0, one launch (start us, length us, event | category | flops | bytes accessed | tf_op | source)
XLA Modules:
  0.0 263.0 jit_solution(16624663204526780865)
XLA Ops:
  7.2 0.0 copy-start
  7.2 0.0 copy-start.2
  7.2 0.0 copy-start.3
  7.2 2.5 broadcast_in_dim.4
  9.7 7.9 %all-to-all-start = ((bf16[8,512,256]{2,1,0:T(8,128)(2,1)}), bf16[8,512,256]{2,1,0:T(8,128)(2,1)S(1)}, u32[]{:S(2)}, u32[]{:S(2)}) async-start(bf16[8,512,256]{2,1,0:T(8,128)(2,1)} %broadcast_in_dim.4), calls=%async_computation | async-start | bytes 4194304 | tf_op jit(solution)/shard_map/all_to_all | solution.py:224
  17.5 0.0 all-gather.2.cloned.1.call-start
  18.2 0.0 copy-done.2
  18.2 0.6 reduce.2.dest_ref
  18.8 0.0 copy-done.3
  18.8 0.6 reduce.3.source_ref
  19.4 26.5 %all-to-all-done = bf16[8,512,256]{2,1,0:T(8,128)(2,1)S(1)} async-done(((bf16[8,512,256]{2,1,0:T(8,128)(2,1)}), bf16[8,512,256]{2,1,0:T(8,128)(2,1)S(1)}, u32[]{:S(2)}, u32[]{:S(2)}) %all-to-all-start) | async-done | bytes 2097184 | tf_op jit(solution)/shard_map/all_to_all | solution.py:224
  46.0 1.4 copy-done.1
  47.4 17.4 %shard_map.111 = f32[64,128,256]{2,1,0:T(8,128)} custom-call(s32[384]{0:T(512)} %reduce.2.dest_ref, s32[384]{0:T(512)} %reduce.3.source_ref, s32[1]{0:T(128)} %bitcast.14.count_ref, bf16[384,128,128]{2,1,0:T(8,128)(2,1)} %bitcast.16, bf16[32,128,256]{2,1,0:T(8,128)(2,1)} %bitcast.20), custom_call_target="tpu_custom_call" | custom-call | flops 3221225472 | bytes 23068672 | tf_op jit(solution)/shard_map/pallas_call | solution.py:73
  64.8 4.0 %convert_element_type.33 = bf16[64,128,256]{2,1,0:T(8,128)(2,1)S(1)} convert(f32[64,128,256]{2,1,0:T(8,128)} %shard_map.111) | non-fusion elementwise | flops 2097152 | bytes 12582912 | tf_op jit(solution)/shard_map/convert_element_type | solution.py:259
  68.8 55.1 %all_to_all.10 = bf16[16,512,256]{2,1,0:T(8,128)(2,1)} all-to-all(bf16[16,512,256]{2,1,0:T(8,128)(2,1)S(1)} %bitcast.18), channel_id=1, replica_groups=mesh['row'=8,'col'=16] {'col'}, dimensions={0} | all-to-all | bytes 8388608 | tf_op jit(solution)/shard_map/all_to_all | solution.py:230
  123.9 2.9 %reduce_sum.33 = bf16[512,256]{1,0:T(8,128)(2,1)S(1)} reduce(bf16[16,512,256]{2,1,0:T(8,128)(2,1)} %all_to_all.10, bf16[]{:T(256)} %constant.4.clone.1), dimensions={0}, to_apply=%region_0.0 | reduce | flops 1966080 | bytes 4456450 | tf_op jit(solution)/shard_map/reduce_sum | solution.py:231
  126.8 0.0 copy-done
  126.8 0.0 copy-done.4
  126.9 0.0 copy-done.5
  126.9 1.1 convert_reduce_fusion
  128.0 1.0 convolution_convert_fusion
  129.0 0.0 all-gather.2.cloned.1.call-update
  129.0 0.3 fusion
  129.3 0.7 pad_maximum_fusion.value_ref
  130.0 41.2 %shard_map.112.value_ref = f32[257,256]{1,0:T(8,128)} custom-call(f32[257,256]{1,0:T(8,128)} %pad_maximum_fusion.value_ref), custom_call_target="tpu_custom_call" | custom-call | tf_op jit(solution)/shard_map/pallas_call | solution.py:130
  171.2 1.4 all-gather.2.cloned.1.call-done
  172.6 18.2 %shard_map.113 = f32[32,128,256]{2,1,0:T(8,128)} custom-call(s32[384]{0:T(512)} %reduce.2.dest_ref, s32[384]{0:T(512)} %reduce.3.source_ref, s32[1]{0:T(128)} %bitcast.15.count_ref, bf16[384,128,128]{2,1,0:T(8,128)(2,1)} %bitcast.17, bf16[64,128,256]{2,1,0:T(8,128)(2,1)} %bitcast.21), custom_call_target="tpu_custom_call" | custom-call | flops 3221225472 | bytes 20971520 | tf_op jit(solution)/shard_map/pallas_call | solution.py:73
  190.8 3.8 %convert_element_type.40 = bf16[32,128,256]{2,1,0:T(8,128)(2,1)} convert(f32[32,128,256]{2,1,0:T(8,128)} %shard_map.113) | non-fusion elementwise | flops 1048576 | bytes 6291456 | tf_op jit(solution)/shard_map/convert_element_type | solution.py:279
  194.6 56.0 %shard_map.114 = (bf16[8,512,256]{2,1,0:T(8,128)(2,1)}, f32[257,256]{1,0:T(8,128)}) custom-call(bf16[8,512,256]{2,1,0:T(8,128)(2,1)} %bitcast.19, f32[257,256]{1,0:T(8,128)} %shard_map.112.value_ref), custom_call_target="tpu_custom_call" | custom-call | bytes 4194304 | tf_op jit(solution)/shard_map/pallas_call | solution.py:201
  250.6 1.3 slice_multiply_fusion.1
  251.9 1.7 slice_multiply_fusion
  253.5 2.6 %reduce_sum.35 = bf16[512,256]{1,0:T(8,128)(2,1)} reduce(bf16[8,512,256]{2,1,0:T(8,128)(2,1)} %get-tuple-element.11, bf16[]{:T(256)} %constant.4.clone.1), dimensions={0}, to_apply=%region_2.3 | reduce | flops 917504 | bytes 2359298 | tf_op jit(solution)/shard_map/reduce_sum | solution.py:237
  (3 shorter events, 0.0 us)
Async XLA Ops:
  7.2 119.7 %copy-start = (bf16[256,256]{1,0:T(8,128)(2,1)S(1)}, bf16[256,256]{1,0:T(8,128)(2,1)}, u32[]{:S(2)}) copy-start(bf16[256,256]{1,0:T(8,128)(2,1)} %param.9) | copy-start | bytes 393220
  7.2 11.1 %copy-start.2 = (s32[1,1,384]{2,1,0:T(1,128)S(1)}, s32[1,1,384]{2,1,0:T(1,128)}, u32[]{:S(2)}) copy-start(s32[1,1,384]{2,1,0:T(1,128)} %param.13) | copy-start | bytes 4612
  7.2 11.6 %copy-start.3 = (s32[1,1,384]{2,1,0:T(1,128)S(1)}, s32[1,1,384]{2,1,0:T(1,128)}, u32[]{:S(2)}) copy-start(s32[1,1,384]{2,1,0:T(1,128)} %param.14) | copy-start | bytes 4612
  9.7 36.3 %all-to-all-start = ((bf16[8,512,256]{2,1,0:T(8,128)(2,1)}), bf16[8,512,256]{2,1,0:T(8,128)(2,1)S(1)}, u32[]{:S(2)}, u32[]{:S(2)}) async-start(bf16[8,512,256]{2,1,0:T(8,128)(2,1)} %broadcast_in_dim.4), calls=%async_computation | async-start | bytes 4194304 | tf_op jit(solution)/shard_map/all_to_all | solution.py:224
  17.5 155.1 %all-gather.2.cloned.1.call-start = ((), (), s32[]{:S(2)}) async-start(), calls=%async_computation.2 | async-start | bytes 4456448 | tf_op jit(solution)/shard_map/all_gather | solution.py:270
  46.0 1.4 copy-start.1
  123.9 2.9 %copy-start.4 = (bf16[512,256]{1,0:T(8,128)(2,1)S(1)}, bf16[512,256]{1,0:T(8,128)(2,1)}, u32[]{:S(2)}) copy-start(bf16[512,256]{1,0:T(8,128)(2,1)} %param.11) | copy-start | bytes 786436
  123.9 2.9 %copy-start.5 = (f32[256]{0:T(256)S(1)}, f32[256]{0:T(256)}, u32[]{:S(2)}) copy-start(f32[256]{0:T(256)} %param.10) | copy-start | bytes 3076
Sparse Core Ops, SparseCore 0:
  129.1 43.4 all-gather.1

commit v9 on v7

--- a/solution.py
+++ b/solution.py
@@ -240,13 +240,14 @@
     grad_agg = jnp.dot(grad_pre, weight.T, preferred_element_type=jnp.float32).astype(jnp.bfloat16)
     packed = jnp.concatenate([local_weight, local_bias[None, :]], axis=0)
     grad_panel = lax.all_gather(grad_agg, "col", axis=0, tiled=True)
-    packed = butterfly_sum(packed, (("col", col_count), ("row", row_count)), 1)
+    packed = butterfly_sum(packed, (("col", col_count),), 1)
     grad_panel, packed = lax.optimization_barrier((grad_panel, packed))
     grad_blocks = grad_panel.reshape(blocks_down, block, width)
     partial_back = accumulate(
         tile_set, dest_ids, source_ids, live_count, grad_blocks, blocks_across, True
     )
     term_back = partial_back.reshape(blocks_across * block, width)
+    packed = lax.psum(packed, "row")
     grad_features = scatter_sum(term_back.astype(jnp.bfloat16), "row", row_count, 0).astype(
         jnp.bfloat16
     )

time: 252 us -> 286 us (1.13)
  waiting for transfers between devices: 26.6 us -> 78 us
  Pallas kernels: 115 us -> 97.9 us
    psum x0 -> x1, waiting for transfers between devices: none -> 47.2 us  [per_device(): packed = lax.psum(packed, 'row')]
    pallas_call x1, Pallas kernels: 62.6 us -> 39.1 us  [butterfly_sum(): pl.pallas_call(functools.partial(butterfly_kernel, tuple(steps)), out_sha...]
    pallas_call x1, Pallas kernels: 34.2 us -> 40.7 us  [exchange(): pl.pallas_call(functools.partial(exchange_kernel, axis, size, spread), ou...]
    all_gather x1, waiting for transfers between devices: 0.02 us -> 4.23 us  [per_device(): grad_panel = lax.all_gather(grad_agg, 'col', axis=0, tiled=True)]
  transfers between devices with their start and end apart: 2 -> 3, of which waited for: 1 -> 3; matrix products, arithmetic and copies ran while one was open for 1% -> 3% of each run, Pallas kernels for 25% -> 31%
where the time goes in v9:
time: 286 us; the launch traced here: 285 us
  Pallas kernels  97.9 us (34%)
  waiting for transfers between devices  78 us (27%)
  blocking collectives  61.7 us (22%)
  other arithmetic  18.2 us (6%)
  between operations  14.8 us (5%)
  starting transfers between devices  7.95 us (3%)
  local copies, waits for them, and re-layouts  3.89 us (1%)
    all_to_all x1, blocking collectives, scatter_sum_native(): got = lax.all_to_all(parts, axis, 0, 0, tiled=False)  61.7 us
    psum x1, waiting for transfers between devices, per_device(): packed = lax.psum(packed, 'row')  47.2 us
    pallas_call x1, Pallas kernels, exchange(): pl.pallas_call(functools.partial(exchange_kernel, axis, size, spread), ou...  40.7 us
    pallas_call x1, Pallas kernels, butterfly_sum(): pl.pallas_call(functools.partial(butterfly_kernel, tuple(steps)), out_sha...  39.1 us
    all_to_all x1, waiting for transfers between devices, gather_all(): got = lax.all_to_all(spread, axis, 0, 0, tiled=False)  26.5 us
    pallas_call x2, Pallas kernels, accumulate(): pl.pallas_call(functools.partial(accumulate_kernel, backward), out_shape=...  18.2 us
    all_to_all x1, starting transfers between devices, gather_all(): got = lax.all_to_all(spread, axis, 0, 0, tiled=False)  7.87 us
  transfers between devices with their start and end apart: 3, of which 3 were waited for; matrix products, arithmetic and copies ran while one was open for 3% of the time, Pallas kernels for 31%

profile of v9, /device:TPU:0, one launch (start us, length us, event | category | flops | bytes accessed | tf_op | source)
XLA Modules:
  0.0 284.8 jit_solution(16730312266739191169)
XLA Ops:
  7.2 0.0 copy-start
  7.2 0.0 copy-start.2
  7.2 0.0 copy-start.3
  7.2 2.5 broadcast_in_dim.4
  9.7 7.9 %all-to-all-start = ((bf16[8,512,256]{2,1,0:T(8,128)(2,1)}), bf16[8,512,256]{2,1,0:T(8,128)(2,1)S(1)}, u32[]{:S(2)}, u32[]{:S(2)}) async-start(bf16[8,512,256]{2,1,0:T(8,128)(2,1)} %broadcast_in_dim.4), calls=%async_computation | async-start | bytes 4194304 | tf_op jit(solution)/shard_map/all_to_all | solution.py:196
  17.5 0.0 all-gather.2.cloned.1.call-start
  18.2 0.0 copy-done.2
  18.2 0.6 reduce.2.dest_ref
  18.8 0.0 copy-done.3
  18.8 0.6 reduce.3.source_ref
  19.4 26.5 %all-to-all-done = bf16[8,512,256]{2,1,0:T(8,128)(2,1)S(1)} async-done(((bf16[8,512,256]{2,1,0:T(8,128)(2,1)}), bf16[8,512,256]{2,1,0:T(8,128)(2,1)S(1)}, u32[]{:S(2)}, u32[]{:S(2)}) %all-to-all-start) | async-done | bytes 2097184 | tf_op jit(solution)/shard_map/all_to_all | solution.py:196
  46.0 1.4 copy-done.1
  47.4 9.5 %shard_map.111 = f32[64,128,256]{2,1,0:T(8,128)} custom-call(s32[384]{0:T(512)} %reduce.2.dest_ref, s32[384]{0:T(512)} %reduce.3.source_ref, s32[1]{0:T(128)} %bitcast.14.count_ref, bf16[384,128,128]{2,1,0:T(8,128)(2,1)} %bitcast.16, bf16[32,128,256]{2,1,0:T(8,128)(2,1)} %bitcast.20), custom_call_target="tpu_custom_call" | custom-call | flops 3221225472 | bytes 23068672 | tf_op jit(solution)/shard_map/pallas_call | solution.py:73
  56.9 4.0 %convert_element_type.33 = bf16[64,128,256]{2,1,0:T(8,128)(2,1)S(1)} convert(f32[64,128,256]{2,1,0:T(8,128)} %shard_map.111) | non-fusion elementwise | flops 2097152 | bytes 12582912 | tf_op jit(solution)/shard_map/convert_element_type | solution.py:231
  60.9 61.7 %all_to_all.10 = bf16[16,512,256]{2,1,0:T(8,128)(2,1)} all-to-all(bf16[16,512,256]{2,1,0:T(8,128)(2,1)S(1)} %bitcast.18), channel_id=1, replica_groups=mesh['row'=8,'col'=16] {'col'}, dimensions={0} | all-to-all | bytes 8388608 | tf_op jit(solution)/shard_map/all_to_all | solution.py:202
  122.6 2.9 %reduce_sum.33 = bf16[512,256]{1,0:T(8,128)(2,1)S(1)} reduce(bf16[16,512,256]{2,1,0:T(8,128)(2,1)} %all_to_all.10, bf16[]{:T(256)} %constant.4.clone.1), dimensions={0}, to_apply=%region_0.0 | reduce | flops 1966080 | bytes 4456450 | tf_op jit(solution)/shard_map/reduce_sum | solution.py:203
  125.5 1.1 convert_reduce_fusion
  126.6 1.0 convolution_convert_fusion
  127.6 0.0 all-gather.2.cloned.1.call-update
  127.6 0.0 all-reduce.2.cloned.1.call-start
  127.7 0.3 fusion
  127.9 0.7 pad_maximum_fusion.value_ref
  128.7 39.1 %shard_map.112 = f32[257,256]{1,0:T(8,128)} custom-call(f32[257,256]{1,0:T(8,128)} %pad_maximum_fusion.value_ref), custom_call_target="tpu_custom_call" | custom-call | tf_op jit(solution)/shard_map/pallas_call | solution.py:130
  167.8 4.2 %all-gather.2.cloned.1.call-done = bf16[8192,256]{1,0:T(8,128)(2,1)} async-done(((bf16[512,256]{1,0:T(8,128)(2,1)}), bf16[8192,256]{1,0:T(8,128)(2,1)}) %all-gather.2.cloned.1.call-update) | async-done | bytes 4194320 | tf_op jit(solution)/shard_map/all_gather | solution.py:242
  172.0 0.0 all-reduce.2.cloned.1.call-update
  172.0 8.7 %shard_map.113 = f32[32,128,256]{2,1,0:T(8,128)} custom-call(s32[384]{0:T(512)} %reduce.2.dest_ref, s32[384]{0:T(512)} %reduce.3.source_ref, s32[1]{0:T(128)} %bitcast.15.count_ref, bf16[384,128,128]{2,1,0:T(8,128)(2,1)} %bitcast.17, bf16[64,128,256]{2,1,0:T(8,128)(2,1)} %bitcast.21), custom_call_target="tpu_custom_call" | custom-call | flops 3221225472 | bytes 20971520 | tf_op jit(solution)/shard_map/pallas_call | solution.py:73
  180.7 3.8 %convert_element_type.40 = bf16[32,128,256]{2,1,0:T(8,128)(2,1)} convert(f32[32,128,256]{2,1,0:T(8,128)} %shard_map.113) | non-fusion elementwise | flops 1048576 | bytes 6291456 | tf_op jit(solution)/shard_map/convert_element_type | solution.py:251
  184.5 40.7 %shard_map.114 = bf16[8,512,256]{2,1,0:T(8,128)(2,1)} custom-call(bf16[8,512,256]{2,1,0:T(8,128)(2,1)} %bitcast.19), custom_call_target="tpu_custom_call" | custom-call | bytes 4194304 | tf_op jit(solution)/shard_map/pallas_call | solution.py:179
  225.2 2.7 reduce_sum.35
  227.8 47.2 %all-reduce.2.cloned.1.call-done = f32[257,256]{1,0:T(8,128)} async-done(((f32[257,256]{1,0:T(8,128)}), f32[257,256]{1,0:T(8,128)}) %all-reduce.2.cloned.1.call-update) | async-done | bytes 263184 | tf_op jit(solution)/shard_map/psum | solution.py:250
  275.0 1.3 slice_multiply_fusion.1
  276.3 1.7 slice_multiply_fusion
  (6 shorter events, 0.0 us)
Async XLA Ops:
  7.2 118.3 %copy-start = (bf16[256,256]{1,0:T(8,128)(2,1)S(1)}, bf16[256,256]{1,0:T(8,128)(2,1)}, u32[]{:S(2)}) copy-start(bf16[256,256]{1,0:T(8,128)(2,1)} %param.9) | copy-start | bytes 393220
  7.2 11.1 %copy-start.2 = (s32[1,1,384]{2,1,0:T(1,128)S(1)}, s32[1,1,384]{2,1,0:T(1,128)}, u32[]{:S(2)}) copy-start(s32[1,1,384]{2,1,0:T(1,128)} %param.13) | copy-start | bytes 4612
  7.2 11.6 %copy-start.3 = (s32[1,1,384]{2,1,0:T(1,128)S(1)}, s32[1,1,384]{2,1,0:T(1,128)}, u32[]{:S(2)}) copy-start(s32[1,1,384]{2,1,0:T(1,128)} %param.14) | copy-start | bytes 4612
  9.7 36.3 %all-to-all-start = ((bf16[8,512,256]{2,1,0:T(8,128)(2,1)}), bf16[8,512,256]{2,1,0:T(8,128)(2,1)S(1)}, u32[]{:S(2)}, u32[]{:S(2)}) async-start(bf16[8,512,256]{2,1,0:T(8,128)(2,1)} %broadcast_in_dim.4), calls=%async_computation | async-start | bytes 4194304 | tf_op jit(solution)/shard_map/all_to_all | solution.py:196
  17.5 154.5 %all-gather.2.cloned.1.call-start = ((), (), s32[]{:S(2)}) async-start(), calls=%async_computation.2 | async-start | bytes 4456448 | tf_op jit(solution)/shard_map/all_gather | solution.py:242
  46.0 1.4 copy-start.1
  122.6 2.9 %copy-start.4 = (bf16[512,256]{1,0:T(8,128)(2,1)S(1)}, bf16[512,256]{1,0:T(8,128)(2,1)}, u32[]{:S(2)}) copy-start(bf16[512,256]{1,0:T(8,128)(2,1)} %param.11) | copy-start | bytes 786436
  122.6 2.9 %copy-start.5 = (f32[256]{0:T(256)S(1)}, f32[256]{0:T(256)}, u32[]{:S(2)}) copy-start(f32[256]{0:T(256)} %param.10) | copy-start | bytes 3076
  127.6 147.4 %all-reduce.2.cloned.1.call-start = ((), (), s32[]{:S(2)}) async-start(), calls=%async_computation.3 | async-start | bytes 540672 | tf_op jit(solution)/shard_map/psum | solution.py:250
Sparse Core Ops, SparseCore 0:
  127.7 44.2 all-gather.1
  174.5 100.4 all-reduce.1

commit v10 on v5

--- a/solution.py
+++ b/solution.py
@@ -8,8 +8,8 @@
 from jax.experimental.pallas import tpu as pltpu
 from jax.sharding import PartitionSpec as P
 
-GROUP = 32
-UNROLL = 32
+GROUP = 128
+UNROLL = 128
 
 
 def accumulate_kernel(backward, dest_ref, source_ref, count_ref, tiles_ref, panel_ref, out_ref):

time: 252 us -> 285 us (1.13); the launches traced: 251 us -> 281 us
  Pallas kernels: 23.7 us -> 63.8 us
  starting transfers between devices: 34.3 us -> 14.2 us
  waiting for transfers between devices: 101 us -> 111 us
    pallas_call x2, Pallas kernels: 23.7 us -> 63.8 us  [accumulate(): pl.pallas_call(functools.partial(accumulate_kernel, backward), out_shape=...]
    ppermute x7, starting transfers between devices: 15.6 us -> 2.72 us  [butterfly_sum(): value = value + lax.ppermute(value, axis, pairs)]
    ppermute x7, waiting for transfers between devices: 52 us -> 62.5 us  [butterfly_sum(): value = value + lax.ppermute(value, axis, pairs)]
    all_to_all x1, starting transfers between devices: 10.8 us -> 3.6 us  [scatter_sum(): got = lax.all_to_all(parts, axis, 0, 0, tiled=False)]
where the time goes in v10:
time: 285 us; the launch traced here: 281 us
  waiting for transfers between devices  111 us (39%)
  Pallas kernels  63.8 us (22%)
  blocking collectives  56.3 us (20%)
  between operations  14.9 us (5%)
  other arithmetic  14.4 us (5%)
  starting transfers between devices  14.2 us (5%)
  local copies, waits for them, and re-layouts  3.85 us (1%)
    pallas_call x2, Pallas kernels, accumulate(): pl.pallas_call(functools.partial(accumulate_kernel, backward), out_shape=...  63.8 us
    ppermute x7, waiting for transfers between devices, butterfly_sum(): value = value + lax.ppermute(value, axis, pairs)  62.5 us
    all_to_all x1, blocking collectives, scatter_sum(): got = lax.all_to_all(parts, axis, 0, 0, tiled=False)  56.3 us
    all_to_all x1, waiting for transfers between devices, gather_all(): got = lax.all_to_all(spread, axis, 0, 0, tiled=False)  26.6 us
    all_to_all x1, waiting for transfers between devices, scatter_sum(): got = lax.all_to_all(parts, axis, 0, 0, tiled=False)  22.3 us
    all_to_all x1, starting transfers between devices, gather_all(): got = lax.all_to_all(spread, axis, 0, 0, tiled=False)  7.87 us
  transfers between devices with their start and end apart: 10, of which 9 were waited for; matrix products, arithmetic and copies ran while one was open for 1% of the time, Pallas kernels for 0%

profile of v10, /device:TPU:0, one launch (start us, length us, event | category | flops | bytes accessed | tf_op | source)
XLA Modules:
  0.0 281.2 jit_solution(15064793438624773407)
XLA Ops:
  7.2 2.5 broadcast_in_dim.4
  9.7 7.9 %all-to-all-start = ((bf16[8,512,256]{2,1,0:T(8,128)(2,1)}), bf16[8,512,256]{2,1,0:T(8,128)(2,1)S(1)}, u32[]{:S(2)}, u32[]{:S(2)}) async-start(bf16[8,512,256]{2,1,0:T(8,128)(2,1)} %broadcast_in_dim.4), calls=%async_computation | async-start | bytes 4194304 | tf_op jit(solution)/shard_map/all_to_all | solution.py:106
  18.2 0.6 reduce.2.dest_ref
  18.8 0.6 reduce.3.source_ref
  19.4 26.6 %all-to-all-done = bf16[8,512,256]{2,1,0:T(8,128)(2,1)S(1)} async-done(((bf16[8,512,256]{2,1,0:T(8,128)(2,1)}), bf16[8,512,256]{2,1,0:T(8,128)(2,1)S(1)}, u32[]{:S(2)}, u32[]{:S(2)}) %all-to-all-start) | async-done | bytes 2097184 | tf_op jit(solution)/shard_map/all_to_all | solution.py:106
  46.0 1.4 copy-done.1
  47.3 29.2 %shard_map.111 = f32[64,128,256]{2,1,0:T(8,128)} custom-call(s32[384]{0:T(512)} %reduce.2.dest_ref, s32[384]{0:T(512)} %reduce.3.source_ref, s32[1]{0:T(128)} %bitcast.14.count_ref, bf16[384,128,128]{2,1,0:T(8,128)(2,1)} %bitcast.16, bf16[32,128,256]{2,1,0:T(8,128)(2,1)} %bitcast.19), custom_call_target="tpu_custom_call" | custom-call | flops 3221225472 | bytes 23068672 | tf_op jit(solution)/shard_map/pallas_call | solution.py:73
  76.6 4.0 %convert_element_type.33 = bf16[64,128,256]{2,1,0:T(8,128)(2,1)S(1)} convert(f32[64,128,256]{2,1,0:T(8,128)} %shard_map.111) | non-fusion elementwise | flops 2097152 | bytes 12582912 | tf_op jit(solution)/shard_map/convert_element_type | solution.py:135
  80.6 56.3 %all_to_all.15 = bf16[16,512,256]{2,1,0:T(8,128)(2,1)} all-to-all(bf16[16,512,256]{2,1,0:T(8,128)(2,1)S(1)} %bitcast.18), channel_id=1, replica_groups=mesh['row'=8,'col'=16] {'col'}, dimensions={0} | all-to-all | bytes 8388608 | tf_op jit(solution)/shard_map/all_to_all | solution.py:112
  136.9 2.9 %reduce_sum.33 = bf16[512,256]{1,0:T(8,128)(2,1)S(1)} reduce(bf16[16,512,256]{2,1,0:T(8,128)(2,1)} %all_to_all.15, bf16[]{:T(256)} %constant.4.clone.1), dimensions={0}, to_apply=%region_0.0 | reduce | flops 1966080 | bytes 4456450 | tf_op jit(solution)/shard_map/reduce_sum | solution.py:113
  139.8 1.1 convert_reduce_fusion
  140.9 1.0 convolution_convert_fusion
  141.9 0.3 fusion.1
  142.2 0.1 collective-permute-start
  142.3 1.5 collective-permute-done
  144.0 13.7 %collective-permute-done.1 = f32[257,256]{1,0:T(8,128)S(1)} collective-permute-done((f32[257,256]{1,0:T(8,128)S(1)}, f32[257,256]{1,0:T(8,128)S(1)}, u32[]{:S(2)}, u32[]{:S(2)}) %collective-permute-start.1) | collective-permute-done | bytes 263200 | tf_op jit(solution)/shard_map/ppermute | solution.py:99
  157.7 0.1 collective-permute-start.2
  157.8 15.2 %collective-permute-done.2 = f32[257,256]{1,0:T(8,128)S(1)} collective-permute-done((f32[257,256]{1,0:T(8,128)S(1)}, f32[257,256]{1,0:T(8,128)S(1)}, u32[]{:S(2)}, u32[]{:S(2)}) %collective-permute-start.2) | collective-permute-done | bytes 263200 | tf_op jit(solution)/shard_map/ppermute | solution.py:99
  173.0 0.1 collective-permute-start.3
  173.1 10.6 %collective-permute-done.3 = f32[257,256]{1,0:T(8,128)S(1)} collective-permute-done((f32[257,256]{1,0:T(8,128)S(1)}, f32[257,256]{1,0:T(8,128)S(1)}, u32[]{:S(2)}, u32[]{:S(2)}) %collective-permute-start.3) | collective-permute-done | bytes 263200 | tf_op jit(solution)/shard_map/ppermute | solution.py:99
  183.7 0.1 collective-permute-start.4
  183.8 7.7 %collective-permute-done.4 = f32[257,256]{1,0:T(8,128)S(1)} collective-permute-done((f32[257,256]{1,0:T(8,128)S(1)}, f32[257,256]{1,0:T(8,128)S(1)}, u32[]{:S(2)}, u32[]{:S(2)}) %collective-permute-start.4) | collective-permute-done | bytes 263200 | tf_op jit(solution)/shard_map/ppermute | solution.py:99
  191.7 8.0 %collective-permute-done.5 = f32[257,256]{1,0:T(8,128)S(1)} collective-permute-done((f32[257,256]{1,0:T(8,128)S(1)}, f32[257,256]{1,0:T(8,128)S(1)}, u32[]{:S(2)}, u32[]{:S(2)}) %collective-permute-start.5) | collective-permute-done | bytes 263200 | tf_op jit(solution)/shard_map/ppermute | solution.py:99
  199.6 2.2 collective-permute-start.6
  201.9 5.8 %collective-permute-done.6 = f32[257,256]{1,0:T(8,128)S(1)} collective-permute-done((f32[257,256]{1,0:T(8,128)S(1)}, f32[257,256]{1,0:T(8,128)S(1)}, u32[]{:S(2)}, u32[]{:S(2)}) %collective-permute-start.6) | collective-permute-done | bytes 263200 | tf_op jit(solution)/shard_map/ppermute | solution.py:99
  207.8 34.5 %shard_map.112 = f32[32,128,256]{2,1,0:T(8,128)} custom-call(s32[384]{0:T(512)} %reduce.2.dest_ref, s32[384]{0:T(512)} %reduce.3.source_ref, s32[1]{0:T(128)} %bitcast.15.count_ref, bf16[384,128,128]{2,1,0:T(8,128)(2,1)} %bitcast.17, bf16[64,128,256]{2,1,0:T(8,128)(2,1)} %bitcast.20), custom_call_target="tpu_custom_call" | custom-call | flops 3221225472 | bytes 20971520 | tf_op jit(solution)/shard_map/pallas_call | solution.py:73
  242.3 3.8 %convert_element_type.40 = bf16[32,128,256]{2,1,0:T(8,128)(2,1)} convert(f32[32,128,256]{2,1,0:T(8,128)} %shard_map.112) | non-fusion elementwise | flops 1048576 | bytes 6291456 | tf_op jit(solution)/shard_map/convert_element_type | solution.py:154
  246.1 3.6 %all-to-all-start.2 = ((bf16[8,512,256]{2,1,0:T(8,128)(2,1)}), bf16[8,512,256]{2,1,0:T(8,128)(2,1)S(1)}, u32[]{:S(2)}, u32[]{:S(2)}) async-start(bf16[8,512,256]{2,1,0:T(8,128)(2,1)} %bitcast.7), calls=%async_computation.2 | async-start | bytes 4194304 | tf_op jit(solution)/shard_map/all_to_all | solution.py:112
  249.7 0.6 slice_multiply_fusion.1
  250.3 0.7 slice_multiply_fusion
  251.0 22.3 %all-to-all-done.2 = bf16[8,512,256]{2,1,0:T(8,128)(2,1)S(1)} async-done(((bf16[8,512,256]{2,1,0:T(8,128)(2,1)}), bf16[8,512,256]{2,1,0:T(8,128)(2,1)S(1)}, u32[]{:S(2)}, u32[]{:S(2)}) %all-to-all-start.2) | async-done | bytes 2097184 | tf_op jit(solution)/shard_map/all_to_all | solution.py:112
  273.3 1.0 reduce_sum.35
  (24 shorter events, 0.5 us)
Async XLA Ops:
  7.2 132.6 %copy-start = (bf16[256,256]{1,0:T(8,128)(2,1)S(1)}, bf16[256,256]{1,0:T(8,128)(2,1)}, u32[]{:S(2)}) copy-start(bf16[256,256]{1,0:T(8,128)(2,1)} %param.9) | copy-start | bytes 393220
  7.2 11.1 %copy-start.2 = (s32[1,1,384]{2,1,0:T(1,128)S(1)}, s32[1,1,384]{2,1,0:T(1,128)}, u32[]{:S(2)}) copy-start(s32[1,1,384]{2,1,0:T(1,128)} %param.13) | copy-start | bytes 4612
  7.2 11.6 %copy-start.3 = (s32[1,1,384]{2,1,0:T(1,128)S(1)}, s32[1,1,384]{2,1,0:T(1,128)}, u32[]{:S(2)}) copy-start(s32[1,1,384]{2,1,0:T(1,128)} %param.14) | copy-start | bytes 4612
  9.7 36.3 %all-to-all-start = ((bf16[8,512,256]{2,1,0:T(8,128)(2,1)}), bf16[8,512,256]{2,1,0:T(8,128)(2,1)S(1)}, u32[]{:S(2)}, u32[]{:S(2)}) async-start(bf16[8,512,256]{2,1,0:T(8,128)(2,1)} %broadcast_in_dim.4), calls=%async_computation | async-start | bytes 4194304 | tf_op jit(solution)/shard_map/all_to_all | solution.py:106
  17.5 190.2 %all-gather.2.cloned.1.call-start = ((), (), s32[]{:S(2)}) async-start(), calls=%async_computation.3 | async-start | bytes 4456448 | tf_op jit(solution)/shard_map/all_gather | solution.py:146
  46.0 1.4 copy-start.1
  136.9 2.9 %copy-start.4 = (bf16[512,256]{1,0:T(8,128)(2,1)S(1)}, bf16[512,256]{1,0:T(8,128)(2,1)}, u32[]{:S(2)}) copy-start(bf16[512,256]{1,0:T(8,128)(2,1)} %param.11) | copy-start | bytes 786436
  136.9 2.9 %copy-start.5 = (f32[256]{0:T(256)S(1)}, f32[256]{0:T(256)}, u32[]{:S(2)}) copy-start(f32[256]{0:T(256)} %param.10) | copy-start | bytes 3076
  142.2 1.6 collective-permute-start
  143.9 13.8 %collective-permute-start.1 = (f32[257,256]{1,0:T(8,128)S(1)}, f32[257,256]{1,0:T(8,128)S(1)}, u32[]{:S(2)}, u32[]{:S(2)}) collective-permute-start(f32[257,256]{1,0:T(8,128)S(1)} %fusion), channel_id=1, source_target_pairs={{0,2},{1,3},{2,0},{3,1},{4,6},{5,7},{6,4},{7,5},{8,10},{9,11},{10,... | collective-permute-start | bytes 789512 | tf_op jit(solution)/shard_map/ppermute | solution.py:99
  157.7 15.3 %collective-permute-start.2 = (f32[257,256]{1,0:T(8,128)S(1)}, f32[257,256]{1,0:T(8,128)S(1)}, u32[]{:S(2)}, u32[]{:S(2)}) collective-permute-start(f32[257,256]{1,0:T(8,128)S(1)} %add.42), channel_id=1, source_target_pairs={{0,4},{1,5},{2,6},{3,7},{4,0},{5,1},{6,2},{7,3},{8,12},{9,13},{10,... | collective-permute-start | bytes 789512 | tf_op jit(solution)/shard_map/ppermute | solution.py:99
  173.0 10.7 %collective-permute-start.3 = (f32[257,256]{1,0:T(8,128)S(1)}, f32[257,256]{1,0:T(8,128)S(1)}, u32[]{:S(2)}, u32[]{:S(2)}) collective-permute-start(f32[257,256]{1,0:T(8,128)S(1)} %add.43), channel_id=1, source_target_pairs={{0,8},{1,9},{2,10},{3,11},{4,12},{5,13},{6,14},{7,15},{8,0},{9,1},... | collective-permute-start | bytes 789512 | tf_op jit(solution)/shard_map/ppermute | solution.py:99
  183.7 7.8 %collective-permute-start.4 = (f32[257,256]{1,0:T(8,128)S(1)}, f32[257,256]{1,0:T(8,128)S(1)}, u32[]{:S(2)}, u32[]{:S(2)}) collective-permute-start(f32[257,256]{1,0:T(8,128)S(1)} %add.44), channel_id=1, source_target_pairs={{0,16},{16,0},{32,48},{48,32},{64,80},{80,64},{96,112},{112,96},{1... | collective-permute-start | bytes 789512 | tf_op jit(solution)/shard_map/ppermute | solution.py:99
  191.6 8.0 %collective-permute-start.5 = (f32[257,256]{1,0:T(8,128)S(1)}, f32[257,256]{1,0:T(8,128)S(1)}, u32[]{:S(2)}, u32[]{:S(2)}) collective-permute-start(f32[257,256]{1,0:T(8,128)S(1)} %add.45), channel_id=1, source_target_pairs={{0,32},{16,48},{32,0},{48,16},{64,96},{80,112},{96,64},{112,80},{1... | collective-permute-start | bytes 789512 | tf_op jit(solution)/shard_map/ppermute | solution.py:99
  199.6 8.0 %collective-permute-start.6 = (f32[257,256]{1,0:T(8,128)S(1)}, f32[257,256]{1,0:T(8,128)S(1)}, u32[]{:S(2)}, u32[]{:S(2)}) collective-permute-start(f32[257,256]{1,0:T(8,128)S(1)} %add.46), channel_id=1, source_target_pairs={{0,64},{16,80},{32,96},{48,112},{64,0},{80,16},{96,32},{112,48},{1... | collective-permute-start | bytes 789512 | tf_op jit(solution)/shard_map/ppermute | solution.py:99
  246.1 27.2 %all-to-all-start.2 = ((bf16[8,512,256]{2,1,0:T(8,128)(2,1)}), bf16[8,512,256]{2,1,0:T(8,128)(2,1)S(1)}, u32[]{:S(2)}, u32[]{:S(2)}) async-start(bf16[8,512,256]{2,1,0:T(8,128)(2,1)} %bitcast.7), calls=%async_computation.2 | async-start | bytes 4194304 | tf_op jit(solution)/shard_map/all_to_all | solution.py:112
Sparse Core Ops, SparseCore 0:
  142.0 41.7 all-gather.1

commit v11 on v10

--- a/solution.py
+++ b/solution.py
@@ -8,8 +8,8 @@
 from jax.experimental.pallas import tpu as pltpu
 from jax.sharding import PartitionSpec as P
 
-GROUP = 128
-UNROLL = 128
+GROUP = 64
+UNROLL = 64
 
 
 def accumulate_kernel(backward, dest_ref, source_ref, count_ref, tiles_ref, panel_ref, out_ref):
@@ -27,21 +27,20 @@
 
     def one_tile(i, checked):
         slot = base + i
+        tile = tiles_ref[i]
+        if checked:
+            tile = jnp.where(slot < live_count, tile, jnp.zeros_like(tile))
         if backward:
             fetch = jnp.clip(dest_ref[slot], 0, in_blocks - 1)
             target = jnp.clip(source_ref[slot], 0, out_blocks - 1)
             contrib = lax.dot_general(
-                tiles_ref[i], panel_ref[fetch], (((0,), (0,)), ((), ())),
+                tile, panel_ref[fetch], (((0,), (0,)), ((), ())),
                 preferred_element_type=jnp.float32,
             )
         else:
             fetch = jnp.clip(source_ref[slot], 0, in_blocks - 1)
             target = jnp.clip(dest_ref[slot], 0, out_blocks - 1)
-            contrib = jnp.dot(
-                tiles_ref[i], panel_ref[fetch], preferred_element_type=jnp.float32
-            )
-        if checked:
-            contrib = jnp.where(slot < live_count, contrib, 0.0)
+            contrib = jnp.dot(tile, panel_ref[fetch], preferred_element_type=jnp.float32)
         out_ref[target] += contrib
 
     @pl.when(base + group <= live_count)
@@ -52,7 +51,7 @@
 
     @pl.when((base < live_count) & (base + group > live_count))
     def _():
-        @pl.loop(0, group)
+        @pl.loop(0, group, unroll=UNROLL)
         def _(i):
             one_tile(i, True)
 

time: 285 us -> 243 us (0.85); the launches traced: 281 us -> 243 us
  Pallas kernels: 63.8 us -> 18.1 us
  starting transfers between devices: 14.2 us -> 23.5 us
  waiting for transfers between devices: 111 us -> 106 us
  blocking collectives: 56.3 us -> 59.9 us
    pallas_call x2, Pallas kernels: 63.8 us -> 18.1 us  [accumulate(): pl.pallas_call(functools.partial(accumulate_kernel, backward), out_shape=...]
    all_to_all x1, starting transfers between devices: 3.6 us -> 9.02 us  [scatter_sum(): got = lax.all_to_all(parts, axis, 0, 0, tiled=False)]
    ppermute x7, waiting for transfers between devices: 62.5 us -> 58.2 us  [butterfly_sum(): value = value + lax.ppermute(value, axis, pairs)]
    ppermute x7, starting transfers between devices: 2.72 us -> 6.63 us  [butterfly_sum(): value = value + lax.ppermute(value, axis, pairs)]
    all_to_all x1, blocking collectives: 56.3 us -> 59.9 us  [scatter_sum(): got = lax.all_to_all(parts, axis, 0, 0, tiled=False)]
where the time goes in v11:
time: 243 us
  waiting for transfers between devices  106 us (44%)
  blocking collectives  59.9 us (25%)
  starting transfers between devices  23.5 us (10%)
  Pallas kernels  18.1 us (7%)
  between operations  14.8 us (6%)
  other arithmetic  14.4 us (6%)
  local copies, waits for them, and re-layouts  3.85 us (2%)
    all_to_all x1, blocking collectives, scatter_sum(): got = lax.all_to_all(parts, axis, 0, 0, tiled=False)  59.9 us
    ppermute x7, waiting for transfers between devices, butterfly_sum(): value = value + lax.ppermute(value, axis, pairs)  58.2 us
    all_to_all x1, waiting for transfers between devices, gather_all(): got = lax.all_to_all(spread, axis, 0, 0, tiled=False)  26.6 us
    all_to_all x1, waiting for transfers between devices, scatter_sum(): got = lax.all_to_all(parts, axis, 0, 0, tiled=False)  20.8 us
    pallas_call x2, Pallas kernels, accumulate(): pl.pallas_call(functools.partial(accumulate_kernel, backward), out_shape=...  18.1 us
    all_to_all x1, starting transfers between devices, scatter_sum(): got = lax.all_to_all(parts, axis, 0, 0, tiled=False)  9.02 us
    all_to_all x1, starting transfers between devices, gather_all(): got = lax.all_to_all(spread, axis, 0, 0, tiled=False)  7.87 us
    ppermute x7, starting transfers between devices, butterfly_sum(): value = value + lax.ppermute(value, axis, pairs)  6.63 us
  transfers between devices with their start and end apart: 10, of which 9 were waited for; matrix products, arithmetic and copies ran while one was open for 1% of the time, Pallas kernels for 0%

profile of v11, /device:TPU:0, one launch (start us, length us, event | category | flops | bytes accessed | tf_op | source)
XLA Modules:
  0.0 242.7 jit_solution(7393928342962568728)
XLA Ops:
  7.2 2.5 %broadcast_in_dim.4 = bf16[8,512,256]{2,1,0:T(8,128)(2,1)} broadcast(bf16[512,256]{1,0:T(8,128)(2,1)} %param.8), dimensions={1,2} | broadcast | bytes 2359296 | tf_op jit(solution)/shard_map/broadcast_in_dim | solution.py:104
  9.7 7.9 %all-to-all-start = ((bf16[8,512,256]{2,1,0:T(8,128)(2,1)}), bf16[8,512,256]{2,1,0:T(8,128)(2,1)S(1)}, u32[]{:S(2)}, u32[]{:S(2)}) async-start(bf16[8,512,256]{2,1,0:T(8,128)(2,1)} %broadcast_in_dim.4), calls=%async_computation | async-start | bytes 4194304 | tf_op jit(solution)/shard_map/all_to_all | solution.py:105
  18.2 0.6 reduce.2.dest_ref
  18.8 0.6 reduce.3.source_ref
  19.4 26.6 %all-to-all-done = bf16[8,512,256]{2,1,0:T(8,128)(2,1)S(1)} async-done(((bf16[8,512,256]{2,1,0:T(8,128)(2,1)}), bf16[8,512,256]{2,1,0:T(8,128)(2,1)S(1)}, u32[]{:S(2)}, u32[]{:S(2)}) %all-to-all-start) | async-done | bytes 2097184 | tf_op jit(solution)/shard_map/all_to_all | solution.py:105
  46.0 1.4 copy-done.1
  47.3 9.5 %shard_map.111 = f32[64,128,256]{2,1,0:T(8,128)} custom-call(s32[384]{0:T(512)} %reduce.2.dest_ref, s32[384]{0:T(512)} %reduce.3.source_ref, s32[1]{0:T(128)} %bitcast.14.count_ref, bf16[384,128,128]{2,1,0:T(8,128)(2,1)} %bitcast.16, bf16[32,128,256]{2,1,0:T(8,128)(2,1)} %bitcast.19), custom_call_target="tpu_custom_call" | custom-call | flops 3221225472 | bytes 23068672 | tf_op jit(solution)/shard_map/pallas_call | solution.py:72
  56.8 4.0 %convert_element_type.33 = bf16[64,128,256]{2,1,0:T(8,128)(2,1)S(1)} convert(f32[64,128,256]{2,1,0:T(8,128)} %shard_map.111) | non-fusion elementwise | flops 2097152 | bytes 12582912 | tf_op jit(solution)/shard_map/convert_element_type | solution.py:134
  60.8 59.9 %all_to_all.15 = bf16[16,512,256]{2,1,0:T(8,128)(2,1)} all-to-all(bf16[16,512,256]{2,1,0:T(8,128)(2,1)S(1)} %bitcast.18), channel_id=1, replica_groups=mesh['row'=8,'col'=16] {'col'}, dimensions={0} | all-to-all | bytes 8388608 | tf_op jit(solution)/shard_map/all_to_all | solution.py:111
  120.7 2.9 %reduce_sum.33 = bf16[512,256]{1,0:T(8,128)(2,1)S(1)} reduce(bf16[16,512,256]{2,1,0:T(8,128)(2,1)} %all_to_all.15, bf16[]{:T(256)} %constant.4.clone.1), dimensions={0}, to_apply=%region_0.0 | reduce | flops 1966080 | bytes 4456450 | tf_op jit(solution)/shard_map/reduce_sum | solution.py:112
  123.6 1.1 convert_reduce_fusion
  124.8 1.0 convolution_convert_fusion
  125.7 0.3 fusion.1
  126.1 0.1 collective-permute-start
  126.1 1.5 collective-permute-done
  127.8 10.9 %collective-permute-done.1 = f32[257,256]{1,0:T(8,128)S(1)} collective-permute-done((f32[257,256]{1,0:T(8,128)S(1)}, f32[257,256]{1,0:T(8,128)S(1)}, u32[]{:S(2)}, u32[]{:S(2)}) %collective-permute-start.1) | collective-permute-done | bytes 263200 | tf_op jit(solution)/shard_map/ppermute | solution.py:98
  138.8 15.3 %collective-permute-done.2 = f32[257,256]{1,0:T(8,128)S(1)} collective-permute-done((f32[257,256]{1,0:T(8,128)S(1)}, f32[257,256]{1,0:T(8,128)S(1)}, u32[]{:S(2)}, u32[]{:S(2)}) %collective-permute-start.2) | collective-permute-done | bytes 263200 | tf_op jit(solution)/shard_map/ppermute | solution.py:98
  154.2 0.1 collective-permute-start.3
  154.3 13.3 %collective-permute-done.3 = f32[257,256]{1,0:T(8,128)S(1)} collective-permute-done((f32[257,256]{1,0:T(8,128)S(1)}, f32[257,256]{1,0:T(8,128)S(1)}, u32[]{:S(2)}, u32[]{:S(2)}) %collective-permute-start.3) | collective-permute-done | bytes 263200 | tf_op jit(solution)/shard_map/ppermute | solution.py:98
  167.6 0.1 collective-permute-start.4
  167.7 6.7 %collective-permute-done.4 = f32[257,256]{1,0:T(8,128)S(1)} collective-permute-done((f32[257,256]{1,0:T(8,128)S(1)}, f32[257,256]{1,0:T(8,128)S(1)}, u32[]{:S(2)}, u32[]{:S(2)}) %collective-permute-start.4) | collective-permute-done | bytes 263200 | tf_op jit(solution)/shard_map/ppermute | solution.py:98
  174.4 4.2 %collective-permute-start.5 = (f32[257,256]{1,0:T(8,128)S(1)}, f32[257,256]{1,0:T(8,128)S(1)}, u32[]{:S(2)}, u32[]{:S(2)}) collective-permute-start(f32[257,256]{1,0:T(8,128)S(1)} %add.45), channel_id=1, source_target_pairs={{0,32},{16,48},{32,0},{48,16},{64,96},{80,112},{96,64},{112,80},{1... | collective-permute-start | bytes 789512 | tf_op jit(solution)/shard_map/ppermute | solution.py:98
  178.6 4.4 %collective-permute-done.5 = f32[257,256]{1,0:T(8,128)S(1)} collective-permute-done((f32[257,256]{1,0:T(8,128)S(1)}, f32[257,256]{1,0:T(8,128)S(1)}, u32[]{:S(2)}, u32[]{:S(2)}) %collective-permute-start.5) | collective-permute-done | bytes 263200 | tf_op jit(solution)/shard_map/ppermute | solution.py:98
  183.1 2.0 collective-permute-start.6
  185.1 6.1 %collective-permute-done.6 = f32[257,256]{1,0:T(8,128)S(1)} collective-permute-done((f32[257,256]{1,0:T(8,128)S(1)}, f32[257,256]{1,0:T(8,128)S(1)}, u32[]{:S(2)}, u32[]{:S(2)}) %collective-permute-start.6) | collective-permute-done | bytes 263200 | tf_op jit(solution)/shard_map/ppermute | solution.py:98
  191.2 8.6 %shard_map.112 = f32[32,128,256]{2,1,0:T(8,128)} custom-call(s32[384]{0:T(512)} %reduce.2.dest_ref, s32[384]{0:T(512)} %reduce.3.source_ref, s32[1]{0:T(128)} %bitcast.15.count_ref, bf16[384,128,128]{2,1,0:T(8,128)(2,1)} %bitcast.17, bf16[64,128,256]{2,1,0:T(8,128)(2,1)} %bitcast.20), custom_call_target="tpu_custom_call" | custom-call | flops 3221225472 | bytes 20971520 | tf_op jit(solution)/shard_map/pallas_call | solution.py:72
  199.9 3.8 %convert_element_type.40 = bf16[32,128,256]{2,1,0:T(8,128)(2,1)} convert(f32[32,128,256]{2,1,0:T(8,128)} %shard_map.112) | non-fusion elementwise | flops 1048576 | bytes 6291456 | tf_op jit(solution)/shard_map/convert_element_type | solution.py:153
  203.7 9.0 %all-to-all-start.2 = ((bf16[8,512,256]{2,1,0:T(8,128)(2,1)}), bf16[8,512,256]{2,1,0:T(8,128)(2,1)S(1)}, u32[]{:S(2)}, u32[]{:S(2)}) async-start(bf16[8,512,256]{2,1,0:T(8,128)(2,1)} %bitcast.7), calls=%async_computation.2 | async-start | bytes 4194304 | tf_op jit(solution)/shard_map/all_to_all | solution.py:111
  212.7 0.6 slice_multiply_fusion.1
  213.2 0.7 slice_multiply_fusion
  214.0 20.8 %all-to-all-done.2 = bf16[8,512,256]{2,1,0:T(8,128)(2,1)S(1)} async-done(((bf16[8,512,256]{2,1,0:T(8,128)(2,1)}), bf16[8,512,256]{2,1,0:T(8,128)(2,1)S(1)}, u32[]{:S(2)}, u32[]{:S(2)}) %all-to-all-start.2) | async-done | bytes 2097184 | tf_op jit(solution)/shard_map/all_to_all | solution.py:111
  234.8 1.0 reduce_sum.35
  (24 shorter events, 0.5 us)
Async XLA Ops:
  7.2 116.4 %copy-start = (bf16[256,256]{1,0:T(8,128)(2,1)S(1)}, bf16[256,256]{1,0:T(8,128)(2,1)}, u32[]{:S(2)}) copy-start(bf16[256,256]{1,0:T(8,128)(2,1)} %param.9) | copy-start | bytes 393220
  7.2 11.1 %copy-start.2 = (s32[1,1,384]{2,1,0:T(1,128)S(1)}, s32[1,1,384]{2,1,0:T(1,128)}, u32[]{:S(2)}) copy-start(s32[1,1,384]{2,1,0:T(1,128)} %param.13) | copy-start | bytes 4612
  7.2 11.6 %copy-start.3 = (s32[1,1,384]{2,1,0:T(1,128)S(1)}, s32[1,1,384]{2,1,0:T(1,128)}, u32[]{:S(2)}) copy-start(s32[1,1,384]{2,1,0:T(1,128)} %param.14) | copy-start | bytes 4612
  9.7 36.3 %all-to-all-start = ((bf16[8,512,256]{2,1,0:T(8,128)(2,1)}), bf16[8,512,256]{2,1,0:T(8,128)(2,1)S(1)}, u32[]{:S(2)}, u32[]{:S(2)}) async-start(bf16[8,512,256]{2,1,0:T(8,128)(2,1)} %broadcast_in_dim.4), calls=%async_computation | async-start | bytes 4194304 | tf_op jit(solution)/shard_map/all_to_all | solution.py:105
  17.5 173.7 %all-gather.2.cloned.1.call-start = ((), (), s32[]{:S(2)}) async-start(), calls=%async_computation.3 | async-start | bytes 4456448 | tf_op jit(solution)/shard_map/all_gather | solution.py:145
  46.0 1.4 copy-start.1
  120.7 2.9 %copy-start.4 = (bf16[512,256]{1,0:T(8,128)(2,1)S(1)}, bf16[512,256]{1,0:T(8,128)(2,1)}, u32[]{:S(2)}) copy-start(bf16[512,256]{1,0:T(8,128)(2,1)} %param.11) | copy-start | bytes 786436
  120.7 2.9 %copy-start.5 = (f32[256]{0:T(256)S(1)}, f32[256]{0:T(256)}, u32[]{:S(2)}) copy-start(f32[256]{0:T(256)} %param.10) | copy-start | bytes 3076
  126.1 1.6 collective-permute-start
  127.7 10.9 %collective-permute-start.1 = (f32[257,256]{1,0:T(8,128)S(1)}, f32[257,256]{1,0:T(8,128)S(1)}, u32[]{:S(2)}, u32[]{:S(2)}) collective-permute-start(f32[257,256]{1,0:T(8,128)S(1)} %fusion), channel_id=1, source_target_pairs={{0,2},{1,3},{2,0},{3,1},{4,6},{5,7},{6,4},{7,5},{8,10},{9,11},{10,... | collective-permute-start | bytes 789512 | tf_op jit(solution)/shard_map/ppermute | solution.py:98
  138.7 15.4 %collective-permute-start.2 = (f32[257,256]{1,0:T(8,128)S(1)}, f32[257,256]{1,0:T(8,128)S(1)}, u32[]{:S(2)}, u32[]{:S(2)}) collective-permute-start(f32[257,256]{1,0:T(8,128)S(1)} %add.42), channel_id=1, source_target_pairs={{0,4},{1,5},{2,6},{3,7},{4,0},{5,1},{6,2},{7,3},{8,12},{9,13},{10,... | collective-permute-start | bytes 789512 | tf_op jit(solution)/shard_map/ppermute | solution.py:98
  154.2 13.4 %collective-permute-start.3 = (f32[257,256]{1,0:T(8,128)S(1)}, f32[257,256]{1,0:T(8,128)S(1)}, u32[]{:S(2)}, u32[]{:S(2)}) collective-permute-start(f32[257,256]{1,0:T(8,128)S(1)} %add.43), channel_id=1, source_target_pairs={{0,8},{1,9},{2,10},{3,11},{4,12},{5,13},{6,14},{7,15},{8,0},{9,1},... | collective-permute-start | bytes 789512 | tf_op jit(solution)/shard_map/ppermute | solution.py:98
  167.6 6.8 %collective-permute-start.4 = (f32[257,256]{1,0:T(8,128)S(1)}, f32[257,256]{1,0:T(8,128)S(1)}, u32[]{:S(2)}, u32[]{:S(2)}) collective-permute-start(f32[257,256]{1,0:T(8,128)S(1)} %add.44), channel_id=1, source_target_pairs={{0,16},{16,0},{32,48},{48,32},{64,80},{80,64},{96,112},{112,96},{1... | collective-permute-start | bytes 789512 | tf_op jit(solution)/shard_map/ppermute | solution.py:98
  174.4 8.7 %collective-permute-start.5 = (f32[257,256]{1,0:T(8,128)S(1)}, f32[257,256]{1,0:T(8,128)S(1)}, u32[]{:S(2)}, u32[]{:S(2)}) collective-permute-start(f32[257,256]{1,0:T(8,128)S(1)} %add.45), channel_id=1, source_target_pairs={{0,32},{16,48},{32,0},{48,16},{64,96},{80,112},{96,64},{112,80},{1... | collective-permute-start | bytes 789512 | tf_op jit(solution)/shard_map/ppermute | solution.py:98
  183.1 8.0 %collective-permute-start.6 = (f32[257,256]{1,0:T(8,128)S(1)}, f32[257,256]{1,0:T(8,128)S(1)}, u32[]{:S(2)}, u32[]{:S(2)}) collective-permute-start(f32[257,256]{1,0:T(8,128)S(1)} %add.46), channel_id=1, source_target_pairs={{0,64},{16,80},{32,96},{48,112},{64,0},{80,16},{96,32},{112,48},{1... | collective-permute-start | bytes 789512 | tf_op jit(solution)/shard_map/ppermute | solution.py:98
  203.7 31.1 %all-to-all-start.2 = ((bf16[8,512,256]{2,1,0:T(8,128)(2,1)}), bf16[8,512,256]{2,1,0:T(8,128)(2,1)S(1)}, u32[]{:S(2)}, u32[]{:S(2)}) async-start(bf16[8,512,256]{2,1,0:T(8,128)(2,1)} %bitcast.7), calls=%async_computation.2 | async-start | bytes 4194304 | tf_op jit(solution)/shard_map/all_to_all | solution.py:111
Sparse Core Ops, SparseCore 0:
  125.9 43.3 all-gather.1

commit v12 on v11

--- a/solution.py
+++ b/solution.py
@@ -90,14 +90,56 @@
     )(dest_ids, source_ids, live_count.reshape(1), tiles, source_blocks)
 
 
-def butterfly_sum(value, axis):
-    size = lax.axis_size(axis)
-    distance = 1
-    while distance < size:
-        pairs = [(i, i ^ distance) for i in range(size)]
-        value = value + lax.ppermute(value, axis, pairs)
-        distance *= 2
-    return value
+def butterfly_kernel(steps, value_ref, out_ref, outgoing, slots, send_sems, recv_sems):
+    partners = []
+    for axis, distance in steps:
+        me = lax.axis_index(axis)
+        bit = (me // distance) % 2
+        partners.append((axis, me + distance - 2 * distance * bit))
+    barrier = pltpu.get_barrier_semaphore()
+    for axis, partner in partners:
+        pl.semaphore_signal(
+            barrier, 1, device_id={axis: partner}, device_id_type=pl.DeviceIdType.MESH
+        )
+    pl.semaphore_wait(barrier, len(partners))
+    out_ref[...] = value_ref[...]
+    for index, (axis, partner) in enumerate(partners):
+        outgoing[...] = out_ref[...].astype(outgoing.dtype)
+        copy = pltpu.make_async_remote_copy(
+            src_ref=outgoing,
+            dst_ref=slots.at[index],
+            send_sem=send_sems.at[index],
+            recv_sem=recv_sems.at[index],
+            device_id={axis: partner},
+            device_id_type=pl.DeviceIdType.MESH,
+        )
+        copy.start()
+        copy.wait_send()
+        copy.wait_recv()
+        out_ref[...] = outgoing[...].astype(jnp.float32) + slots[index].astype(jnp.float32)
+
+
+def butterfly_sum(value, axes, tag):
+    steps = []
+    for axis, size in axes:
+        distance = 1
+        while distance < size:
+            steps.append((axis, distance))
+            distance *= 2
+    count = len(steps)
+    return pl.pallas_call(
+        functools.partial(butterfly_kernel, tuple(steps)),
+        out_shape=jax.ShapeDtypeStruct(value.shape, value.dtype),
+        in_specs=[pl.BlockSpec(memory_space=pltpu.VMEM)],
+        out_specs=pl.BlockSpec(memory_space=pltpu.VMEM),
+        scratch_shapes=[
+            pltpu.VMEM(value.shape, jnp.bfloat16),
+            pltpu.VMEM((count,) + value.shape, jnp.bfloat16),
+            pltpu.SemaphoreType.DMA((count,)),
+            pltpu.SemaphoreType.DMA((count,)),
+        ],
+        compiler_params=pltpu.CompilerParams(collective_id=tag, has_side_effects=True),
+    )(value)
 
 
 def gather_all(value, axis, size):
@@ -143,7 +185,7 @@
     grad_agg = jnp.dot(grad_pre, weight.T, preferred_element_type=jnp.float32).astype(jnp.bfloat16)
     packed = jnp.concatenate([local_weight, local_bias[None, :]], axis=0)
     grad_panel = lax.all_gather(grad_agg, "col", axis=0, tiled=True)
-    packed = butterfly_sum(butterfly_sum(packed, "col"), "row")
+    packed = butterfly_sum(packed, (("col", col_count), ("row", row_count)), 1)
     grad_panel, packed = lax.optimization_barrier((grad_panel, packed))
     grad_blocks = grad_panel.reshape(blocks_down, block, width)
     partial_back = accumulate(

time: 243 us -> 226 us (0.930)
  waiting for transfers between devices: 106 us -> 54.3 us
  Pallas kernels: 18.1 us -> 58.9 us
  starting transfers between devices: 23.5 us -> 15.3 us
    ppermute x7 -> x0, waiting for transfers between devices: 58.2 us -> none  [butterfly_sum(): value = value + lax.ppermute(value, axis, pairs)]
    pallas_call x0 -> x1, Pallas kernels: none -> 43.3 us  [butterfly_sum(): pl.pallas_call(functools.partial(butterfly_kernel, tuple(steps)), out_sha...]
    all_to_all x1, waiting for transfers between devices: 20.8 us -> 27.7 us  [scatter_sum(): got = lax.all_to_all(parts, axis, 0, 0, tiled=False)]
    ppermute x7 -> x0, starting transfers between devices: 6.63 us -> none  [butterfly_sum(): value = value + lax.ppermute(value, axis, pairs)]
    pallas_call x2, Pallas kernels: 18.1 us -> 15.6 us  [accumulate(): pl.pallas_call(functools.partial(accumulate_kernel, backward), out_shape=...]
  transfers between devices with their start and end apart: 10 -> 3, of which waited for: 9 -> 2; matrix products, arithmetic and copies ran while one was open for 1% -> 2% of each run, Pallas kernels for 0% -> 19%
where the time goes in v12:
time: 226 us; the launch traced here: 224 us
  blocking collectives  59 us (26%)
  Pallas kernels  58.9 us (26%)
  waiting for transfers between devices  54.3 us (24%)
  starting transfers between devices  15.3 us (7%)
  other arithmetic  14.9 us (7%)
  between operations  14.8 us (7%)
  local copies, waits for them, and re-layouts  3.88 us (2%)
  matrix products  2.36 us (1%)
    all_to_all x1, blocking collectives, scatter_sum(): got = lax.all_to_all(parts, axis, 0, 0, tiled=False)  59 us
    pallas_call x1, Pallas kernels, butterfly_sum(): pl.pallas_call(functools.partial(butterfly_kernel, tuple(steps)), out_sha...  43.3 us
    all_to_all x1, waiting for transfers between devices, scatter_sum(): got = lax.all_to_all(parts, axis, 0, 0, tiled=False)  27.7 us
    all_to_all x1, waiting for transfers between devices, gather_all(): got = lax.all_to_all(spread, axis, 0, 0, tiled=False)  26.6 us
    pallas_call x2, Pallas kernels, accumulate(): pl.pallas_call(functools.partial(accumulate_kernel, backward), out_shape=...  15.6 us
    all_to_all x1, starting transfers between devices, gather_all(): got = lax.all_to_all(spread, axis, 0, 0, tiled=False)  7.87 us
    all_to_all x1, starting transfers between devices, scatter_sum(): got = lax.all_to_all(parts, axis, 0, 0, tiled=False)  7.38 us
  transfers between devices with their start and end apart: 3, of which 2 were waited for; matrix products, arithmetic and copies ran while one was open for 2% of the time, Pallas kernels for 19%

profile of v12, /device:TPU:0, one launch (start us, length us, event | category | flops | bytes accessed | tf_op | source)
XLA Modules:
  0.0 223.5 jit_solution(1228550376972255333)
XLA Ops:
  7.2 0.0 copy-start
  7.2 0.0 copy-start.3
  7.2 0.0 copy-start.4
  7.2 2.5 %broadcast_in_dim.4 = bf16[8,512,256]{2,1,0:T(8,128)(2,1)} broadcast(bf16[512,256]{1,0:T(8,128)(2,1)} %param.8), dimensions={1,2} | broadcast | bytes 2359296 | tf_op jit(solution)/shard_map/broadcast_in_dim | solution.py:146
  9.7 7.9 %all-to-all-start = ((bf16[8,512,256]{2,1,0:T(8,128)(2,1)}), bf16[8,512,256]{2,1,0:T(8,128)(2,1)S(1)}, u32[]{:S(2)}, u32[]{:S(2)}) async-start(bf16[8,512,256]{2,1,0:T(8,128)(2,1)} %broadcast_in_dim.4), calls=%async_computation | async-start | bytes 4194304 | tf_op jit(solution)/shard_map/all_to_all | solution.py:147
  17.5 0.0 all-gather.2.cloned.1.call-start
  18.2 0.6 reduce.2.dest_ref
  18.8 0.5 reduce.3.source_ref
  19.4 26.6 %all-to-all-done = bf16[8,512,256]{2,1,0:T(8,128)(2,1)S(1)} async-done(((bf16[8,512,256]{2,1,0:T(8,128)(2,1)}), bf16[8,512,256]{2,1,0:T(8,128)(2,1)S(1)}, u32[]{:S(2)}, u32[]{:S(2)}) %all-to-all-start) | async-done | bytes 2097184 | tf_op jit(solution)/shard_map/all_to_all | solution.py:147
  46.0 1.4 copy-done.1
  47.4 8.2 %shard_map.111 = f32[64,128,256]{2,1,0:T(8,128)} custom-call(s32[384]{0:T(512)} %reduce.2.dest_ref, s32[384]{0:T(512)} %reduce.3.source_ref, s32[1]{0:T(128)} %bitcast.14.count_ref, bf16[384,128,128]{2,1,0:T(8,128)(2,1)} %bitcast.16, bf16[32,128,256]{2,1,0:T(8,128)(2,1)} %bitcast.19), custom_call_target="tpu_custom_call" | custom-call | flops 3221225472 | bytes 23068672 | tf_op jit(solution)/shard_map/pallas_call | solution.py:72
  55.6 4.0 %convert_element_type.33 = bf16[64,128,256]{2,1,0:T(8,128)(2,1)S(1)} convert(f32[64,128,256]{2,1,0:T(8,128)} %shard_map.111) | non-fusion elementwise | flops 2097152 | bytes 12582912 | tf_op jit(solution)/shard_map/convert_element_type | solution.py:176
  59.6 59.0 %all_to_all.15 = bf16[16,512,256]{2,1,0:T(8,128)(2,1)} all-to-all(bf16[16,512,256]{2,1,0:T(8,128)(2,1)S(1)} %bitcast.18), channel_id=1, replica_groups=mesh['row'=8,'col'=16] {'col'}, dimensions={0} | all-to-all | bytes 8388608 | tf_op jit(solution)/shard_map/all_to_all | solution.py:153
  118.6 2.9 %reduce_sum.33 = bf16[512,256]{1,0:T(8,128)(2,1)S(1)} reduce(bf16[16,512,256]{2,1,0:T(8,128)(2,1)} %all_to_all.15, bf16[]{:T(256)} %constant.4.clone.1), dimensions={0}, to_apply=%region_0.0 | reduce | flops 1966080 | bytes 4456450 | tf_op jit(solution)/shard_map/reduce_sum | solution.py:154
  121.5 0.0 copy-done
  121.5 0.0 copy-done.5
  121.6 0.0 copy-done.6
  121.6 1.1 convert_reduce_fusion
  122.7 1.0 convolution_convert_fusion
  123.7 0.0 all-gather.2.cloned.1.call-update
  123.7 0.3 fusion
  124.0 0.7 pad_maximum_fusion.value_ref
  124.7 43.3 %shard_map.112 = f32[257,256]{1,0:T(8,128)} custom-call(f32[257,256]{1,0:T(8,128)} %pad_maximum_fusion.value_ref), custom_call_target="tpu_custom_call" | custom-call | tf_op jit(solution)/shard_map/pallas_call | solution.py:130
  168.0 0.0 all-gather.2.cloned.1.call-done
  168.0 7.4 %shard_map.113 = f32[32,128,256]{2,1,0:T(8,128)} custom-call(s32[384]{0:T(512)} %reduce.2.dest_ref, s32[384]{0:T(512)} %reduce.3.source_ref, s32[1]{0:T(128)} %bitcast.15.count_ref, bf16[384,128,128]{2,1,0:T(8,128)(2,1)} %bitcast.17, bf16[64,128,256]{2,1,0:T(8,128)(2,1)} %bitcast.20), custom_call_target="tpu_custom_call" | custom-call | flops 3221225472 | bytes 20971520 | tf_op jit(solution)/shard_map/pallas_call | solution.py:72
  175.4 3.9 %convert_element_type.40 = bf16[32,128,256]{2,1,0:T(8,128)(2,1)} convert(f32[32,128,256]{2,1,0:T(8,128)} %shard_map.113) | non-fusion elementwise | flops 1048576 | bytes 6291456 | tf_op jit(solution)/shard_map/convert_element_type | solution.py:195
  179.3 7.4 %all-to-all-start.2 = ((bf16[8,512,256]{2,1,0:T(8,128)(2,1)}), bf16[8,512,256]{2,1,0:T(8,128)(2,1)S(1)}, u32[]{:S(2)}, u32[]{:S(2)}) async-start(bf16[8,512,256]{2,1,0:T(8,128)(2,1)} %bitcast.7), calls=%async_computation.2 | async-start | bytes 4194304 | tf_op jit(solution)/shard_map/all_to_all | solution.py:153
  186.7 0.0 copy-done.2
  186.7 0.6 slice_multiply_fusion.1
  187.2 0.7 slice_multiply_fusion
  188.0 27.7 %all-to-all-done.2 = bf16[8,512,256]{2,1,0:T(8,128)(2,1)S(1)} async-done(((bf16[8,512,256]{2,1,0:T(8,128)(2,1)}), bf16[8,512,256]{2,1,0:T(8,128)(2,1)S(1)}, u32[]{:S(2)}, u32[]{:S(2)}) %all-to-all-start.2) | async-done | bytes 2097184 | tf_op jit(solution)/shard_map/all_to_all | solution.py:153
  215.7 1.0 reduce_sum.35
  (6 shorter events, 0.0 us)
Async XLA Ops:
  7.2 114.4 %copy-start = (bf16[256,256]{1,0:T(8,128)(2,1)S(1)}, bf16[256,256]{1,0:T(8,128)(2,1)}, u32[]{:S(2)}) copy-start(bf16[256,256]{1,0:T(8,128)(2,1)} %param.9) | copy-start | bytes 393220
  7.2 11.0 %copy-start.3 = (s32[1,1,384]{2,1,0:T(1,128)S(1)}, s32[1,1,384]{2,1,0:T(1,128)}, u32[]{:S(2)}) copy-start(s32[1,1,384]{2,1,0:T(1,128)} %param.13) | copy-start | bytes 4612
  7.2 11.6 %copy-start.4 = (s32[1,1,384]{2,1,0:T(1,128)S(1)}, s32[1,1,384]{2,1,0:T(1,128)}, u32[]{:S(2)}) copy-start(s32[1,1,384]{2,1,0:T(1,128)} %param.14) | copy-start | bytes 4612
  9.7 36.3 %all-to-all-start = ((bf16[8,512,256]{2,1,0:T(8,128)(2,1)}), bf16[8,512,256]{2,1,0:T(8,128)(2,1)S(1)}, u32[]{:S(2)}, u32[]{:S(2)}) async-start(bf16[8,512,256]{2,1,0:T(8,128)(2,1)} %broadcast_in_dim.4), calls=%async_computation | async-start | bytes 4194304 | tf_op jit(solution)/shard_map/all_to_all | solution.py:147
  17.5 150.5 %all-gather.2.cloned.1.call-start = ((), (), s32[]{:S(2)}) async-start(), calls=%async_computation.3 | async-start | bytes 4456448 | tf_op jit(solution)/shard_map/all_gather | solution.py:187
  46.0 1.4 copy-start.1
  118.6 2.9 %copy-start.5 = (bf16[512,256]{1,0:T(8,128)(2,1)S(1)}, bf16[512,256]{1,0:T(8,128)(2,1)}, u32[]{:S(2)}) copy-start(bf16[512,256]{1,0:T(8,128)(2,1)} %param.11) | copy-start | bytes 786436
  118.6 2.9 %copy-start.6 = (f32[256]{0:T(256)S(1)}, f32[256]{0:T(256)}, u32[]{:S(2)}) copy-start(f32[256]{0:T(256)} %param.10) | copy-start | bytes 3076
  175.4 11.3 %copy-start.2 = (f32[257,256]{1,0:T(8,128)S(1)}, f32[257,256]{1,0:T(8,128)}, u32[]{:S(2)}) copy-start(f32[257,256]{1,0:T(8,128)} %shard_map.112) | copy-start | bytes 789508
  179.3 36.4 %all-to-all-start.2 = ((bf16[8,512,256]{2,1,0:T(8,128)(2,1)}), bf16[8,512,256]{2,1,0:T(8,128)(2,1)S(1)}, u32[]{:S(2)}, u32[]{:S(2)}) async-start(bf16[8,512,256]{2,1,0:T(8,128)(2,1)} %bitcast.7), calls=%async_computation.2 | async-start | bytes 4194304 | tf_op jit(solution)/shard_map/all_to_all | solution.py:153
Sparse Core Ops, SparseCore 0:
  123.8 40.2 all-gather.1

commit v13 on v7

--- a/solution.py
+++ b/solution.py
@@ -8,8 +8,8 @@
 from jax.experimental.pallas import tpu as pltpu
 from jax.sharding import PartitionSpec as P
 
-GROUP = 32
-UNROLL = 32
+GROUP = 64
+UNROLL = 64
 
 
 def accumulate_kernel(backward, dest_ref, source_ref, count_ref, tiles_ref, panel_ref, out_ref):
@@ -27,21 +27,20 @@
 
     def one_tile(i, checked):
         slot = base + i
+        tile = tiles_ref[i]
+        if checked:
+            tile = jnp.where(slot < live_count, tile, jnp.zeros_like(tile))
         if backward:
             fetch = jnp.clip(dest_ref[slot], 0, in_blocks - 1)
             target = jnp.clip(source_ref[slot], 0, out_blocks - 1)
             contrib = lax.dot_general(
-                tiles_ref[i], panel_ref[fetch], (((0,), (0,)), ((), ())),
+                tile, panel_ref[fetch], (((0,), (0,)), ((), ())),
                 preferred_element_type=jnp.float32,
             )
         else:
             fetch = jnp.clip(source_ref[slot], 0, in_blocks - 1)
             target = jnp.clip(dest_ref[slot], 0, out_blocks - 1)
-            contrib = jnp.dot(
-                tiles_ref[i], panel_ref[fetch], preferred_element_type=jnp.float32
-            )
-        if checked:
-            contrib = jnp.where(slot < live_count, contrib, 0.0)
+            contrib = jnp.dot(tile, panel_ref[fetch], preferred_element_type=jnp.float32)
         out_ref[target] += contrib
 
     @pl.when(base + group <= live_count)
@@ -52,7 +51,7 @@
 
     @pl.when((base < live_count) & (base + group > live_count))
     def _():
-        @pl.loop(0, group)
+        @pl.loop(0, group, unroll=UNROLL)
         def _(i):
             one_tile(i, True)
 
@@ -91,23 +90,33 @@
     )(dest_ids, source_ids, live_count.reshape(1), tiles, source_blocks)
 
 
-def butterfly_kernel(steps, value_ref, out_ref, slots, send_sems, recv_sems):
+def butterfly_kernel(steps, value_ref, out_ref, outgoing, narrow_slots, wide_slots,
+                     send_sems, recv_sems):
+    barrier = pltpu.get_barrier_semaphore()
     partners = []
-    for axis, distance in steps:
+    for axis, distance, narrow in steps:
         me = lax.axis_index(axis)
         bit = (me // distance) % 2
-        partners.append((axis, me + distance - 2 * distance * bit))
-    barrier = pltpu.get_barrier_semaphore()
-    for axis, partner in partners:
+        partners.append((axis, me + distance - 2 * distance * bit, narrow))
+    for axis, partner, narrow in partners:
         pl.semaphore_signal(
             barrier, 1, device_id={axis: partner}, device_id_type=pl.DeviceIdType.MESH
         )
     pl.semaphore_wait(barrier, len(partners))
     out_ref[...] = value_ref[...]
-    for index, (axis, partner) in enumerate(partners):
+    narrow_index = 0
+    wide_index = 0
+    for index, (axis, partner, narrow) in enumerate(partners):
+        if narrow:
+            outgoing[...] = out_ref[...].astype(outgoing.dtype)
+            source = outgoing
+            landing = narrow_slots.at[narrow_index]
+        else:
+            source = out_ref
+            landing = wide_slots.at[wide_index]
         copy = pltpu.make_async_remote_copy(
-            src_ref=out_ref,
-            dst_ref=slots.at[index],
+            src_ref=source,
+            dst_ref=landing,
             send_sem=send_sems.at[index],
             recv_sem=recv_sems.at[index],
             device_id={axis: partner},
@@ -116,24 +125,33 @@
         copy.start()
         copy.wait_send()
         copy.wait_recv()
-        out_ref[...] = out_ref[...] + slots[index]
+        if narrow:
+            out_ref[...] = outgoing[...].astype(jnp.float32) + landing[...].astype(jnp.float32)
+            narrow_index += 1
+        else:
+            out_ref[...] = out_ref[...] + landing[...]
+            wide_index += 1
 
 
 def butterfly_sum(value, axes, tag):
     steps = []
-    for axis, size in axes:
+    for axis, size, narrow in axes:
         distance = 1
         while distance < size:
-            steps.append((axis, distance))
+            steps.append((axis, distance, narrow))
             distance *= 2
     count = len(steps)
+    narrow_count = max(sum(1 for step in steps if step[2]), 1)
+    wide_count = max(count - narrow_count, 1)
     return pl.pallas_call(
         functools.partial(butterfly_kernel, tuple(steps)),
         out_shape=jax.ShapeDtypeStruct(value.shape, value.dtype),
         in_specs=[pl.BlockSpec(memory_space=pltpu.VMEM)],
         out_specs=pl.BlockSpec(memory_space=pltpu.VMEM),
         scratch_shapes=[
-            pltpu.VMEM((count,) + value.shape, value.dtype),
+            pltpu.VMEM(value.shape, jnp.bfloat16),
+            pltpu.VMEM((narrow_count,) + value.shape, jnp.bfloat16),
+            pltpu.VMEM((wide_count,) + value.shape, value.dtype),
             pltpu.SemaphoreType.DMA((count,)),
             pltpu.SemaphoreType.DMA((count,)),
         ],
@@ -197,15 +215,15 @@
     return got.reshape((size * value.shape[0],) + value.shape[1:])
 
 
-def scatter_sum_native(value, axis, size):
+def scatter_sum_pallas(value, axis, size, tag):
+    parts = value.reshape((size, value.shape[0] // size) + value.shape[1:])
+    got = exchange(parts, axis, size, False, tag)
+    return jnp.sum(got.astype(jnp.float32), axis=0)
+
+
+def scatter_sum(value, axis, size):
     parts = value.reshape((size, value.shape[0] // size) + value.shape[1:])
     got = lax.all_to_all(parts, axis, 0, 0, tiled=False)
-    return jnp.sum(got.astype(jnp.float32), axis=0)
-
-
-def scatter_sum(value, axis, size, tag):
-    parts = value.reshape((size, value.shape[0] // size) + value.shape[1:])
-    got = exchange(parts, axis, size, False, tag)
     return jnp.sum(got.astype(jnp.float32), axis=0)
 
 
@@ -228,7 +246,7 @@
         tile_set, dest_ids, source_ids, live_count, panel_blocks, blocks_down, False
     )
     term = partial_value.reshape(blocks_down * block, width)
-    summed = scatter_sum_native(term.astype(jnp.bfloat16), "col", col_count)
+    summed = scatter_sum(term.astype(jnp.bfloat16), "col", col_count)
     aggregated = summed.astype(jnp.bfloat16)
     preact = jnp.dot(aggregated, weight, preferred_element_type=jnp.float32) + bias
     hidden = jax.nn.silu(preact).astype(jnp.bfloat16)
@@ -240,14 +258,14 @@
     grad_agg = jnp.dot(grad_pre, weight.T, preferred_element_type=jnp.float32).astype(jnp.bfloat16)
     packed = jnp.concatenate([local_weight, local_bias[None, :]], axis=0)
     grad_panel = lax.all_gather(grad_agg, "col", axis=0, tiled=True)
-    packed = butterfly_sum(packed, (("col", col_count), ("row", row_count)), 1)
+    packed = butterfly_sum(packed, (("col", col_count, True), ("row", row_count, False)), 1)
     grad_panel, packed = lax.optimization_barrier((grad_panel, packed))
     grad_blocks = grad_panel.reshape(blocks_down, block, width)
     partial_back = accumulate(
         tile_set, dest_ids, source_ids, live_count, grad_blocks, blocks_across, True
     )
     term_back = partial_back.reshape(blocks_across * block, width)
-    grad_features = scatter_sum(term_back.astype(jnp.bfloat16), "row", row_count, 0).astype(
+    grad_features = scatter_sum_pallas(term_back.astype(jnp.bfloat16), "row", row_count, 0).astype(
         jnp.bfloat16
     )
     grad_weight = packed[:width] * factor

time: 252 us -> 230 us (0.913)
  Pallas kernels: 115 us -> 92.5 us
    pallas_call x1, Pallas kernels: 62.6 us -> 45 us  [butterfly_sum(): pl.pallas_call(functools.partial(butterfly_kernel, tuple(steps)), out_sha...]
    pallas_call x2, Pallas kernels: 18.2 us -> 15.6 us  [accumulate(): pl.pallas_call(functools.partial(accumulate_kernel, backward), out_shape=...]
  transfers between devices with their start and end apart: 2 -> 2, of which waited for: 1 -> 1; matrix products, arithmetic and copies ran while one was open for 1% -> 1% of each run, Pallas kernels for 25% -> 20%
where the time goes in v13:
time: 230 us; the launch traced here: 228 us
  Pallas kernels  92.5 us (40%)
  blocking collectives  61.6 us (27%)
  waiting for transfers between devices  26.6 us (12%)
  other arithmetic  18.1 us (8%)
  between operations  14.8 us (6%)
  starting transfers between devices  7.9 us (3%)
  local copies, waits for them, and re-layouts  3.89 us (2%)
  matrix products  2.35 us (1%)
    all_to_all x1, blocking collectives, scatter_sum(): got = lax.all_to_all(parts, axis, 0, 0, tiled=False)  61.6 us
    pallas_call x1, Pallas kernels, butterfly_sum(): pl.pallas_call(functools.partial(butterfly_kernel, tuple(steps)), out_sha...  45 us
    pallas_call x1, Pallas kernels, exchange(): pl.pallas_call(functools.partial(exchange_kernel, axis, size, spread), ou...  31.9 us
    all_to_all x1, waiting for transfers between devices, gather_all(): got = lax.all_to_all(spread, axis, 0, 0, tiled=False)  26.6 us
    pallas_call x2, Pallas kernels, accumulate(): pl.pallas_call(functools.partial(accumulate_kernel, backward), out_shape=...  15.6 us
    all_to_all x1, starting transfers between devices, gather_all(): got = lax.all_to_all(spread, axis, 0, 0, tiled=False)  7.87 us
  transfers between devices with their start and end apart: 2, of which 1 were waited for; matrix products, arithmetic and copies ran while one was open for 1% of the time, Pallas kernels for 20%

profile of v13, /device:TPU:0, one launch (start us, length us, event | category | flops | bytes accessed | tf_op | source)
XLA Modules:
  0.0 227.8 jit_solution(7668555017672351829)
XLA Ops:
  7.2 0.0 copy-start
  7.2 0.0 copy-start.2
  7.2 0.0 copy-start.3
  7.2 2.5 %broadcast_in_dim.4 = bf16[8,512,256]{2,1,0:T(8,128)(2,1)} broadcast(bf16[512,256]{1,0:T(8,128)(2,1)} %param.8), dimensions={1,2} | broadcast | bytes 2359296 | tf_op jit(solution)/shard_map/broadcast_in_dim | solution.py:213
  9.7 7.9 %all-to-all-start = ((bf16[8,512,256]{2,1,0:T(8,128)(2,1)}), bf16[8,512,256]{2,1,0:T(8,128)(2,1)S(1)}, u32[]{:S(2)}, u32[]{:S(2)}) async-start(bf16[8,512,256]{2,1,0:T(8,128)(2,1)} %broadcast_in_dim.4), calls=%async_computation | async-start | bytes 4194304 | tf_op jit(solution)/shard_map/all_to_all | solution.py:214
  17.5 0.0 all-gather.2.cloned.1.call-start
  18.2 0.0 copy-done.2
  18.2 0.6 reduce.2.dest_ref
  18.8 0.0 copy-done.3
  18.8 0.5 reduce.3.source_ref
  19.4 26.6 %all-to-all-done = bf16[8,512,256]{2,1,0:T(8,128)(2,1)S(1)} async-done(((bf16[8,512,256]{2,1,0:T(8,128)(2,1)}), bf16[8,512,256]{2,1,0:T(8,128)(2,1)S(1)}, u32[]{:S(2)}, u32[]{:S(2)}) %all-to-all-start) | async-done | bytes 2097184 | tf_op jit(solution)/shard_map/all_to_all | solution.py:214
  46.0 1.4 copy-done.1
  47.4 8.2 %shard_map.111 = f32[64,128,256]{2,1,0:T(8,128)} custom-call(s32[384]{0:T(512)} %reduce.2.dest_ref, s32[384]{0:T(512)} %reduce.3.source_ref, s32[1]{0:T(128)} %bitcast.14.count_ref, bf16[384,128,128]{2,1,0:T(8,128)(2,1)} %bitcast.16, bf16[32,128,256]{2,1,0:T(8,128)(2,1)} %bitcast.20), custom_call_target="tpu_custom_call" | custom-call | flops 3221225472 | bytes 23068672 | tf_op jit(solution)/shard_map/pallas_call | solution.py:72
  55.6 4.0 %convert_element_type.33 = bf16[64,128,256]{2,1,0:T(8,128)(2,1)S(1)} convert(f32[64,128,256]{2,1,0:T(8,128)} %shard_map.111) | non-fusion elementwise | flops 2097152 | bytes 12582912 | tf_op jit(solution)/shard_map/convert_element_type | solution.py:249
  59.6 61.6 %all_to_all.10 = bf16[16,512,256]{2,1,0:T(8,128)(2,1)} all-to-all(bf16[16,512,256]{2,1,0:T(8,128)(2,1)S(1)} %bitcast.18), channel_id=1, replica_groups=mesh['row'=8,'col'=16] {'col'}, dimensions={0} | all-to-all | bytes 8388608 | tf_op jit(solution)/shard_map/all_to_all | solution.py:226
  121.2 2.9 %reduce_sum.33 = bf16[512,256]{1,0:T(8,128)(2,1)S(1)} reduce(bf16[16,512,256]{2,1,0:T(8,128)(2,1)} %all_to_all.10, bf16[]{:T(256)} %constant.4.clone.1), dimensions={0}, to_apply=%region_0.0 | reduce | flops 1966080 | bytes 4456450 | tf_op jit(solution)/shard_map/reduce_sum | solution.py:227
  124.1 0.0 copy-done
  124.1 0.0 copy-done.4
  124.1 0.0 copy-done.5
  124.1 1.1 convert_reduce_fusion
  125.3 1.0 convolution_convert_fusion
  126.2 0.0 all-gather.2.cloned.1.call-update
  126.2 0.3 fusion
  126.5 0.7 pad_maximum_fusion.value_ref
  127.2 45.0 %shard_map.112 = f32[257,256]{1,0:T(8,128)} custom-call(f32[257,256]{1,0:T(8,128)} %pad_maximum_fusion.value_ref), custom_call_target="tpu_custom_call" | custom-call | tf_op jit(solution)/shard_map/pallas_call | solution.py:146
  172.3 0.0 all-gather.2.cloned.1.call-done
  172.3 1.3 slice_multiply_fusion.1
  173.6 1.7 slice_multiply_fusion
  175.2 7.4 %shard_map.113 = f32[32,128,256]{2,1,0:T(8,128)} custom-call(s32[384]{0:T(512)} %reduce.2.dest_ref, s32[384]{0:T(512)} %reduce.3.source_ref, s32[1]{0:T(128)} %bitcast.15.count_ref, bf16[384,128,128]{2,1,0:T(8,128)(2,1)} %bitcast.17, bf16[64,128,256]{2,1,0:T(8,128)(2,1)} %bitcast.21), custom_call_target="tpu_custom_call" | custom-call | flops 3221225472 | bytes 20971520 | tf_op jit(solution)/shard_map/pallas_call | solution.py:72
  182.6 3.8 %convert_element_type.40 = bf16[32,128,256]{2,1,0:T(8,128)(2,1)} convert(f32[32,128,256]{2,1,0:T(8,128)} %shard_map.113) | non-fusion elementwise | flops 1048576 | bytes 6291456 | tf_op jit(solution)/shard_map/convert_element_type | solution.py:268
  186.5 31.9 %shard_map.114 = bf16[8,512,256]{2,1,0:T(8,128)(2,1)} custom-call(bf16[8,512,256]{2,1,0:T(8,128)(2,1)} %bitcast.19), custom_call_target="tpu_custom_call" | custom-call | bytes 4194304 | tf_op jit(solution)/shard_map/pallas_call | solution.py:197
  218.3 2.7 %reduce_sum.35 = bf16[512,256]{1,0:T(8,128)(2,1)} reduce(bf16[8,512,256]{2,1,0:T(8,128)(2,1)} %shard_map.114, bf16[]{:T(256)} %constant.4.clone.1), dimensions={0}, to_apply=%region_2.3 | reduce | flops 917504 | bytes 2359298 | tf_op jit(solution)/shard_map/reduce_sum | solution.py:221
  (3 shorter events, 0.0 us)
Async XLA Ops:
  7.2 116.9 %copy-start = (bf16[256,256]{1,0:T(8,128)(2,1)S(1)}, bf16[256,256]{1,0:T(8,128)(2,1)}, u32[]{:S(2)}) copy-start(bf16[256,256]{1,0:T(8,128)(2,1)} %param.9) | copy-start | bytes 393220
  7.2 11.1 %copy-start.2 = (s32[1,1,384]{2,1,0:T(1,128)S(1)}, s32[1,1,384]{2,1,0:T(1,128)}, u32[]{:S(2)}) copy-start(s32[1,1,384]{2,1,0:T(1,128)} %param.13) | copy-start | bytes 4612
  7.2 11.6 %copy-start.3 = (s32[1,1,384]{2,1,0:T(1,128)S(1)}, s32[1,1,384]{2,1,0:T(1,128)}, u32[]{:S(2)}) copy-start(s32[1,1,384]{2,1,0:T(1,128)} %param.14) | copy-start | bytes 4612
  9.7 36.3 %all-to-all-start = ((bf16[8,512,256]{2,1,0:T(8,128)(2,1)}), bf16[8,512,256]{2,1,0:T(8,128)(2,1)S(1)}, u32[]{:S(2)}, u32[]{:S(2)}) async-start(bf16[8,512,256]{2,1,0:T(8,128)(2,1)} %broadcast_in_dim.4), calls=%async_computation | async-start | bytes 4194304 | tf_op jit(solution)/shard_map/all_to_all | solution.py:214
  17.5 154.8 %all-gather.2.cloned.1.call-start = ((), (), s32[]{:S(2)}) async-start(), calls=%async_computation.2 | async-start | bytes 4456448 | tf_op jit(solution)/shard_map/all_gather | solution.py:260
  46.0 1.4 copy-start.1
  121.2 2.9 %copy-start.4 = (bf16[512,256]{1,0:T(8,128)(2,1)S(1)}, bf16[512,256]{1,0:T(8,128)(2,1)}, u32[]{:S(2)}) copy-start(bf16[512,256]{1,0:T(8,128)(2,1)} %param.11) | copy-start | bytes 786436
  121.2 2.9 %copy-start.5 = (f32[256]{0:T(256)S(1)}, f32[256]{0:T(256)}, u32[]{:S(2)}) copy-start(f32[256]{0:T(256)} %param.10) | copy-start | bytes 3076
Sparse Core Ops, SparseCore 0:
  126.4 38.5 all-gather.1

commit v14 on v12

--- a/solution.py
+++ b/solution.py
@@ -12,7 +12,8 @@
 UNROLL = 64
 
 
-def accumulate_kernel(backward, dest_ref, source_ref, count_ref, tiles_ref, panel_ref, out_ref):
+def accumulate_kernel(backward, dest_ref, source_ref, count_ref, tiles_ref, panel_ref, result_ref,
+                      out_ref):
     step = pl.program_id(0)
     group = tiles_ref.shape[0]
     out_blocks = out_ref.shape[0]
@@ -55,6 +56,10 @@
         def _(i):
             one_tile(i, True)
 
+    @pl.when(step == pl.num_programs(0) - 1)
+    def _():
+        result_ref[...] = out_ref[...].astype(result_ref.dtype)
+
 
 def accumulate(tiles, dest_ids, source_ids, live_count, source_blocks, out_blocks, backward):
     slots, block, _ = tiles.shape
@@ -71,7 +76,7 @@
     bytes_accessed = tiles.size * 2 + source_blocks.size * 2 + out_blocks * block * width * 4
     return pl.pallas_call(
         functools.partial(accumulate_kernel, backward),
-        out_shape=jax.ShapeDtypeStruct((out_blocks, block, width), jnp.float32),
+        out_shape=jax.ShapeDtypeStruct((out_blocks, block, width), jnp.bfloat16),
         grid_spec=pltpu.PrefetchScalarGridSpec(
             num_scalar_prefetch=3,
             grid=(steps,),
@@ -80,6 +85,7 @@
                 pl.BlockSpec((in_blocks, block, width), lambda g, d, s, c: (0, 0, 0)),
             ],
             out_specs=pl.BlockSpec((out_blocks, block, width), lambda g, d, s, c: (0, 0, 0)),
+            scratch_shapes=[pltpu.VMEM((out_blocks, block, width), jnp.float32)],
         ),
         compiler_params=pltpu.CompilerParams(
             dimension_semantics=("arbitrary",), vmem_limit_bytes=60 * 1024 * 1024

time: 226 us -> 217 us (0.960)
  other arithmetic: 14.9 us -> 7.13 us
  starting transfers between devices: 15.3 us -> 11.8 us
    convert_element_type x2 -> x0, other arithmetic: 7.86 us -> none  [the longest x1 3.98 us: per_device(): summed = scatter_sum(term.astype(jnp.bfloat16), 'col', col_count)]
    all_to_all x1, starting transfers between devices: 7.38 us -> 3.91 us  [scatter_sum(): got = lax.all_to_all(parts, axis, 0, 0, tiled=False)]
  transfers between devices with their start and end apart: 3 -> 3, of which waited for: 2 -> 2; matrix products, arithmetic and copies ran while one was open for 2% -> 2% of each run, Pallas kernels for 19% -> 20%
where the time goes in v14:
time: 217 us; the launch traced here: 214 us
  blocking collectives  60.1 us (28%)
  Pallas kernels  59 us (27%)
  waiting for transfers between devices  54.7 us (25%)
  between operations  14.8 us (7%)
  starting transfers between devices  11.8 us (5%)
  other arithmetic  7.13 us (3%)
  local copies, waits for them, and re-layouts  3.82 us (2%)
  matrix products  2.36 us (1%)
    all_to_all x1, blocking collectives, scatter_sum(): got = lax.all_to_all(parts, axis, 0, 0, tiled=False)  60.1 us
    pallas_call x1, Pallas kernels, butterfly_sum(): pl.pallas_call(functools.partial(butterfly_kernel, tuple(steps)), out_sha...  42.1 us
    all_to_all x1, waiting for transfers between devices, scatter_sum(): got = lax.all_to_all(parts, axis, 0, 0, tiled=False)  28.1 us
    all_to_all x1, waiting for transfers between devices, gather_all(): got = lax.all_to_all(spread, axis, 0, 0, tiled=False)  26.5 us
    pallas_call x2, Pallas kernels, accumulate(): pl.pallas_call(functools.partial(accumulate_kernel, backward), out_shape=...  16.9 us
    all_to_all x1, starting transfers between devices, gather_all(): got = lax.all_to_all(spread, axis, 0, 0, tiled=False)  7.87 us
  transfers between devices with their start and end apart: 3, of which 2 were waited for; matrix products, arithmetic and copies ran while one was open for 2% of the time, Pallas kernels for 20%

profile of v14, /device:TPU:0, one launch (start us, length us, event | category | flops | bytes accessed | tf_op | source)
XLA Modules:
  0.0 213.6 jit_solution(633559220858764022)
XLA Ops:
  7.2 0.0 copy-start
  7.2 0.0 copy-start.3
  7.2 0.0 copy-start.4
  7.2 2.5 %broadcast_in_dim.4 = bf16[8,512,256]{2,1,0:T(8,128)(2,1)} broadcast(bf16[512,256]{1,0:T(8,128)(2,1)} %param.8), dimensions={1,2} | broadcast | bytes 2359296 | tf_op jit(solution)/shard_map/broadcast_in_dim | solution.py:152
  9.7 7.9 %all-to-all-start = ((bf16[8,512,256]{2,1,0:T(8,128)(2,1)}), bf16[8,512,256]{2,1,0:T(8,128)(2,1)S(1)}, u32[]{:S(2)}, u32[]{:S(2)}) async-start(bf16[8,512,256]{2,1,0:T(8,128)(2,1)} %broadcast_in_dim.4), calls=%async_computation | async-start | bytes 4194304 | tf_op jit(solution)/shard_map/all_to_all | solution.py:153
  17.5 0.0 all-gather.2.cloned.1.call-start
  18.2 0.0 copy-done.3
  18.2 0.6 reduce.2.dest_ref
  18.8 0.0 copy-done.4
  18.8 0.6 reduce.3.source_ref
  19.4 26.5 %all-to-all-done = bf16[8,512,256]{2,1,0:T(8,128)(2,1)S(1)} async-done(((bf16[8,512,256]{2,1,0:T(8,128)(2,1)}), bf16[8,512,256]{2,1,0:T(8,128)(2,1)S(1)}, u32[]{:S(2)}, u32[]{:S(2)}) %all-to-all-start) | async-done | bytes 2097184 | tf_op jit(solution)/shard_map/all_to_all | solution.py:153
  46.0 1.3 copy-done.1
  47.3 8.6 %shard_map.111 = bf16[64,128,256]{2,1,0:T(8,128)(2,1)} custom-call(s32[384]{0:T(512)} %reduce.2.dest_ref, s32[384]{0:T(512)} %reduce.3.source_ref, s32[1]{0:T(128)} %bitcast.14.count_ref, bf16[384,128,128]{2,1,0:T(8,128)(2,1)} %bitcast.16, bf16[32,128,256]{2,1,0:T(8,128)(2,1)} %bitcast.19), custom_call_target="tpu_custom_call" | custom-call | flops 3221225472 | bytes 23068672 | tf_op jit(solution)/shard_map/pallas_call | solution.py:77
  55.9 60.1 %all_to_all.15 = bf16[16,512,256]{2,1,0:T(8,128)(2,1)} all-to-all(bf16[16,512,256]{2,1,0:T(8,128)(2,1)} %bitcast.18), channel_id=1, replica_groups=mesh['row'=8,'col'=16] {'col'}, dimensions={0} | all-to-all | bytes 8388608 | tf_op jit(solution)/shard_map/all_to_all | solution.py:159
  116.0 2.9 %reduce_sum.33 = bf16[512,256]{1,0:T(8,128)(2,1)S(1)} reduce(bf16[16,512,256]{2,1,0:T(8,128)(2,1)} %all_to_all.15, bf16[]{:T(256)} %constant.4.clone.1), dimensions={0}, to_apply=%region_0.0 | reduce | flops 1966080 | bytes 4456450 | tf_op jit(solution)/shard_map/reduce_sum | solution.py:160
  118.9 0.0 copy-done
  118.9 0.0 copy-done.5
  118.9 0.0 copy-done.6
  118.9 1.1 convert_reduce_fusion
  120.1 1.0 convolution_convert_fusion
  121.0 0.0 all-gather.2.cloned.1.call-update
  121.1 0.3 fusion
  121.3 0.7 pad_maximum_fusion.value_ref
  122.1 42.1 %shard_map.112 = f32[257,256]{1,0:T(8,128)} custom-call(f32[257,256]{1,0:T(8,128)} %pad_maximum_fusion.value_ref), custom_call_target="tpu_custom_call" | custom-call | tf_op jit(solution)/shard_map/pallas_call | solution.py:136
  164.1 0.0 all-gather.2.cloned.1.call-done
  164.1 8.3 %shard_map.113 = bf16[32,128,256]{2,1,0:T(8,128)(2,1)} custom-call(s32[384]{0:T(512)} %reduce.2.dest_ref, s32[384]{0:T(512)} %reduce.3.source_ref, s32[1]{0:T(128)} %bitcast.15.count_ref, bf16[384,128,128]{2,1,0:T(8,128)(2,1)} %bitcast.17, bf16[64,128,256]{2,1,0:T(8,128)(2,1)} %bitcast.21), custom_call_target="tpu_custom_call" | custom-call | flops 3221225472 | bytes 20971520 | tf_op jit(solution)/shard_map/pallas_call | solution.py:77
  172.4 3.9 %all-to-all-start.2 = ((bf16[8,512,256]{2,1,0:T(8,128)(2,1)}), bf16[8,512,256]{2,1,0:T(8,128)(2,1)S(1)}, u32[]{:S(2)}, u32[]{:S(2)}) async-start(bf16[8,512,256]{2,1,0:T(8,128)(2,1)} %bitcast.20), calls=%async_computation.2 | async-start | bytes 4194304 | tf_op jit(solution)/shard_map/all_to_all | solution.py:159
  176.3 0.0 copy-done.2
  176.3 0.6 slice_multiply_fusion.1
  176.9 0.7 slice_multiply_fusion
  177.6 28.1 %all-to-all-done.2 = bf16[8,512,256]{2,1,0:T(8,128)(2,1)S(1)} async-done(((bf16[8,512,256]{2,1,0:T(8,128)(2,1)}), bf16[8,512,256]{2,1,0:T(8,128)(2,1)S(1)}, u32[]{:S(2)}, u32[]{:S(2)}) %all-to-all-start.2) | async-done | bytes 2097184 | tf_op jit(solution)/shard_map/all_to_all | solution.py:159
  205.7 1.0 reduce_sum.35
  (4 shorter events, 0.0 us)
Async XLA Ops:
  7.2 111.8 %copy-start = (bf16[256,256]{1,0:T(8,128)(2,1)S(1)}, bf16[256,256]{1,0:T(8,128)(2,1)}, u32[]{:S(2)}) copy-start(bf16[256,256]{1,0:T(8,128)(2,1)} %param.9) | copy-start | bytes 393220
  7.2 11.0 %copy-start.3 = (s32[1,1,384]{2,1,0:T(1,128)S(1)}, s32[1,1,384]{2,1,0:T(1,128)}, u32[]{:S(2)}) copy-start(s32[1,1,384]{2,1,0:T(1,128)} %param.13) | copy-start | bytes 4612
  7.2 11.6 %copy-start.4 = (s32[1,1,384]{2,1,0:T(1,128)S(1)}, s32[1,1,384]{2,1,0:T(1,128)}, u32[]{:S(2)}) copy-start(s32[1,1,384]{2,1,0:T(1,128)} %param.14) | copy-start | bytes 4612
  9.7 36.3 %all-to-all-start = ((bf16[8,512,256]{2,1,0:T(8,128)(2,1)}), bf16[8,512,256]{2,1,0:T(8,128)(2,1)S(1)}, u32[]{:S(2)}, u32[]{:S(2)}) async-start(bf16[8,512,256]{2,1,0:T(8,128)(2,1)} %broadcast_in_dim.4), calls=%async_computation | async-start | bytes 4194304 | tf_op jit(solution)/shard_map/all_to_all | solution.py:153
  17.5 146.6 %all-gather.2.cloned.1.call-start = ((), (), s32[]{:S(2)}) async-start(), calls=%async_computation.3 | async-start | bytes 4456448 | tf_op jit(solution)/shard_map/all_gather | solution.py:193
  46.0 1.3 copy-start.1
  116.0 2.9 %copy-start.5 = (bf16[512,256]{1,0:T(8,128)(2,1)S(1)}, bf16[512,256]{1,0:T(8,128)(2,1)}, u32[]{:S(2)}) copy-start(bf16[512,256]{1,0:T(8,128)(2,1)} %param.11) | copy-start | bytes 786436
  116.0 2.9 %copy-start.6 = (f32[256]{0:T(256)S(1)}, f32[256]{0:T(256)}, u32[]{:S(2)}) copy-start(f32[256]{0:T(256)} %param.10) | copy-start | bytes 3076
  172.4 3.9 %copy-start.2 = (f32[257,256]{1,0:T(8,128)S(1)}, f32[257,256]{1,0:T(8,128)}, u32[]{:S(2)}) copy-start(f32[257,256]{1,0:T(8,128)} %shard_map.112) | copy-start | bytes 789508
  172.4 33.3 %all-to-all-start.2 = ((bf16[8,512,256]{2,1,0:T(8,128)(2,1)}), bf16[8,512,256]{2,1,0:T(8,128)(2,1)S(1)}, u32[]{:S(2)}, u32[]{:S(2)}) async-start(bf16[8,512,256]{2,1,0:T(8,128)(2,1)} %bitcast.20), calls=%async_computation.2 | async-start | bytes 4194304 | tf_op jit(solution)/shard_map/all_to_all | solution.py:159
Sparse Core Ops, SparseCore 0:
  121.2 39.4 all-gather.1

commit v15 on v14

--- a/solution.py
+++ b/solution.py
@@ -61,7 +61,8 @@
         result_ref[...] = out_ref[...].astype(result_ref.dtype)
 
 
-def accumulate(tiles, dest_ids, source_ids, live_count, source_blocks, out_blocks, backward):
+def accumulate(tiles, dest_ids, source_ids, live_count, source_blocks, out_blocks, backward,
+               out_dtype=jnp.bfloat16):
     slots, block, _ = tiles.shape
     width = source_blocks.shape[-1]
     in_blocks = source_blocks.shape[0]
@@ -76,7 +77,7 @@
     bytes_accessed = tiles.size * 2 + source_blocks.size * 2 + out_blocks * block * width * 4
     return pl.pallas_call(
         functools.partial(accumulate_kernel, backward),
-        out_shape=jax.ShapeDtypeStruct((out_blocks, block, width), jnp.bfloat16),
+        out_shape=jax.ShapeDtypeStruct((out_blocks, block, width), out_dtype),
         grid_spec=pltpu.PrefetchScalarGridSpec(
             num_scalar_prefetch=3,
             grid=(steps,),
@@ -160,6 +161,18 @@
     return jnp.sum(got.astype(jnp.float32), axis=0)
 
 
+def scatter_sum_paired(value, axis, size):
+    parity = lax.axis_index(axis) % 2
+    chunks = value.reshape((size // 2, 2, value.shape[0] // size) + value.shape[1:])
+    keep = jnp.where(parity == 0, chunks[:, 0], chunks[:, 1])
+    send = jnp.where(parity == 0, chunks[:, 1], chunks[:, 0])
+    got = lax.ppermute(send, axis, [(i, i ^ 1) for i in range(size)])
+    paired = (keep + got).astype(jnp.bfloat16)
+    groups = [list(range(start, size, 2)) for start in range(2)]
+    spread = lax.all_to_all(paired, axis, 0, 0, tiled=False, axis_index_groups=groups)
+    return jnp.sum(spread.astype(jnp.float32), axis=0)
+
+
 def per_device(features, weight, bias, cotangent, tiles, tile_rows, tile_cols, tile_counts):
     tile_set = tiles[0, 0]
     dest_ids = tile_rows[0, 0]
@@ -176,10 +189,10 @@
     panel = gather_all(features, "row", row_count)
     panel_blocks = panel.reshape(blocks_across, block, width)
     partial_value = accumulate(
-        tile_set, dest_ids, source_ids, live_count, panel_blocks, blocks_down, False
+        tile_set, dest_ids, source_ids, live_count, panel_blocks, blocks_down, False, jnp.float32
     )
     term = partial_value.reshape(blocks_down * block, width)
-    summed = scatter_sum(term.astype(jnp.bfloat16), "col", col_count)
+    summed = scatter_sum_paired(term, "col", col_count)
     aggregated = summed.astype(jnp.bfloat16)
     preact = jnp.dot(aggregated, weight, preferred_element_type=jnp.float32) + bias
     hidden = jax.nn.silu(preact).astype(jnp.bfloat16)

time: 217 us -> 209 us (0.963)
  the two profiles are of different devices: /device:TPU:0 before, /device:TPU:57 now
where the time goes in v15:
time: 209 us; the launch traced here: 208 us
  waiting for transfers between devices  62.9 us (30%)
  Pallas kernels  56.5 us (27%)
  blocking collectives  31.9 us (15%)
  starting transfers between devices  25.4 us (12%)
  between operations  14.8 us (7%)
  other arithmetic  10.3 us (5%)
  local copies, waits for them, and re-layouts  3.86 us (2%)
  matrix products  2.36 us (1%)
    pallas_call x1, Pallas kernels, butterfly_sum(): pl.pallas_call(functools.partial(butterfly_kernel, tuple(steps)), out_sha...  40.7 us
    all_to_all x1, blocking collectives, scatter_sum_paired(): lax.all_to_all(paired, axis, 0, 0, tiled=False, axis_index_groups=groups)  31.9 us
    all_to_all x1, waiting for transfers between devices, scatter_sum(): got = lax.all_to_all(parts, axis, 0, 0, tiled=False)  29.6 us
    all_to_all x1, waiting for transfers between devices, gather_all(): got = lax.all_to_all(spread, axis, 0, 0, tiled=False)  24.8 us
    pallas_call x2, Pallas kernels, accumulate(): pl.pallas_call(functools.partial(accumulate_kernel, backward), out_shape=...  15.8 us
    all_to_all x1, starting transfers between devices, scatter_sum(): got = lax.all_to_all(parts, axis, 0, 0, tiled=False)  12.8 us
    ppermute x1, waiting for transfers between devices, scatter_sum_paired(): got = lax.ppermute(send, axis, [(i, i ^ 1) for i in range(size)])  6.79 us
    all_to_all x1, starting transfers between devices, gather_all(): got = lax.all_to_all(spread, axis, 0, 0, tiled=False)  6.54 us
  transfers between devices with their start and end apart: 4, of which 4 were waited for; matrix products, arithmetic and copies ran while one was open for 2% of the time, Pallas kernels for 20%

profile of v15, /device:TPU:57, one launch (start us, length us, event | category | flops | bytes accessed | tf_op | source)
XLA Modules:
  0.0 208.0 jit_solution(5005824932432234287)
XLA Ops:
  7.2 0.0 copy-start
  7.2 2.5 %broadcast_in_dim.4 = bf16[8,512,256]{2,1,0:T(8,128)(2,1)} broadcast(bf16[512,256]{1,0:T(8,128)(2,1)} %param.8), dimensions={1,2} | broadcast | bytes 2359296 | tf_op jit(solution)/shard_map/broadcast_in_dim | solution.py:153
  9.7 6.5 %all-to-all-start = ((bf16[8,512,256]{2,1,0:T(8,128)(2,1)}), bf16[8,512,256]{2,1,0:T(8,128)(2,1)S(1)}, u32[]{:S(2)}, u32[]{:S(2)}) async-start(bf16[8,512,256]{2,1,0:T(8,128)(2,1)} %broadcast_in_dim.4), calls=%async_computation | async-start | bytes 4194304 | tf_op jit(solution)/shard_map/all_to_all | solution.py:154
  16.9 0.0 copy-done.4
  16.9 0.6 reduce.2.dest_ref
  17.5 0.6 reduce.3.source_ref
  18.1 24.8 %all-to-all-done = bf16[8,512,256]{2,1,0:T(8,128)(2,1)S(1)} async-done(((bf16[8,512,256]{2,1,0:T(8,128)(2,1)}), bf16[8,512,256]{2,1,0:T(8,128)(2,1)S(1)}, u32[]{:S(2)}, u32[]{:S(2)}) %all-to-all-start) | async-done | bytes 2097184 | tf_op jit(solution)/shard_map/all_to_all | solution.py:154
  42.9 1.4 copy-done.2
  44.3 8.8 %shard_map.111 = f32[64,128,256]{2,1,0:T(8,128)} custom-call(s32[384]{0:T(512)} %reduce.2.dest_ref, s32[384]{0:T(512)} %reduce.3.source_ref, s32[1]{0:T(128)} %bitcast.36.count_ref, bf16[384,128,128]{2,1,0:T(8,128)(2,1)} %bitcast.40, bf16[32,128,256]{2,1,0:T(8,128)(2,1)} %bitcast.43), custom_call_target="tpu_custom_call" | custom-call | flops 3221225472 | bytes 23068672 | tf_op jit(solution)/shard_map/pallas_call | solution.py:78
  53.1 4.3 %select_bitcast_fusion = f32[8,512,256]{2,1,0:T(8,128)S(1)} fusion(f32[8,2,512,256]{3,2,1,0:T(8,128)} %bitcast.38, pred[]{:T(512)S(6)} %eq.6), kind=kLoop, calls=%fused_computation.4 | loop fusion | flops 1048576 | bytes 12582913 | tf_op jit(solution)/shard_map/jit(_where)/select_n | solution.py:168
  57.4 6.1 %collective-permute-start = (f32[8,512,256]{2,1,0:T(8,128)S(1)}, f32[8,512,256]{2,1,0:T(8,128)S(1)}, u32[]{:S(2)}, u32[]{:S(2)}) collective-permute-start(f32[8,512,256]{2,1,0:T(8,128)S(1)} %select_bitcast_fusion), channel_id=1, source_target_pairs={{0,1},{1,0},{2,3},{3,2},{4,5},{5,4},{6,7},{7,6},{8,9},{9,8},{10,11... | collective-permute-start | bytes 12582920 | tf_op jit(solution)/shard_map/ppermute | solution.py:169
  63.5 6.8 %collective-permute-done = f32[8,512,256]{2,1,0:T(8,128)S(1)} collective-permute-done((f32[8,512,256]{2,1,0:T(8,128)S(1)}, f32[8,512,256]{2,1,0:T(8,128)S(1)}, u32[]{:S(2)}, u32[]{:S(2)}) %collective-permute-start) | collective-permute-done | bytes 4194336 | tf_op jit(solution)/shard_map/ppermute | solution.py:169
  70.3 1.3 fusion.2
  71.6 0.0 copy-start.6
  71.6 0.0 copy-start.7
  71.7 31.9 %all_to_all.15 = bf16[8,512,256]{2,1,0:T(8,128)(2,1)S(1)} all-to-all(bf16[8,512,256]{2,1,0:T(8,128)(2,1)S(1)} %fusion.2), channel_id=1, replica_groups={{0,2,4,6,8,10,12,14},{1,3,5,7,9,11,13,15},{16,18,20,22,24,26,28,30},{17..., dimensions={0} | all-to-all | bytes 4194304 | tf_op jit(solution)/shard_map/all_to_all | solution.py:172
  103.5 0.4 reduce_sum.33
  103.9 0.0 copy-done
  103.9 0.0 copy-done.6
  103.9 1.1 convert_reduce_fusion
  105.1 1.0 convolution_convert_fusion
  106.0 0.0 all-gather.2.cloned.1.call-update
  106.0 0.3 fusion.3
  106.3 0.7 pad_maximum_fusion.value_ref
  107.0 40.7 %shard_map.112 = f32[257,256]{1,0:T(8,128)} custom-call(f32[257,256]{1,0:T(8,128)} %pad_maximum_fusion.value_ref), custom_call_target="tpu_custom_call" | custom-call | tf_op jit(solution)/shard_map/pallas_call | solution.py:137
  147.8 1.7 all-gather.2.cloned.1.call-done
  149.5 7.0 %shard_map.113 = bf16[32,128,256]{2,1,0:T(8,128)(2,1)} custom-call(s32[384]{0:T(512)} %reduce.2.dest_ref, s32[384]{0:T(512)} %reduce.3.source_ref, s32[1]{0:T(128)} %bitcast.37.count_ref, bf16[384,128,128]{2,1,0:T(8,128)(2,1)} %bitcast.41, bf16[64,128,256]{2,1,0:T(8,128)(2,1)} %bitcast.44), custom_call_target="tpu_custom_call" | custom-call | flops 3221225472 | bytes 20971520 | tf_op jit(solution)/shard_map/pallas_call | solution.py:78
  156.4 12.8 %all-to-all-start.2 = ((bf16[8,512,256]{2,1,0:T(8,128)(2,1)}), bf16[8,512,256]{2,1,0:T(8,128)(2,1)S(1)}, u32[]{:S(2)}, u32[]{:S(2)}) async-start(bf16[8,512,256]{2,1,0:T(8,128)(2,1)} %bitcast.42), calls=%async_computation.2 | async-start | bytes 4194304 | tf_op jit(solution)/shard_map/all_to_all | solution.py:160
  169.2 0.6 slice_multiply_fusion.1
  169.8 0.7 slice_multiply_fusion
  170.5 29.6 %all-to-all-done.2 = bf16[8,512,256]{2,1,0:T(8,128)(2,1)S(1)} async-done(((bf16[8,512,256]{2,1,0:T(8,128)(2,1)}), bf16[8,512,256]{2,1,0:T(8,128)(2,1)S(1)}, u32[]{:S(2)}, u32[]{:S(2)}) %all-to-all-start.2) | async-done | bytes 2097184 | tf_op jit(solution)/shard_map/all_to_all | solution.py:160
  200.1 1.0 reduce_sum.35
  (10 shorter events, 0.0 us)
Async XLA Ops:
  7.2 96.7 %copy-start = (bf16[256,256]{1,0:T(8,128)(2,1)S(1)}, bf16[256,256]{1,0:T(8,128)(2,1)}, u32[]{:S(2)}) copy-start(bf16[256,256]{1,0:T(8,128)(2,1)} %param.9) | copy-start | bytes 393220
  7.2 9.7 %copy-start.4 = (s32[1,1,384]{2,1,0:T(1,128)S(1)}, s32[1,1,384]{2,1,0:T(1,128)}, u32[]{:S(2)}) copy-start(s32[1,1,384]{2,1,0:T(1,128)} %param.13) | copy-start | bytes 4612
  7.2 10.3 %copy-start.5 = (s32[1,1,384]{2,1,0:T(1,128)S(1)}, s32[1,1,384]{2,1,0:T(1,128)}, u32[]{:S(2)}) copy-start(s32[1,1,384]{2,1,0:T(1,128)} %param.14) | copy-start | bytes 4612
  9.7 33.2 %all-to-all-start = ((bf16[8,512,256]{2,1,0:T(8,128)(2,1)}), bf16[8,512,256]{2,1,0:T(8,128)(2,1)S(1)}, u32[]{:S(2)}, u32[]{:S(2)}) async-start(bf16[8,512,256]{2,1,0:T(8,128)(2,1)} %broadcast_in_dim.4), calls=%async_computation | async-start | bytes 4194304 | tf_op jit(solution)/shard_map/all_to_all | solution.py:154
  16.2 133.3 %all-gather.2.cloned.1.call-start = ((), (), s32[]{:S(2)}) async-start(), calls=%async_computation.3 | async-start | bytes 4456448 | tf_op jit(solution)/shard_map/all_gather | solution.py:206
  42.9 1.4 copy-start.2
  53.1 17.2 %copy-start.1 = (f32[64,128,256]{2,1,0:T(8,128)S(1)}, f32[64,128,256]{2,1,0:T(8,128)}, u32[]{:S(2)}) copy-start(f32[64,128,256]{2,1,0:T(8,128)} %shard_map.111) | copy-start | bytes 25165828
  57.4 12.9 %collective-permute-start = (f32[8,512,256]{2,1,0:T(8,128)S(1)}, f32[8,512,256]{2,1,0:T(8,128)S(1)}, u32[]{:S(2)}, u32[]{:S(2)}) collective-permute-start(f32[8,512,256]{2,1,0:T(8,128)S(1)} %select_bitcast_fusion), channel_id=1, source_target_pairs={{0,1},{1,0},{2,3},{3,2},{4,5},{5,4},{6,7},{7,6},{8,9},{9,8},{10,11... | collective-permute-start | bytes 12582920 | tf_op jit(solution)/shard_map/ppermute | solution.py:169
  71.6 32.3 %copy-start.6 = (bf16[512,256]{1,0:T(8,128)(2,1)S(1)}, bf16[512,256]{1,0:T(8,128)(2,1)}, u32[]{:S(2)}) copy-start(bf16[512,256]{1,0:T(8,128)(2,1)} %param.11) | copy-start | bytes 786436
  71.6 32.3 %copy-start.7 = (f32[256]{0:T(256)S(1)}, f32[256]{0:T(256)}, u32[]{:S(2)}) copy-start(f32[256]{0:T(256)} %param.10) | copy-start | bytes 3076
  156.4 12.8 %copy-start.3 = (f32[257,256]{1,0:T(8,128)S(1)}, f32[257,256]{1,0:T(8,128)}, u32[]{:S(2)}) copy-start(f32[257,256]{1,0:T(8,128)} %shard_map.112) | copy-start | bytes 789508
  156.4 43.7 %all-to-all-start.2 = ((bf16[8,512,256]{2,1,0:T(8,128)(2,1)}), bf16[8,512,256]{2,1,0:T(8,128)(2,1)S(1)}, u32[]{:S(2)}, u32[]{:S(2)}) async-start(bf16[8,512,256]{2,1,0:T(8,128)(2,1)} %bitcast.42), calls=%async_computation.2 | async-start | bytes 4194304 | tf_op jit(solution)/shard_map/all_to_all | solution.py:160
Sparse Core Ops, SparseCore 0:
  106.2 43.2 all-gather.1

commit v16 on v15

--- a/solution.py
+++ b/solution.py
@@ -12,8 +12,9 @@
 UNROLL = 64
 
 
-def accumulate_kernel(backward, dest_ref, source_ref, count_ref, tiles_ref, panel_ref, result_ref,
-                      out_ref):
+def accumulate_kernel(backward, split, dest_ref, source_ref, count_ref, tiles_ref, panel_ref,
+                      *refs):
+    out_ref = refs[-1]
     step = pl.program_id(0)
     group = tiles_ref.shape[0]
     out_blocks = out_ref.shape[0]
@@ -58,11 +59,19 @@
 
     @pl.when(step == pl.num_programs(0) - 1)
     def _():
-        result_ref[...] = out_ref[...].astype(result_ref.dtype)
+        if split:
+            keep_ref, send_ref = refs[0], refs[1]
+            per = keep_ref.shape[1]
+            parity = lax.axis_index(split) % 2
+            for k in range(keep_ref.shape[0]):
+                keep_ref[k] = out_ref[pl.ds((2 * k + parity) * per, per)]
+                send_ref[k] = out_ref[pl.ds((2 * k + 1 - parity) * per, per)]
+        else:
+            refs[0][...] = out_ref[...].astype(refs[0].dtype)
 
 
 def accumulate(tiles, dest_ids, source_ids, live_count, source_blocks, out_blocks, backward,
-               out_dtype=jnp.bfloat16):
+               out_dtype=jnp.bfloat16, split=None, split_size=1):
     slots, block, _ = tiles.shape
     width = source_blocks.shape[-1]
     in_blocks = source_blocks.shape[0]
@@ -73,11 +82,22 @@
         last = jnp.maximum(count[0] - 1, 0) // group
         return (jnp.minimum(g, last), 0, 0)
 
+    if split:
+        half = split_size // 2
+        per = out_blocks // split_size
+        part = jax.ShapeDtypeStruct((half, per, block, width), jnp.float32)
+        out_shape = (part, part)
+        out_specs = (
+            pl.BlockSpec((half, per, block, width), lambda g, d, s, c: (0, 0, 0, 0)),
+        ) * 2
+    else:
+        out_shape = jax.ShapeDtypeStruct((out_blocks, block, width), out_dtype)
+        out_specs = pl.BlockSpec((out_blocks, block, width), lambda g, d, s, c: (0, 0, 0))
     flops = 2 * slots * block * block * width
     bytes_accessed = tiles.size * 2 + source_blocks.size * 2 + out_blocks * block * width * 4
     return pl.pallas_call(
-        functools.partial(accumulate_kernel, backward),
-        out_shape=jax.ShapeDtypeStruct((out_blocks, block, width), out_dtype),
+        functools.partial(accumulate_kernel, backward, split),
+        out_shape=out_shape,
         grid_spec=pltpu.PrefetchScalarGridSpec(
             num_scalar_prefetch=3,
             grid=(steps,),
@@ -85,7 +105,7 @@
                 pl.BlockSpec((group, block, block), tile_map),
                 pl.BlockSpec((in_blocks, block, width), lambda g, d, s, c: (0, 0, 0)),
             ],
-            out_specs=pl.BlockSpec((out_blocks, block, width), lambda g, d, s, c: (0, 0, 0)),
+            out_specs=out_specs,
             scratch_shapes=[pltpu.VMEM((out_blocks, block, width), jnp.float32)],
         ),
         compiler_params=pltpu.CompilerParams(
@@ -161,11 +181,7 @@
     return jnp.sum(got.astype(jnp.float32), axis=0)
 
 
-def scatter_sum_paired(value, axis, size):
-    parity = lax.axis_index(axis) % 2
-    chunks = value.reshape((size // 2, 2, value.shape[0] // size) + value.shape[1:])
-    keep = jnp.where(parity == 0, chunks[:, 0], chunks[:, 1])
-    send = jnp.where(parity == 0, chunks[:, 1], chunks[:, 0])
+def scatter_sum_paired(keep, send, axis, size):
     got = lax.ppermute(send, axis, [(i, i ^ 1) for i in range(size)])
     paired = (keep + got).astype(jnp.bfloat16)
     groups = [list(range(start, size, 2)) for start in range(2)]
@@ -188,11 +204,14 @@
     factor = 1.0 / math.sqrt(own_nodes * row_count * col_count)
     panel = gather_all(features, "row", row_count)
     panel_blocks = panel.reshape(blocks_across, block, width)
-    partial_value = accumulate(
-        tile_set, dest_ids, source_ids, live_count, panel_blocks, blocks_down, False, jnp.float32
-    )
-    term = partial_value.reshape(blocks_down * block, width)
-    summed = scatter_sum_paired(term, "col", col_count)
+    keep, send = accumulate(
+        tile_set, dest_ids, source_ids, live_count, panel_blocks, blocks_down, False,
+        split="col", split_size=col_count,
+    )
+    chunk_shape = (col_count // 2, own_nodes, width)
+    summed = scatter_sum_paired(
+        keep.reshape(chunk_shape), send.reshape(chunk_shape), "col", col_count
+    )
     aggregated = summed.astype(jnp.bfloat16)
     preact = jnp.dot(aggregated, weight, preferred_element_type=jnp.float32) + bias
     hidden = jax.nn.silu(preact).astype(jnp.bfloat16)

time: 209 us -> 201 us (0.962)
  the two profiles are of different devices: /device:TPU:57 before, /device:TPU:0 now
where the time goes in v16:
time: 201 us; the launch traced here: 200 us
  Pallas kernels  59.6 us (30%)
  waiting for transfers between devices  56.7 us (28%)
  blocking collectives  36.8 us (18%)
  starting transfers between devices  18.3 us (9%)
  between operations  14.8 us (7%)
  other arithmetic  7.46 us (4%)
  local copies, waits for them, and re-layouts  3.86 us (2%)
  matrix products  2.36 us (1%)
    pallas_call x1, Pallas kernels, butterfly_sum(): pl.pallas_call(functools.partial(butterfly_kernel, tuple(steps)), out_sha...  41.3 us
    all_to_all x1, blocking collectives, scatter_sum_paired(): lax.all_to_all(paired, axis, 0, 0, tiled=False, axis_index_groups=groups)  36.8 us
    all_to_all x1, waiting for transfers between devices, gather_all(): got = lax.all_to_all(spread, axis, 0, 0, tiled=False)  26.5 us
    all_to_all x1, waiting for transfers between devices, scatter_sum(): got = lax.all_to_all(parts, axis, 0, 0, tiled=False)  22.7 us
    pallas_call x2, Pallas kernels, accumulate(): pl.pallas_call(functools.partial(accumulate_kernel, backward, split), out...  18.3 us
    all_to_all x1, starting transfers between devices, scatter_sum(): got = lax.all_to_all(parts, axis, 0, 0, tiled=False)  10.4 us
    all_to_all x1, starting transfers between devices, gather_all(): got = lax.all_to_all(spread, axis, 0, 0, tiled=False)  7.87 us
    ppermute x1, waiting for transfers between devices, scatter_sum_paired(): got = lax.ppermute(send, axis, [(i, i ^ 1) for i in range(size)])  7.37 us
  transfers between devices with their start and end apart: 4, of which 3 were waited for; matrix products, arithmetic and copies ran while one was open for 2% of the time, Pallas kernels for 21%

profile of v16, /device:TPU:0, one launch (start us, length us, event | category | flops | bytes accessed | tf_op | source)
XLA Modules:
  0.0 199.9 jit_solution(6402131499142554826)
XLA Ops:
  7.2 0.0 copy-start
  7.2 0.0 copy-start.3
  7.2 2.5 %broadcast_in_dim.4 = bf16[8,512,256]{2,1,0:T(8,128)(2,1)} broadcast(bf16[512,256]{1,0:T(8,128)(2,1)} %param.8), dimensions={1,2} | broadcast | bytes 2359296 | tf_op jit(solution)/shard_map/broadcast_in_dim | solution.py:173
  9.7 7.9 %all-to-all-start = ((bf16[8,512,256]{2,1,0:T(8,128)(2,1)}), bf16[8,512,256]{2,1,0:T(8,128)(2,1)S(1)}, u32[]{:S(2)}, u32[]{:S(2)}) async-start(bf16[8,512,256]{2,1,0:T(8,128)(2,1)} %broadcast_in_dim.4), calls=%async_computation | async-start | bytes 4194304 | tf_op jit(solution)/shard_map/all_to_all | solution.py:174
  17.5 0.0 all-gather.2.cloned.1.call-start
  18.2 0.6 reduce.2.dest_ref
  18.8 0.0 copy-done.4
  18.8 0.6 reduce.3.source_ref
  19.4 26.5 %all-to-all-done = bf16[8,512,256]{2,1,0:T(8,128)(2,1)S(1)} async-done(((bf16[8,512,256]{2,1,0:T(8,128)(2,1)}), bf16[8,512,256]{2,1,0:T(8,128)(2,1)S(1)}, u32[]{:S(2)}, u32[]{:S(2)}) %all-to-all-start) | async-done | bytes 2097184 | tf_op jit(solution)/shard_map/all_to_all | solution.py:174
  46.0 1.4 copy-done.1
  47.3 10.1 %shard_map.111 = (f32[8,4,128,256]{3,2,1,0:T(8,128)}, f32[8,4,128,256]{3,2,1,0:T(8,128)}) custom-call(s32[384]{0:T(512)} %reduce.2.dest_ref, s32[384]{0:T(512)} %reduce.3.source_ref, s32[1]{0:T(128)} %bitcast.18.count_ref, bf16[384,128,128]{2,1,0:T(8,128)(2,1)} %bitcast.20, bf16[32,128,256]{2,1,0:T(8,128)(2,1)} %bitcast.22), custom_call_target="tpu_custom_call" | custom-call | flops 3221225472 | bytes 23068672 | tf_op jit(solution)/shard_map/pallas_call | solution.py:98
  57.4 0.0 collective-permute-start
  57.4 7.4 %collective-permute-done = f32[8,512,256]{2,1,0:T(8,128)S(1)} collective-permute-done((f32[8,512,256]{2,1,0:T(8,128)}, f32[8,512,256]{2,1,0:T(8,128)S(1)}, u32[]{:S(2)}, u32[]{:S(2)}) %collective-permute-start) | collective-permute-done | bytes 4194336 | tf_op jit(solution)/shard_map/ppermute | solution.py:185
  64.8 2.8 %fusion = bf16[8,512,256]{2,1,0:T(8,128)(2,1)S(1)} fusion(f32[8,512,256]{2,1,0:T(8,128)S(1)} %collective-permute-done, f32[8,4,128,256]{3,2,1,0:T(8,128)} %get-tuple-element.8), kind=kLoop, calls=%fused_computation.1 | loop fusion | flops 2097152 | bytes 10485760 | tf_op jit(solution)/shard_map/convert_element_type | solution.py:186
  67.6 0.0 copy-start.5
  67.6 0.0 copy-start.6
  67.6 36.8 %all_to_all.15 = bf16[8,512,256]{2,1,0:T(8,128)(2,1)S(1)} all-to-all(bf16[8,512,256]{2,1,0:T(8,128)(2,1)S(1)} %fusion), channel_id=1, replica_groups={{0,2,4,6,8,10,12,14},{1,3,5,7,9,11,13,15},{16,18,20,22,24,26,28,30},{17..., dimensions={0} | all-to-all | bytes 4194304 | tf_op jit(solution)/shard_map/all_to_all | solution.py:188
  104.5 0.4 reduce_sum.33
  104.9 1.1 convert_reduce_fusion
  106.0 1.0 convolution_convert_fusion
  107.0 0.0 all-gather.2.cloned.1.call-update
  107.0 0.3 fusion.1
  107.3 0.7 pad_maximum_fusion.value_ref
  108.0 41.3 %shard_map.112 = f32[257,256]{1,0:T(8,128)} custom-call(f32[257,256]{1,0:T(8,128)} %pad_maximum_fusion.value_ref), custom_call_target="tpu_custom_call" | custom-call | tf_op jit(solution)/shard_map/pallas_call | solution.py:157
  149.3 0.0 all-gather.2.cloned.1.call-done
  149.3 8.2 %shard_map.113 = bf16[32,128,256]{2,1,0:T(8,128)(2,1)} custom-call(s32[384]{0:T(512)} %reduce.2.dest_ref, s32[384]{0:T(512)} %reduce.3.source_ref, s32[1]{0:T(128)} %bitcast.19.count_ref, bf16[384,128,128]{2,1,0:T(8,128)(2,1)} %bitcast.21, bf16[64,128,256]{2,1,0:T(8,128)(2,1)} %bitcast.24), custom_call_target="tpu_custom_call" | custom-call | flops 3221225472 | bytes 20971520 | tf_op jit(solution)/shard_map/pallas_call | solution.py:98
  157.6 10.4 %all-to-all-start.2 = ((bf16[8,512,256]{2,1,0:T(8,128)(2,1)}), bf16[8,512,256]{2,1,0:T(8,128)(2,1)S(1)}, u32[]{:S(2)}, u32[]{:S(2)}) async-start(bf16[8,512,256]{2,1,0:T(8,128)(2,1)} %bitcast.23), calls=%async_computation.2 | async-start | bytes 4194304 | tf_op jit(solution)/shard_map/all_to_all | solution.py:180
  168.0 0.0 copy-done.2
  168.0 0.6 slice_multiply_fusion.1
  168.5 0.7 slice_multiply_fusion
  169.2 22.7 %all-to-all-done.2 = bf16[8,512,256]{2,1,0:T(8,128)(2,1)S(1)} async-done(((bf16[8,512,256]{2,1,0:T(8,128)(2,1)}), bf16[8,512,256]{2,1,0:T(8,128)(2,1)S(1)}, u32[]{:S(2)}, u32[]{:S(2)}) %all-to-all-start.2) | async-done | bytes 2097184 | tf_op jit(solution)/shard_map/all_to_all | solution.py:180
  192.0 1.0 reduce_sum.35
  (7 shorter events, 0.0 us)
Async XLA Ops:
  7.2 97.7 %copy-start = (bf16[256,256]{1,0:T(8,128)(2,1)S(1)}, bf16[256,256]{1,0:T(8,128)(2,1)}, u32[]{:S(2)}) copy-start(bf16[256,256]{1,0:T(8,128)(2,1)} %param.9) | copy-start | bytes 393220
  7.2 11.0 %copy-start.3 = (s32[1,1,384]{2,1,0:T(1,128)S(1)}, s32[1,1,384]{2,1,0:T(1,128)}, u32[]{:S(2)}) copy-start(s32[1,1,384]{2,1,0:T(1,128)} %param.13) | copy-start | bytes 4612
  7.2 11.6 %copy-start.4 = (s32[1,1,384]{2,1,0:T(1,128)S(1)}, s32[1,1,384]{2,1,0:T(1,128)}, u32[]{:S(2)}) copy-start(s32[1,1,384]{2,1,0:T(1,128)} %param.14) | copy-start | bytes 4612
  9.7 36.3 %all-to-all-start = ((bf16[8,512,256]{2,1,0:T(8,128)(2,1)}), bf16[8,512,256]{2,1,0:T(8,128)(2,1)S(1)}, u32[]{:S(2)}, u32[]{:S(2)}) async-start(bf16[8,512,256]{2,1,0:T(8,128)(2,1)} %broadcast_in_dim.4), calls=%async_computation | async-start | bytes 4194304 | tf_op jit(solution)/shard_map/all_to_all | solution.py:174
  17.5 131.8 %all-gather.2.cloned.1.call-start = ((), (), s32[]{:S(2)}) async-start(), calls=%async_computation.3 | async-start | bytes 4456448 | tf_op jit(solution)/shard_map/all_gather | solution.py:225
  46.0 1.4 copy-start.1
  57.4 7.4 %collective-permute-start = (f32[8,512,256]{2,1,0:T(8,128)}, f32[8,512,256]{2,1,0:T(8,128)S(1)}, u32[]{:S(2)}, u32[]{:S(2)}) collective-permute-start(f32[8,512,256]{2,1,0:T(8,128)} %bitcast.27), channel_id=1, source_target_pairs={{0,1},{1,0},{2,3},{3,2},{4,5},{5,4},{6,7},{7,6},{8,9},{9,8},{10,11... | collective-permute-start | bytes 12582920 | tf_op jit(solution)/shard_map/ppermute | solution.py:185
  67.6 37.3 %copy-start.5 = (bf16[512,256]{1,0:T(8,128)(2,1)S(1)}, bf16[512,256]{1,0:T(8,128)(2,1)}, u32[]{:S(2)}) copy-start(bf16[512,256]{1,0:T(8,128)(2,1)} %param.11) | copy-start | bytes 786436
  67.6 37.3 %copy-start.6 = (f32[256]{0:T(256)S(1)}, f32[256]{0:T(256)}, u32[]{:S(2)}) copy-start(f32[256]{0:T(256)} %param.10) | copy-start | bytes 3076
  157.6 10.4 %copy-start.2 = (f32[257,256]{1,0:T(8,128)S(1)}, f32[257,256]{1,0:T(8,128)}, u32[]{:S(2)}) copy-start(f32[257,256]{1,0:T(8,128)} %shard_map.112) | copy-start | bytes 789508
  157.6 34.4 %all-to-all-start.2 = ((bf16[8,512,256]{2,1,0:T(8,128)(2,1)}), bf16[8,512,256]{2,1,0:T(8,128)(2,1)S(1)}, u32[]{:S(2)}, u32[]{:S(2)}) async-start(bf16[8,512,256]{2,1,0:T(8,128)(2,1)} %bitcast.23), calls=%async_computation.2 | async-start | bytes 4194304 | tf_op jit(solution)/shard_map/all_to_all | solution.py:180
Sparse Core Ops, SparseCore 0:
  107.1 38.0 all-gather.1
